TPU v7x, 32 devices: a whole 2x2x4 slice. The times are simulated.
32 devices in a mesh: rows: 2 (over x), feat: 16 (over z, y, core).
Axes of the slice: x: 2, y: 2, z: 4, core: 2. Of those that a mesh axis runs over, the one named last changes fastest.
Arguments:
- slab_grads: bfloat16 [448, 262144], P('rows', 'feat'), may hold values from -6 to 6
- basis: bfloat16 [262144, 1024], P('feat', 'rows'), may hold values from -0.01171875 to 0.01171875
- eigenvalues: float32 [1024], replicated, may hold values from 0.02 to 2
- store_rows: bfloat16 [16384, 1024], P(('rows', 'feat')), may hold values from -0.1875 to 0.1875
- slab_index: int32 [448], replicated, may hold values from 0 to 16383
Outputs:
- scores: float32 [448, 16384], P(None, ('rows', 'feat'))
All inputs are finite; a program needn't handle non-finite values.
Results may differ from a plain program's by a relative error of at most 0.0029.
Values may be sent and summed in bfloat16 or wider, within the bound.
No kernel may reach another device: no remote copies, remote signals or barrier semaphores. Data moves between devices by JAX's collectives and lax.ppermute only.
A program may use at most 128 MiB of HBM per device.

v0:
```python
import jax
import jax.numpy as jnp
from jax import lax
from jax.sharding import PartitionSpec as P

DAMPING = 0.1


def shards(slab_grads, basis, eigenvalues, store_rows, slab_index):
    feat_groups = lax.axis_size("feat")
    store_count = store_rows.shape[0]
    first_column = (lax.axis_index("rows") * feat_groups + lax.axis_index("feat")) * store_count
    columns = first_column + jnp.arange(store_count, dtype=jnp.int32)
    local_dirs = basis.shape[1]
    partial_value = jnp.dot(
        lax.all_gather(slab_grads, "rows", axis=0, tiled=True),
        basis,
        preferred_element_type=jnp.float32,
    )
    summed = lax.psum(partial_value, "feat")
    scales = lax.dynamic_slice_in_dim(
        eigenvalues, lax.axis_index("rows") * local_dirs, local_dirs, 0
    )
    whitened = (summed / (scales + DAMPING)).astype(jnp.bfloat16)
    gathered = lax.all_gather(whitened, "rows", axis=1, tiled=True)
    product = lax.dot_general(
        gathered, store_rows, (((1,), (1,)), ((), ())), preferred_element_type=jnp.float32
    )
    return jnp.where(slab_index[:, None] == columns[None, :], jnp.zeros_like(product), product)


def solution(mesh):
    in_specs = (P("rows", "feat"), P("feat", "rows"), P(), P(("rows", "feat"), None), P())
    out_specs = P(None, ("rows", "feat"))
    return jax.shard_map(shards, mesh=mesh, in_specs=in_specs, out_specs=out_specs, check_vma=False)
```

profile of v0, /device:TPU:0, one launch (start us, length us, event | category | flops | bytes accessed | tf_op | source)
XLA Modules:
  0.0 319.1 jit_solution(506024882513834059)
XLA Ops:
  6.5 0.0 copy-start
  6.5 0.0 all-gather.2.cloned.1.call-start
  6.5 0.7 all-gather.2.cloned.1.call-update
  7.3 0.0 copy-start.1
  7.3 0.0 copy-start.2
  7.3 0.0 all-reduce.2.cloned.1.call-start
  7.3 179.8 %all-gather.2.cloned.1.call-done = bf16[448,16384]{1,0:T(8,128)(2,1)} async-done(((bf16[224,16384]{1,0:T(8,128)(2,1)}), bf16[448,16384]{1,0:T(8,128)(2,1)}) %all-gather.2.cloned.1.call-update) | async-done | bytes 14680080 | tf_op jit(solution)/shard_map/all_gather | solution.py:16
  187.2 16.5 %fusion = f32[448,512]{1,0:T(8,128)} fusion(bf16[448,16384]{1,0:T(8,128)(2,1)} %all-gather.2.cloned.1.call-done, bf16[16384,512]{1,0:T(8,128)(2,1)} %param.6), kind=kOutput, calls=%fused_computation.4 | convolution fusion | flops 7516192768 | bytes 32374784 | tf_op jit(solution)/shard_map/dot_general | solution.py:15
  203.7 0.0 all-reduce.2.cloned.1.call-update
  203.7 0.0 copy-done.1
  203.7 0.1 dynamic-slice_add_fusion
  203.8 92.3 %all-reduce.2.cloned.1.call-done = f32[448,512]{1,0:T(8,128)} async-done(((f32[448,512]{1,0:T(8,128)}), f32[448,512]{1,0:T(8,128)}) %all-reduce.2.cloned.1.call-update) | async-done | bytes 917520 | tf_op jit(solution)/shard_map/psum | solution.py:20
  296.1 1.3 divide_convert_fusion
  297.4 13.2 %all_gather.7 = bf16[448,1024]{1,0:T(8,128)(2,1)S(1)} all-gather(bf16[448,512]{1,0:T(8,128)(2,1)S(1)} %divide_convert_fusion), channel_id=1, replica_groups=mesh['rows'=2,'feat'=16] {'rows'}, dimensions={1}, use_global_device_ids=true | all-gather | bytes 1376256 | tf_op jit(solution)/shard_map/all_gather | solution.py:25
  310.7 0.0 copy-done
  310.7 0.0 copy-done.2
  310.7 1.6 convolution_select_fusion
  (1 shorter events, 0.0 us)
Async XLA Ops:
  6.5 304.1 %copy-start = (bf16[512,1024]{1,0:T(8,128)(2,1)S(1)}, bf16[512,1024]{1,0:T(8,128)(2,1)}, u32[]{:S(2)}) copy-start(bf16[512,1024]{1,0:T(8,128)(2,1)} %param.8) | copy-start | bytes 3145732
  6.5 180.6 %all-gather.2.cloned.1.call-start = ((), (), s32[]{:S(2)}) async-start(), calls=%async_computation | async-start | bytes 22020096 | tf_op jit(solution)/shard_map/all_gather | solution.py:16
  7.3 196.5 %copy-start.1 = (f32[1024]{0:T(1024)S(1)}, f32[1024]{0:T(1024)}, u32[]{:S(2)}) copy-start(f32[1024]{0:T(1024)} %param.7) | copy-start | bytes 12292
  7.3 303.4 %copy-start.2 = (s32[448]{0:T(512)S(1)}, s32[448]{0:T(512)}, u32[]{:S(2)}) copy-start(s32[448]{0:T(512)} %param.9) | copy-start | bytes 5380
  7.3 288.9 %all-reduce.2.cloned.1.call-start = ((), (), s32[]{:S(2)}) async-start(), calls=%async_computation.1 | async-start | bytes 1835008 | tf_op jit(solution)/shard_map/psum | solution.py:20
Sparse Core Ops, SparseCore 0:
  8.9 178.2 all-gather.1
  203.8 92.2 all-reduce.1
where the time goes:
time: 319 us
  waiting for transfers between devices  273 us (86%)
  matrix products  18.1 us (6%)
  between operations  13.4 us (4%)
  blocking collectives  13.2 us (4%)
    all_gather x1, waiting for transfers between devices, shards(): lax.all_gather(slab_grads, 'rows', axis=0, tiled=True)  180 us
    psum x1, waiting for transfers between devices, shards(): summed = lax.psum(partial_value, 'feat')  92.3 us
    dot_general x1, matrix products, shards(): jnp.dot(lax.all_gather(slab_grads, 'rows', axis=0, tiled=True), basis, pr...  16.5 us
    all_gather x1, blocking collectives, shards(): gathered = lax.all_gather(whitened, 'rows', axis=1, tiled=True)  13.2 us
  transfers between devices with their start and end apart: 2, of which 2 were waited for; matrix products, arithmetic and copies ran while one was open for 0% of the time, Pallas kernels for 0%

commit v1 on v0

v1 whole, which is shorter than its diff:
```python
import functools

import jax
import jax.numpy as jnp
from jax import lax
from jax.experimental import pallas as pl
from jax.experimental.pallas import tpu as pltpu
from jax.sharding import PartitionSpec as P


DAMPING = 0.1
CONTRACT_LAST = (((1,), (1,)), ((), ()))


def parity(number, count):
    bits = 0
    while count > 1:
        bits = bits ^ number
        number = number >> 1
        count //= 2
    return bits & 1


def exchange(value, row_groups, feat_groups, row_flip, feat_flip):
    count = row_groups * feat_groups
    pairs = [
        (i, (((i // feat_groups) ^ row_flip) * feat_groups) + ((i % feat_groups) ^ feat_flip))
        for i in range(count)
    ]
    return lax.ppermute(value, ("rows", "feat"), pairs)


def after(value, *needed):
    return lax.optimization_barrier((value, *needed))[0]


def score_kernel(where_ref, whitened_ref, store_ref, index_ref, out_ref):
    product = lax.dot_general(
        whitened_ref[...], store_ref[...], CONTRACT_LAST, preferred_element_type=jnp.float32
    )
    columns = where_ref[1] + lax.broadcasted_iota(jnp.int32, product.shape, 1)
    out_ref[...] = jnp.where(index_ref[...] == columns, jnp.zeros_like(product), product)


def score(whitened, store, slab_index, row, first_column, row_groups):
    rows = whitened.shape[0] // row_groups
    directions = whitened.shape[1]
    count = store.shape[0]
    return pl.pallas_call(
        score_kernel,
        out_shape=jax.ShapeDtypeStruct((whitened.shape[0], count), jnp.float32),
        grid_spec=pltpu.PrefetchScalarGridSpec(
            num_scalar_prefetch=1,
            grid=(row_groups,),
            in_specs=[
                pl.BlockSpec((rows, directions), lambda a, where: (a, 0)),
                pl.BlockSpec((count, directions), lambda a, where: (0, 0)),
                pl.BlockSpec((rows, 1), lambda a, where: (a ^ where[0], 0)),
            ],
            out_specs=pl.BlockSpec((rows, count), lambda a, where: (a ^ where[0], 0)),
        ),
        name="score",
    )(jnp.stack([row, first_column]).astype(jnp.int32), whitened, store, slab_index[:, None])


def shards(slab_grads, basis, eigenvalues, store_rows, slab_index, *, row_groups, feat_groups):
    row, feat = lax.axis_index("rows"), lax.axis_index("feat")
    store_count = store_rows.shape[0]
    first_column = (row * feat_groups + feat) * store_count
    rows, features = slab_grads.shape
    directions = basis.shape[1]
    half = directions // 2
    side = parity(row, row_groups) ^ parity(feat, feat_groups)
    swap = functools.partial(exchange, row_groups=row_groups, feat_groups=feat_groups)

    def cross(value, flip):
        return swap(value, row_flip=flip, feat_flip=bin(flip).count("1") & 1)

    tail = max(rows * 3 // 14 // 16 * 16, 16)
    lead = 16
    middle = lead + (rows - tail - lead) // 16 * 8
    cuts = [0, lead, middle, rows - tail]
    feature_cuts = [0, features // 2, features * 7 // 8, features]

    last = row_groups - 1
    far = [swap(slab_grads, row_flip=flip, feat_flip=0) for flip in range(1, last)]
    head = slab_grads[:lead]
    rest = after(slab_grads, head)
    pieces = [head] + [rest[a:b] for a, b in zip(cuts[1:-1], cuts[2:])]
    pieces += [rest[rows - tail :, a:b] for a, b in zip(feature_cuts[:-1], feature_cuts[1:])]
    moved = []
    for piece in pieces:
        moved.append(swap(piece, row_flip=last, feat_flip=0))

    scales = lax.dynamic_slice_in_dim(
        eigenvalues, row * directions + side * half, half, 0
    )[None, :] + DAMPING
    order = []
    for flip in range(row_groups):
        base = (row ^ flip) * directions
        for part in (side, 1 - side):
            order.append(lax.dynamic_slice_in_dim(store_rows, base + part * half, half, 1))
    store = jnp.concatenate(order, 1)

    def project(block, a=0, b=features):
        return jnp.dot(block, basis[a:b], preferred_element_type=jnp.float32)

    def halves(partial_value):
        mine = lax.dynamic_slice_in_dim(partial_value, side * half, half, 1)
        other = lax.dynamic_slice_in_dim(partial_value, (1 - side) * half, half, 1)
        return mine + swap(other, row_flip=0, feat_flip=1)

    def totals(total):
        yield total
        bit = 2
        while bit < feat_groups:
            total = total + swap(total, row_flip=0, feat_flip=bit | 1)
            bit *= 2
            yield total

    def whiten(total):
        return (total / scales).astype(jnp.bfloat16)

    def reduce(partial_value):
        return whiten(list(totals(halves(partial_value)))[-1])

    early = [reduce(project(after(slab_grads, *pieces)))]
    for block in far:
        early.append(reduce(project(after(block, early[-1]))))
    first, second, third = moved[:3]
    lead_value = project(after(first, early[-1]))
    near = project(after(second, early[-1], lead_value))
    early.append(reduce(jnp.concatenate([lead_value, near], 0)))
    middle = project(after(third, early[-1]))
    middle_totals = list(totals(halves(middle)))
    early.append(whiten(middle_totals[-1]))
    early = jnp.concatenate(early, 0)
    early = jnp.concatenate([early, swap(early, row_flip=0, feat_flip=1)], 1)
    early = [early] + [cross(early, flip) for flip in range(1, row_groups)]

    late = project(after(moved[3], middle_totals[1]), *feature_cuts[:2])
    late += project(after(moved[4], late, middle_totals[2]), *feature_cuts[1:3])
    late += project(after(moved[5], late, early[0]), *feature_cuts[2:])
    late = reduce(late)
    late = jnp.concatenate([late] + [cross(late, flip) for flip in range(1, row_groups)], 0)
    pair = swap(late, row_flip=0, feat_flip=1)
    late = [
        jnp.concatenate([late[f * tail : (f + 1) * tail], pair[f * tail : (f + 1) * tail]], 1)
        for f in range(row_groups)
    ]
    columns = []
    for flip in range(row_groups):
        whole = jnp.concatenate([early[flip], late[flip]], 0)
        order = [a ^ flip for a in range(row_groups)]
        columns.append(
            whole
            if flip == 0
            else jnp.concatenate([whole[i * rows : (i + 1) * rows] for i in order], 0)
        )
    whitened = jnp.concatenate(columns, 1)
    return score(whitened, store, slab_index, row, first_column, row_groups)


def plain(slab_grads, basis, eigenvalues, store_rows, slab_index, *, row_groups, feat_groups):
    store_count = store_rows.shape[0]
    first_column = (lax.axis_index("rows") * feat_groups + lax.axis_index("feat")) * store_count
    columns = first_column + jnp.arange(store_count, dtype=jnp.int32)
    local_dirs = basis.shape[1]
    partial_value = jnp.dot(
        lax.all_gather(slab_grads, "rows", axis=0, tiled=True),
        basis,
        preferred_element_type=jnp.float32,
    )
    summed = lax.psum(partial_value, "feat")
    scales = lax.dynamic_slice_in_dim(
        eigenvalues, lax.axis_index("rows") * local_dirs, local_dirs, 0
    )
    whitened = (summed / (scales + DAMPING)).astype(jnp.bfloat16)
    gathered = lax.all_gather(whitened, "rows", axis=1, tiled=True)
    product = lax.dot_general(
        gathered, store_rows, CONTRACT_LAST, preferred_element_type=jnp.float32
    )
    return jnp.where(slab_index[:, None] == columns[None, :], jnp.zeros_like(product), product)


def solution(mesh):
    row_groups, feat_groups = mesh.shape["rows"], mesh.shape["feat"]
    powers = all(n > 1 and n & (n - 1) == 0 for n in (row_groups, feat_groups))

    def body(*args):
        sizes = dict(row_groups=row_groups, feat_groups=feat_groups)
        rows = args[0].shape[0]
        if not powers or rows < 96 or rows % 16 or args[1].shape[1] % 2:
            return plain(*args, **sizes)
        return shards(*args, **sizes)

    in_specs = (P("rows", "feat"), P("feat", "rows"), P(), P(("rows", "feat"), None), P())
    out_specs = P(None, ("rows", "feat"))
    return jax.shard_map(body, mesh=mesh, in_specs=in_specs, out_specs=out_specs, check_vma=False)
```

time: 319 us -> 202 us (0.63)
  waiting for transfers between devices: 273 us -> 113 us
  starting transfers between devices: 0.04 us -> 35.3 us
  matrix products: 18.1 us -> 32.9 us
  blocking collectives: 13.2 us -> 0 us
  between operations: 13.4 us -> 0.29 us
  local copies, waits for them, and re-layouts: 0.01 us -> 11.7 us
  Pallas kernels: 0 us -> 3.89 us
  other arithmetic: 1.36 us -> 4.79 us
    all_gather x1 -> x0, waiting for transfers between devices: 180 us -> none  [shards(): lax.all_gather(slab_grads, 'rows', axis=0, tiled=True)]
    ppermute x0 -> x26, waiting for transfers between devices: none -> 113 us  [exchange(): return lax.ppermute(value, ('rows', 'feat'), pairs)]
    psum x1 -> x0, waiting for transfers between devices: 92.3 us -> none  [shards(): summed = lax.psum(partial_value, 'feat')]
    ppermute x0 -> x26, starting transfers between devices: none -> 35.3 us  [exchange(): return lax.ppermute(value, ('rows', 'feat'), pairs)]
    dot_general x2 -> x7, matrix products: 18.1 us -> 32.9 us  [project(): return jnp.dot(block, basis[a:b], preferred_element_type=jnp.float32)]
    all_gather x1 -> x0, blocking collectives: 13.2 us -> none  [shards(): gathered = lax.all_gather(whitened, 'rows', axis=1, tiled=True)]
    slice x0 -> x7, local copies, waits for them, and re-layouts: none -> 9.93 us  [the longest x1 5.49 us: shards(): pieces = [head] + [rest[a:b] for a, b in zip(cuts[1:-1], cuts[2:])]]
    pallas_call x0 -> x1, Pallas kernels: none -> 3.89 us  [score(): pl.pallas_call(score_kernel, out_shape=jax.ShapeDtypeStruct((whitened.sha...]
  transfers between devices with their start and end apart: 2 -> 26, of which waited for: 2 -> 22; matrix products, arithmetic and copies ran while one was open for 0% -> 20% of each run, Pallas kernels for 0% -> 0%
where the time goes in v1:
time: 202 us
  waiting for transfers between devices  113 us (56%)
  starting transfers between devices  35.3 us (17%)
  matrix products  32.9 us (16%)
  local copies, waits for them, and re-layouts  11.7 us (6%)
  other arithmetic  4.79 us (2%)
  Pallas kernels  3.89 us (2%)
    ppermute x26, waiting for transfers between devices, exchange(): return lax.ppermute(value, ('rows', 'feat'), pairs)  113 us
    ppermute x26, starting transfers between devices, exchange(): return lax.ppermute(value, ('rows', 'feat'), pairs)  35.3 us
    dot_general x7, matrix products, project(): return jnp.dot(block, basis[a:b], preferred_element_type=jnp.float32)  32.9 us
    slice x1, local copies, waits for them, and re-layouts, shards(): pieces = [head] + [rest[a:b] for a, b in zip(cuts[1:-1], cuts[2:])]  5.49 us
  transfers between devices with their start and end apart: 26, of which 22 were waited for; matrix products, arithmetic and copies ran while one was open for 20% of the time, Pallas kernels for 0%

profile of v1, /device:TPU:0, one launch (start us, length us, event | category | flops | bytes accessed | tf_op | source)
XLA Modules:
  0.0 201.5 jit_solution(14338297158281593217)
XLA Ops:
  0.0 1.9 slice.39
  1.9 5.5 %fusion.17 = (bf16[80,16384]{1,0:T(8,128)(2,1)}, bf16[80,16384]{1,0:T(8,128)(2,1)}) fusion(bf16[224,16384]{1,0:T(8,128)(2,1)} %param.5), kind=kLoop, calls=%fused_computation.39 | loop fusion | bytes 10485760 | tf_op jit(solution)/shard_map/slice | solution.py:89
  7.4 3.0 %collective-permute-start.5 = (bf16[80,16384]{1,0:T(8,128)(2,1)}, bf16[80,16384]{1,0:T(8,128)(2,1)S(1)}, u32[]{:S(2)}, u32[]{:S(2)}) collective-permute-start(bf16[80,16384]{1,0:T(8,128)(2,1)} %get-tuple-element.21), channel_id=1, source_target_pairs={{0,16},{1,17},{2,18},{3,19},{4,20},{5,21},{6,22},{7,23},{8,24},{9,... | collective-permute-start | bytes 7864328 | tf_op jit(solution)/shard_map/ppermute | solution.py:30
  10.4 0.9 slice.42
  11.3 0.9 slice.43
  12.2 0.7 slice.44
  12.9 7.9 %fusion.19 = f32[224,512]{1,0:T(8,128)S(1)} fusion(bf16[224,16384]{1,0:T(8,128)(2,1)S(1)} %copy-done, bf16[16384,512]{1,0:T(8,128)(2,1)} %param.6), kind=kOutput, calls=%fused_computation.41 | convolution fusion | flops 3758096384 | bytes 24576000 | tf_op jit(solution)/shard_map/dot_general | solution.py:106
  20.8 0.7 constant_dynamic-slice_fusion.6
  21.5 1.7 collective-permute-done
  23.2 1.3 collective-permute-start.1
  24.5 6.3 %collective-permute-done.1 = f32[224,256]{1,0:T(8,128)S(1)} collective-permute-done((f32[224,256]{1,0:T(8,128)S(1)}, f32[224,256]{1,0:T(8,128)S(1)}, u32[]{:S(2)}, u32[]{:S(2)}) %collective-permute-start.1) | collective-permute-done | bytes 229408 | tf_op jit(solution)/shard_map/ppermute | solution.py:30
  30.9 1.7 collective-permute-start.2
  32.6 0.5 collective-permute-start.4
  33.1 5.1 %collective-permute-done.2 = f32[224,256]{1,0:T(8,128)S(1)} collective-permute-done((f32[224,256]{1,0:T(8,128)S(1)}, f32[224,256]{1,0:T(8,128)S(1)}, u32[]{:S(2)}, u32[]{:S(2)}) %collective-permute-start.2) | collective-permute-done | bytes 229408 | tf_op jit(solution)/shard_map/ppermute | solution.py:30
  38.3 3.0 %collective-permute-start.3 = (f32[224,256]{1,0:T(8,128)S(1)}, f32[224,256]{1,0:T(8,128)}, u32[]{:S(2)}, u32[]{:S(2)}) collective-permute-start(f32[224,256]{1,0:T(8,128)S(1)} %add.107), channel_id=1, source_target_pairs={{0,9},{1,8},{2,11},{3,10},{4,13},{5,12},{6,15},{7,14},{8,1},{9,0},... | collective-permute-start | bytes 688136 | tf_op jit(solution)/shard_map/ppermute | solution.py:30
  41.3 0.5 collective-permute-start.10
  41.8 0.8 dynamic-slice_add_fusion.3
  42.6 9.3 %collective-permute-done.3 = f32[224,256]{1,0:T(8,128)} collective-permute-done((f32[224,256]{1,0:T(8,128)S(1)}, f32[224,256]{1,0:T(8,128)}, u32[]{:S(2)}, u32[]{:S(2)}) %collective-permute-start.3) | collective-permute-done | bytes 229408 | tf_op jit(solution)/shard_map/ppermute | solution.py:30
  51.9 1.0 divide_convert_fusion
  52.8 26.7 %collective-permute-done.4 = bf16[16,16384]{1,0:T(8,128)(2,1)S(1)} collective-permute-done((bf16[16,16384]{1,0:T(8,128)(2,1)}, bf16[16,16384]{1,0:T(8,128)(2,1)S(1)}, u32[]{:S(2)}, u32[]{:S(2)}) %collective-permute-start.4) | collective-permute-done | bytes 524320 | tf_op jit(solution)/shard_map/ppermute | solution.py:30
  79.5 8.2 %fusion.20 = f32[16,512]{1,0:T(8,128)S(1)} fusion(bf16[16,16384]{1,0:T(8,128)(2,1)S(1)} %collective-permute-done.4, bf16[16384,512]{1,0:T(8,128)(2,1)} %param.6), kind=kOutput, calls=%fused_computation.42 | convolution fusion | flops 268435456 | bytes 17334272 | tf_op jit(solution)/shard_map/dot_general | solution.py:106
  87.7 8.9 %fusion.21 = f32[80,512]{1,0:T(8,128)S(1)} fusion(bf16[80,16384]{1,0:T(8,128)(2,1)S(1)} %collective-permute-done.5, bf16[16384,512]{1,0:T(8,128)(2,1)} %param.6), kind=kOutput, calls=%fused_computation.43 | convolution fusion | flops 1342177280 | bytes 19562496 | tf_op jit(solution)/shard_map/dot_general | solution.py:106
  96.8 1.3 collective-permute-done.6
  98.1 1.9 collective-permute-start.7
  100.0 2.9 %collective-permute-done.7 = f32[96,256]{1,0:T(8,128)S(1)} collective-permute-done((f32[96,256]{1,0:T(8,128)S(1)}, f32[96,256]{1,0:T(8,128)S(1)}, u32[]{:S(2)}, u32[]{:S(2)}) %collective-permute-start.7) | collective-permute-done | bytes 98336 | tf_op jit(solution)/shard_map/ppermute | solution.py:30
  102.8 2.4 %collective-permute-start.8 = (f32[96,256]{1,0:T(8,128)S(1)}, f32[96,256]{1,0:T(8,128)S(1)}, u32[]{:S(2)}, u32[]{:S(2)}) collective-permute-start(f32[96,256]{1,0:T(8,128)S(1)} %add.114), channel_id=1, source_target_pairs={{0,5},{1,4},{2,7},{3,6},{4,1},{5,0},{6,3},{7,2},{8,13},{9,12},{10,... | collective-permute-start | bytes 294920 | tf_op jit(solution)/shard_map/ppermute | solution.py:30
  105.3 3.1 %collective-permute-done.8 = f32[96,256]{1,0:T(8,128)S(1)} collective-permute-done((f32[96,256]{1,0:T(8,128)S(1)}, f32[96,256]{1,0:T(8,128)S(1)}, u32[]{:S(2)}, u32[]{:S(2)}) %collective-permute-start.8) | collective-permute-done | bytes 98336 | tf_op jit(solution)/shard_map/ppermute | solution.py:30
  108.3 2.8 %collective-permute-start.9 = (f32[96,256]{1,0:T(8,128)S(1)}, f32[96,256]{1,0:T(8,128)S(1)}, u32[]{:S(2)}, u32[]{:S(2)}) collective-permute-start(f32[96,256]{1,0:T(8,128)S(1)} %add.115), channel_id=1, source_target_pairs={{0,9},{1,8},{2,11},{3,10},{4,13},{5,12},{6,15},{7,14},{8,1},{9,0},... | collective-permute-start | bytes 294920 | tf_op jit(solution)/shard_map/ppermute | solution.py:30
  111.1 1.5 collective-permute-start.16
  112.6 3.3 %collective-permute-done.9 = f32[96,256]{1,0:T(8,128)S(1)} collective-permute-done((f32[96,256]{1,0:T(8,128)S(1)}, f32[96,256]{1,0:T(8,128)S(1)}, u32[]{:S(2)}, u32[]{:S(2)}) %collective-permute-start.9) | collective-permute-done | bytes 98336 | tf_op jit(solution)/shard_map/ppermute | solution.py:30
  116.0 19.8 %collective-permute-done.10 = bf16[80,16384]{1,0:T(8,128)(2,1)} collective-permute-done((bf16[80,16384]{1,0:T(8,128)(2,1)}, bf16[80,16384]{1,0:T(8,128)(2,1)}, u32[]{:S(2)}, u32[]{:S(2)}) %collective-permute-start.10) | collective-permute-done | bytes 2621472 | tf_op jit(solution)/shard_map/ppermute | solution.py:30
  135.8 4.8 %fusion.22 = f32[80,512]{1,0:T(8,128)S(1)} fusion(bf16[80,16384]{1,0:T(8,128)(2,1)} %collective-permute-done.10, bf16[16384,512]{1,0:T(8,128)(2,1)S(1)} %bitcast.15), kind=kOutput, calls=%fused_computation.44 | convolution fusion | flops 1342177280 | bytes 19562496 | tf_op jit(solution)/shard_map/dot_general | solution.py:106
  140.7 1.3 collective-permute-done.11
  142.0 1.9 collective-permute-start.12
  143.9 2.5 %collective-permute-done.12 = f32[80,256]{1,0:T(8,128)S(1)} collective-permute-done((f32[80,256]{1,0:T(8,128)S(1)}, f32[80,256]{1,0:T(8,128)S(1)}, u32[]{:S(2)}, u32[]{:S(2)}) %collective-permute-start.12) | collective-permute-done | bytes 81952 | tf_op jit(solution)/shard_map/ppermute | solution.py:30
  146.4 2.3 %collective-permute-start.13 = (f32[80,256]{1,0:T(8,128)S(1)}, f32[80,256]{1,0:T(8,128)S(1)}, u32[]{:S(2)}, u32[]{:S(2)}) collective-permute-start(f32[80,256]{1,0:T(8,128)S(1)} %add.118), channel_id=1, source_target_pairs={{0,5},{1,4},{2,7},{3,6},{4,1},{5,0},{6,3},{7,2},{8,13},{9,12},{10,... | collective-permute-start | bytes 245768 | tf_op jit(solution)/shard_map/ppermute | solution.py:30
  148.7 1.5 collective-permute-start.17
  150.2 0.5 collective-permute-start.18
  150.7 1.3 collective-permute-done.16
  152.1 2.1 %collective-permute-start.14 = (f32[80,256]{1,0:T(8,128)S(1)}, f32[80,256]{1,0:T(8,128)S(1)}, u32[]{:S(2)}, u32[]{:S(2)}) collective-permute-start(f32[80,256]{1,0:T(8,128)S(1)} %add.119), channel_id=1, source_target_pairs={{0,9},{1,8},{2,11},{3,10},{4,13},{5,12},{6,15},{7,14},{8,1},{9,0},... | collective-permute-start | bytes 245768 | tf_op jit(solution)/shard_map/ppermute | solution.py:30
  154.2 1.5 fusion
  155.7 9.2 %collective-permute-done.17 = bf16[48,6144]{1,0:T(8,128)(2,1)S(1)} collective-permute-done((bf16[48,6144]{1,0:T(8,128)(2,1)S(1)}, bf16[48,6144]{1,0:T(8,128)(2,1)S(1)}, u32[]{:S(2)}, u32[]{:S(2)}) %collective-permute-start.17) | collective-permute-done | bytes 589856 | tf_op jit(solution)/shard_map/ppermute | solution.py:30
  164.9 0.1 collective-permute-start.15
  165.0 1.2 fusion.9
  166.2 0.2 collective-permute-done.15
  166.5 2.1 %collective-permute-done.18 = bf16[48,2048]{1,0:T(8,128)(2,1)S(1)} collective-permute-done((bf16[48,2048]{1,0:T(8,128)(2,1)S(1)}, bf16[48,2048]{1,0:T(8,128)(2,1)S(1)}, u32[]{:S(2)}, u32[]{:S(2)}) %collective-permute-start.18) | collective-permute-done | bytes 196640 | tf_op jit(solution)/shard_map/ppermute | solution.py:30
  168.6 0.5 fusion.6
  169.1 1.2 collective-permute-done.19
  170.4 1.6 collective-permute-start.20
  172.0 2.2 %collective-permute-done.20 = f32[48,256]{1,0:T(8,128)S(1)} collective-permute-done((f32[48,256]{1,0:T(8,128)S(1)}, f32[48,256]{1,0:T(8,128)S(1)}, u32[]{:S(2)}, u32[]{:S(2)}) %collective-permute-start.20) | collective-permute-done | bytes 49184 | tf_op jit(solution)/shard_map/ppermute | solution.py:30
  174.1 1.7 collective-permute-start.21
  175.8 2.1 %collective-permute-done.21 = f32[48,256]{1,0:T(8,128)S(1)} collective-permute-done((f32[48,256]{1,0:T(8,128)S(1)}, f32[48,256]{1,0:T(8,128)S(1)}, u32[]{:S(2)}, u32[]{:S(2)}) %collective-permute-start.21) | collective-permute-done | bytes 49184 | tf_op jit(solution)/shard_map/ppermute | solution.py:30
  177.9 2.7 %collective-permute-start.22 = (f32[48,256]{1,0:T(8,128)S(1)}, f32[48,256]{1,0:T(8,128)S(1)}, u32[]{:S(2)}, u32[]{:S(2)}) collective-permute-start(f32[48,256]{1,0:T(8,128)S(1)} %add.125), channel_id=1, source_target_pairs={{0,9},{1,8},{2,11},{3,10},{4,13},{5,12},{6,15},{7,14},{8,1},{9,0},... | collective-permute-start | bytes 147464 | tf_op jit(solution)/shard_map/ppermute | solution.py:30
  180.6 0.1 constant_dynamic-slice_fusion.3
  180.7 1.7 collective-permute-done.22
  182.4 1.8 collective-permute-start.23
  184.2 1.1 pad_maximum_fusion.store_ref
  185.4 0.4 collective-permute-done.23
  185.7 0.3 collective-permute-start.24
  186.1 0.6 pad_add_fusion.where_ref
  186.6 0.9 copy.6.index_ref
  187.5 9.1 %collective-permute-done.25 = bf16[400,512]{1,0:T(8,128)(2,1)S(1)} collective-permute-done((bf16[400,512]{1,0:T(8,128)(2,1)S(1)}, bf16[400,512]{1,0:T(8,128)(2,1)S(1)}, u32[]{:S(2)}, u32[]{:S(2)}) %collective-permute-start.25) | collective-permute-done | bytes 409632 | tf_op jit(solution)/shard_map/ppermute | solution.py:30
  196.6 1.1 fusion.13.whitened_ref
  197.7 3.9 %score.1 = f32[448,512]{1,0:T(8,128)} custom-call(s32[2]{0:T(128)} %pad_add_fusion.where_ref, bf16[448,1024]{1,0:T(8,128)(2,1)} %fusion.13.whitened_ref, bf16[512,1024]{1,0:T(8,128)(2,1)} %pad_maximum_fusion.store_ref, s32[448,1]{1,0:T(8,128)} %copy.6.index_ref), custom_call_target="tpu_custom_call" | custom-call | tf_op jit(solution)/shard_map/score/pallas_call | solution.py:49
  (53 shorter events, 0.6 us)
Async XLA Ops:
  1.9 8.5 %copy-start = (bf16[224,16384]{1,0:T(8,128)(2,1)S(1)}, bf16[224,16384]{1,0:T(8,128)(2,1)}, u32[]{:S(2)}) copy-start(bf16[224,16384]{1,0:T(8,128)(2,1)} %param.5) | copy-start | bytes 22020100
  7.4 80.3 %collective-permute-start.5 = (bf16[80,16384]{1,0:T(8,128)(2,1)}, bf16[80,16384]{1,0:T(8,128)(2,1)S(1)}, u32[]{:S(2)}, u32[]{:S(2)}) collective-permute-start(bf16[80,16384]{1,0:T(8,128)(2,1)} %get-tuple-element.21), channel_id=1, source_target_pairs={{0,16},{1,17},{2,18},{3,19},{4,20},{5,21},{6,22},{7,23},{8,24},{9,... | collective-permute-start | bytes 7864328 | tf_op jit(solution)/shard_map/ppermute | solution.py:30
  21.5 1.7 collective-permute-start
  23.2 7.6 %collective-permute-start.1 = (f32[224,256]{1,0:T(8,128)S(1)}, f32[224,256]{1,0:T(8,128)S(1)}, u32[]{:S(2)}, u32[]{:S(2)}) collective-permute-start(f32[224,256]{1,0:T(8,128)S(1)} %dynamic-slice_add_fusion), channel_id=1, source_target_pairs={{0,3},{1,2},{2,1},{3,0},{4,7},{5,6},{6,5},{7,4},{8,11},{9,10},{10,... | collective-permute-start | bytes 688136 | tf_op jit(solution)/shard_map/ppermute | solution.py:30
  30.9 7.3 %collective-permute-start.2 = (f32[224,256]{1,0:T(8,128)S(1)}, f32[224,256]{1,0:T(8,128)S(1)}, u32[]{:S(2)}, u32[]{:S(2)}) collective-permute-start(f32[224,256]{1,0:T(8,128)S(1)} %add.106), channel_id=1, source_target_pairs={{0,5},{1,4},{2,7},{3,6},{4,1},{5,0},{6,3},{7,2},{8,13},{9,12},{10,... | collective-permute-start | bytes 688136 | tf_op jit(solution)/shard_map/ppermute | solution.py:30
  32.6 46.9 %collective-permute-start.4 = (bf16[16,16384]{1,0:T(8,128)(2,1)}, bf16[16,16384]{1,0:T(8,128)(2,1)S(1)}, u32[]{:S(2)}, u32[]{:S(2)}) collective-permute-start(bf16[16,16384]{1,0:T(8,128)(2,1)} %slice.39), channel_id=1, source_target_pairs={{0,16},{1,17},{2,18},{3,19},{4,20},{5,21},{6,22},{7,23},{8,24},{9,... | collective-permute-start | bytes 1572872 | tf_op jit(solution)/shard_map/ppermute | solution.py:30
  38.3 13.6 %collective-permute-start.3 = (f32[224,256]{1,0:T(8,128)S(1)}, f32[224,256]{1,0:T(8,128)}, u32[]{:S(2)}, u32[]{:S(2)}) collective-permute-start(f32[224,256]{1,0:T(8,128)S(1)} %add.107), channel_id=1, source_target_pairs={{0,9},{1,8},{2,11},{3,10},{4,13},{5,12},{6,15},{7,14},{8,1},{9,0},... | collective-permute-start | bytes 688136 | tf_op jit(solution)/shard_map/ppermute | solution.py:30
  41.3 94.5 %collective-permute-start.10 = (bf16[80,16384]{1,0:T(8,128)(2,1)}, bf16[80,16384]{1,0:T(8,128)(2,1)}, u32[]{:S(2)}, u32[]{:S(2)}) collective-permute-start(bf16[80,16384]{1,0:T(8,128)(2,1)} %get-tuple-element.22), channel_id=1, source_target_pairs={{0,16},{1,17},{2,18},{3,19},{4,20},{5,21},{6,22},{7,23},{8,24},{9,... | collective-permute-start | bytes 7864328 | tf_op jit(solution)/shard_map/ppermute | solution.py:30
  79.5 56.3 %slice-start = ((s8[16777216]{0:T(1024)(128)(4,1)}), s8[4194304]{0:T(1024)(128)(4,1)S(1)}, s32[]{:S(2)}) async-start(s8[16777216]{0:T(1024)(128)(4,1)} %bitcast.14), calls=%async_computation | async-start | bytes 8388608
  79.5 56.3 %slice-start.1 = ((s8[16777216]{0:T(1024)(128)(4,1)}), s8[4194304]{0:T(1024)(128)(4,1)S(1)}, s32[]{:S(2)}) async-start(s8[16777216]{0:T(1024)(128)(4,1)} %bitcast.14), calls=%async_computation.1 | async-start | bytes 8388608
  87.7 23.4 %copy-start.2 = (bf16[48,8192]{1,0:T(8,128)(2,1)S(1)}, bf16[48,8192]{1,0:T(8,128)(2,1)}, u32[]{:S(2)}) copy-start(bf16[48,8192]{1,0:T(8,128)(2,1)} %slice.42) | copy-start | bytes 2359300
  87.7 48.1 %slice-start.2 = ((s8[16777216]{0:T(1024)(128)(4,1)}), s8[4194304]{0:T(1024)(128)(4,1)S(1)}, s32[]{:S(2)}) async-start(s8[16777216]{0:T(1024)(128)(4,1)} %bitcast.14), calls=%async_computation.2 | async-start | bytes 8388608
  87.7 48.1 %slice-start.3 = ((s8[16777216]{0:T(1024)(128)(4,1)}), s8[4194304]{0:T(1024)(128)(4,1)S(1)}, s32[]{:S(2)}) async-start(s8[16777216]{0:T(1024)(128)(4,1)} %bitcast.14), calls=%async_computation.3 | async-start | bytes 8388608
  96.7 1.4 collective-permute-start.6
  98.1 4.7 %collective-permute-start.7 = (f32[96,256]{1,0:T(8,128)S(1)}, f32[96,256]{1,0:T(8,128)S(1)}, u32[]{:S(2)}, u32[]{:S(2)}) collective-permute-start(f32[96,256]{1,0:T(8,128)S(1)} %fusion.16), channel_id=1, source_target_pairs={{0,3},{1,2},{2,1},{3,0},{4,7},{5,6},{6,5},{7,4},{8,11},{9,10},{10,... | collective-permute-start | bytes 294920 | tf_op jit(solution)/shard_map/ppermute | solution.py:30
  102.8 5.5 %collective-permute-start.8 = (f32[96,256]{1,0:T(8,128)S(1)}, f32[96,256]{1,0:T(8,128)S(1)}, u32[]{:S(2)}, u32[]{:S(2)}) collective-permute-start(f32[96,256]{1,0:T(8,128)S(1)} %add.114), channel_id=1, source_target_pairs={{0,5},{1,4},{2,7},{3,6},{4,1},{5,0},{6,3},{7,2},{8,13},{9,12},{10,... | collective-permute-start | bytes 294920 | tf_op jit(solution)/shard_map/ppermute | solution.py:30
  108.3 7.6 %collective-permute-start.9 = (f32[96,256]{1,0:T(8,128)S(1)}, f32[96,256]{1,0:T(8,128)S(1)}, u32[]{:S(2)}, u32[]{:S(2)}) collective-permute-start(f32[96,256]{1,0:T(8,128)S(1)} %add.115), channel_id=1, source_target_pairs={{0,9},{1,8},{2,11},{3,10},{4,13},{5,12},{6,15},{7,14},{8,1},{9,0},... | collective-permute-start | bytes 294920 | tf_op jit(solution)/shard_map/ppermute | solution.py:30
  111.1 40.9 %collective-permute-start.16 = (bf16[48,8192]{1,0:T(8,128)(2,1)S(1)}, bf16[48,8192]{1,0:T(8,128)(2,1)S(1)}, u32[]{:S(2)}, u32[]{:S(2)}) collective-permute-start(bf16[48,8192]{1,0:T(8,128)(2,1)S(1)} %copy-done.2), channel_id=1, source_target_pairs={{0,16},{1,17},{2,18},{3,19},{4,20},{5,21},{6,22},{7,23},{8,24},{9,... | collective-permute-start | bytes 2359304 | tf_op jit(solution)/shard_map/ppermute | solution.py:30
  116.0 32.7 %copy-start.3 = (bf16[48,6144]{1,0:T(8,128)(2,1)S(1)}, bf16[48,6144]{1,0:T(8,128)(2,1)}, u32[]{:S(2)}) copy-start(bf16[48,6144]{1,0:T(8,128)(2,1)} %slice.43) | copy-start | bytes 1769476
  116.0 34.2 %copy-start.4 = (bf16[48,2048]{1,0:T(8,128)(2,1)S(1)}, bf16[48,2048]{1,0:T(8,128)(2,1)}, u32[]{:S(2)}) copy-start(bf16[48,2048]{1,0:T(8,128)(2,1)} %slice.44) | copy-start | bytes 589828
  140.6 1.3 collective-permute-start.11
  142.0 4.4 %collective-permute-start.12 = (f32[80,256]{1,0:T(8,128)S(1)}, f32[80,256]{1,0:T(8,128)S(1)}, u32[]{:S(2)}, u32[]{:S(2)}) collective-permute-start(f32[80,256]{1,0:T(8,128)S(1)} %dynamic-slice_add_fusion.1), channel_id=1, source_target_pairs={{0,3},{1,2},{2,1},{3,0},{4,7},{5,6},{6,5},{7,4},{8,11},{9,10},{10,... | collective-permute-start | bytes 245768 | tf_op jit(solution)/shard_map/ppermute | solution.py:30
  146.4 5.7 %collective-permute-start.13 = (f32[80,256]{1,0:T(8,128)S(1)}, f32[80,256]{1,0:T(8,128)S(1)}, u32[]{:S(2)}, u32[]{:S(2)}) collective-permute-start(f32[80,256]{1,0:T(8,128)S(1)} %add.118), channel_id=1, source_target_pairs={{0,5},{1,4},{2,7},{3,6},{4,1},{5,0},{6,3},{7,2},{8,13},{9,12},{10,... | collective-permute-start | bytes 245768 | tf_op jit(solution)/shard_map/ppermute | solution.py:30
  148.7 16.2 %collective-permute-start.17 = (bf16[48,6144]{1,0:T(8,128)(2,1)S(1)}, bf16[48,6144]{1,0:T(8,128)(2,1)S(1)}, u32[]{:S(2)}, u32[]{:S(2)}) collective-permute-start(bf16[48,6144]{1,0:T(8,128)(2,1)S(1)} %copy-done.3), channel_id=1, source_target_pairs={{0,16},{1,17},{2,18},{3,19},{4,20},{5,21},{6,22},{7,23},{8,24},{9,... | collective-permute-start | bytes 1769480 | tf_op jit(solution)/shard_map/ppermute | solution.py:30
  150.2 18.4 %collective-permute-start.18 = (bf16[48,2048]{1,0:T(8,128)(2,1)S(1)}, bf16[48,2048]{1,0:T(8,128)(2,1)S(1)}, u32[]{:S(2)}, u32[]{:S(2)}) collective-permute-start(bf16[48,2048]{1,0:T(8,128)(2,1)S(1)} %copy-done.4), channel_id=1, source_target_pairs={{0,16},{1,17},{2,18},{3,19},{4,20},{5,21},{6,22},{7,23},{8,24},{9,... | collective-permute-start | bytes 589832 | tf_op jit(solution)/shard_map/ppermute | solution.py:30
  152.1 12.8 %collective-permute-start.14 = (f32[80,256]{1,0:T(8,128)S(1)}, f32[80,256]{1,0:T(8,128)S(1)}, u32[]{:S(2)}, u32[]{:S(2)}) collective-permute-start(f32[80,256]{1,0:T(8,128)S(1)} %add.119), channel_id=1, source_target_pairs={{0,9},{1,8},{2,11},{3,10},{4,13},{5,12},{6,15},{7,14},{8,1},{9,0},... | collective-permute-start | bytes 245768 | tf_op jit(solution)/shard_map/ppermute | solution.py:30
  164.9 1.5 collective-permute-start.15
  166.2 14.4 %copy-start.1 = (bf16[512,1024]{1,0:T(8,128)(2,1)S(1)}, bf16[512,1024]{1,0:T(8,128)(2,1)}, u32[]{:S(2)}) copy-start(bf16[512,1024]{1,0:T(8,128)(2,1)} %param.8) | copy-start | bytes 3145732
  169.0 17.6 %copy-start.5 = (s32[448]{0:T(512)S(1)}, s32[448]{0:T(512)}, u32[]{:S(2)}) copy-start(s32[448]{0:T(512)} %param.9) | copy-start | bytes 5380
  169.1 1.3 collective-permute-start.19
  170.4 3.8 %collective-permute-start.20 = (f32[48,256]{1,0:T(8,128)S(1)}, f32[48,256]{1,0:T(8,128)S(1)}, u32[]{:S(2)}, u32[]{:S(2)}) collective-permute-start(f32[48,256]{1,0:T(8,128)S(1)} %dynamic-slice_add_fusion.2), channel_id=1, source_target_pairs={{0,3},{1,2},{2,1},{3,0},{4,7},{5,6},{6,5},{7,4},{8,11},{9,10},{10,... | collective-permute-start | bytes 147464 | tf_op jit(solution)/shard_map/ppermute | solution.py:30
  174.1 3.7 %collective-permute-start.21 = (f32[48,256]{1,0:T(8,128)S(1)}, f32[48,256]{1,0:T(8,128)S(1)}, u32[]{:S(2)}, u32[]{:S(2)}) collective-permute-start(f32[48,256]{1,0:T(8,128)S(1)} %add.124), channel_id=1, source_target_pairs={{0,5},{1,4},{2,7},{3,6},{4,1},{5,0},{6,3},{7,2},{8,13},{9,12},{10,... | collective-permute-start | bytes 147464 | tf_op jit(solution)/shard_map/ppermute | solution.py:30
  177.9 4.5 %collective-permute-start.22 = (f32[48,256]{1,0:T(8,128)S(1)}, f32[48,256]{1,0:T(8,128)S(1)}, u32[]{:S(2)}, u32[]{:S(2)}) collective-permute-start(f32[48,256]{1,0:T(8,128)S(1)} %add.125), channel_id=1, source_target_pairs={{0,9},{1,8},{2,11},{3,10},{4,13},{5,12},{6,15},{7,14},{8,1},{9,0},... | collective-permute-start | bytes 147464 | tf_op jit(solution)/shard_map/ppermute | solution.py:30
  182.4 3.3 %collective-permute-start.23 = (bf16[48,256]{1,0:T(8,128)(2,1)S(1)}, bf16[48,256]{1,0:T(8,128)(2,1)S(1)}, u32[]{:S(2)}, u32[]{:S(2)}) collective-permute-start(bf16[48,256]{1,0:T(8,128)(2,1)S(1)} %divide_convert_fusion.3), channel_id=1, source_target_pairs={{0,17},{1,16},{2,19},{3,18},{4,21},{5,20},{6,23},{7,22},{8,25},{9,... | collective-permute-start | bytes 73736 | tf_op jit(solution)/shard_map/ppermute | solution.py:30
  185.3 11.2 %collective-permute-start.25 = (bf16[400,512]{1,0:T(8,128)(2,1)S(1)}, bf16[400,512]{1,0:T(8,128)(2,1)S(1)}, u32[]{:S(2)}, u32[]{:S(2)}) collective-permute-start(bf16[400,512]{1,0:T(8,128)(2,1)S(1)} %pad_maximum_fusion.3), channel_id=1, source_target_pairs={{0,17},{1,16},{2,19},{3,18},{4,21},{5,20},{6,23},{7,22},{8,25},{9,... | collective-permute-start | bytes 1228808 | tf_op jit(solution)/shard_map/ppermute | solution.py:30
  185.7 1.8 collective-permute-start.24

commit v2 on v1

--- a/solution.py
+++ b/solution.py
@@ -34,33 +34,58 @@
     return lax.optimization_barrier((value, *needed))[0]
 
 
-def score_kernel(where_ref, whitened_ref, store_ref, index_ref, out_ref):
-    product = lax.dot_general(
-        whitened_ref[...], store_ref[...], CONTRACT_LAST, preferred_element_type=jnp.float32
-    )
-    columns = where_ref[1] + lax.broadcasted_iota(jnp.int32, product.shape, 1)
-    out_ref[...] = jnp.where(index_ref[...] == columns, jnp.zeros_like(product), product)
-
-
-def score(whitened, store, slab_index, row, first_column, row_groups):
-    rows = whitened.shape[0] // row_groups
-    directions = whitened.shape[1]
-    count = store.shape[0]
+def score_kernel(row_groups, rows, tail, _, *refs):
+    early = refs[:row_groups]
+    late_ref, pair_ref, store_ref, index_ref, out_ref = refs[row_groups:]
+    half = late_ref.shape[1]
+    same = index_ref[...] == lax.broadcasted_iota(jnp.int32, out_ref.shape, 1)
+
+    def dot(block, flip, part, size):
+        spot = (2 * flip + part) * half
+        return lax.dot_general(
+            block,
+            store_ref[:, spot : spot + size],
+            CONTRACT_LAST,
+            preferred_element_type=jnp.float32,
+        )
+
+    for place in range(row_groups):
+
+        @pl.when(pl.program_id(0) == place)
+        def _():
+            head, foot = 0.0, 0.0
+            for flip in range(row_groups):
+                block = (place ^ flip) * rows
+                head += dot(early[flip][block : block + rows - tail, :], flip, 0, 2 * half)
+                if place ^ flip == row_groups - 1:
+                    spot = flip * tail
+                    foot += dot(late_ref[spot : spot + tail, :], flip, 0, half)
+                    foot += dot(pair_ref[spot : spot + tail, :], flip, 1, half)
+                else:
+                    foot += dot(
+                        early[flip][block + rows - tail : block + rows, :], flip, 0, 2 * half
+                    )
+            product = jnp.concatenate([head, foot], 0)
+            out_ref[...] = jnp.where(same, jnp.zeros_like(product), product)
+
+
+def score(where, early, late, pair, store, slab_index, rows, tail):
+    row_groups, count = len(early), store.shape[0]
+    whole = [
+        pl.BlockSpec(a.shape, lambda a, where: (0, 0)) for a in (*early, late, pair, store)
+    ]
     return pl.pallas_call(
-        score_kernel,
-        out_shape=jax.ShapeDtypeStruct((whitened.shape[0], count), jnp.float32),
+        functools.partial(score_kernel, row_groups, rows, tail),
+        out_shape=jax.ShapeDtypeStruct((rows * row_groups, count), jnp.float32),
         grid_spec=pltpu.PrefetchScalarGridSpec(
             num_scalar_prefetch=1,
             grid=(row_groups,),
-            in_specs=[
-                pl.BlockSpec((rows, directions), lambda a, where: (a, 0)),
-                pl.BlockSpec((count, directions), lambda a, where: (0, 0)),
-                pl.BlockSpec((rows, 1), lambda a, where: (a ^ where[0], 0)),
-            ],
+            in_specs=whole + [pl.BlockSpec((rows, 1), lambda a, where: (a ^ where[0], 0))],
             out_specs=pl.BlockSpec((rows, count), lambda a, where: (a ^ where[0], 0)),
         ),
+        compiler_params=pltpu.CompilerParams(vmem_limit_bytes=24 << 20),
         name="score",
-    )(jnp.stack([row, first_column]).astype(jnp.int32), whitened, store, slab_index[:, None])
+    )(where, *early, late, pair, store, slab_index)
 
 
 def shards(slab_grads, basis, eigenvalues, store_rows, slab_index, *, row_groups, feat_groups):
@@ -76,18 +101,27 @@
     def cross(value, flip):
         return swap(value, row_flip=flip, feat_flip=bin(flip).count("1") & 1)
 
-    tail = max(rows * 3 // 14 // 16 * 16, 16)
-    lead = 16
-    middle = lead + (rows - tail - lead) // 16 * 8
-    cuts = [0, lead, middle, rows - tail]
-    feature_cuts = [0, features // 2, features * 7 // 8, features]
+    tail = max(rows // 7 // 16 * 16, 16)
+    near = (rows - tail) * 2 // 3 // 16 * 16
+    lead = min(32, near // 2)
+    quarter = features // 4
+    cuts = [
+        (0, lead, 0, quarter),
+        (0, lead, quarter, features),
+        (lead, near, 0, features),
+        (near, rows - tail, 0, features),
+        (rows - tail, rows, 0, 2 * quarter),
+        (rows - tail, rows, 2 * quarter, features - quarter // 2),
+        (rows - tail, rows, features - quarter // 2, features),
+    ]
 
     last = row_groups - 1
     far = [swap(slab_grads, row_flip=flip, feat_flip=0) for flip in range(1, last)]
-    head = slab_grads[:lead]
-    rest = after(slab_grads, head)
-    pieces = [head] + [rest[a:b] for a, b in zip(cuts[1:-1], cuts[2:])]
-    pieces += [rest[rows - tail :, a:b] for a, b in zip(feature_cuts[:-1], feature_cuts[1:])]
+    pieces, ready = [], slab_grads
+    for i, (r0, r1, f0, f1) in enumerate(cuts):
+        pieces.append(ready[r0:r1, f0:f1])
+        if i < 2:
+            ready = after(slab_grads, pieces[-1])
     moved = []
     for piece in pieces:
         moved.append(swap(piece, row_flip=last, feat_flip=0))
@@ -101,9 +135,14 @@
         for part in (side, 1 - side):
             order.append(lax.dynamic_slice_in_dim(store_rows, base + part * half, half, 1))
     store = jnp.concatenate(order, 1)
-
-    def project(block, a=0, b=features):
-        return jnp.dot(block, basis[a:b], preferred_element_type=jnp.float32)
+    where = row.astype(jnp.int32).reshape(1)
+    index = slab_index[:, None] - first_column
+
+    def project(i, *needed):
+        _, _, f0, f1 = cuts[i]
+        return jnp.dot(
+            after(moved[i], *needed), basis[f0:f1], preferred_element_type=jnp.float32
+        )
 
     def halves(partial_value):
         mine = lax.dynamic_slice_in_dim(partial_value, side * half, half, 1)
@@ -124,41 +163,29 @@
     def reduce(partial_value):
         return whiten(list(totals(halves(partial_value)))[-1])
 
-    early = [reduce(project(after(slab_grads, *pieces)))]
-    for block in far:
-        early.append(reduce(project(after(block, early[-1]))))
-    first, second, third = moved[:3]
-    lead_value = project(after(first, early[-1]))
-    near = project(after(second, early[-1], lead_value))
-    early.append(reduce(jnp.concatenate([lead_value, near], 0)))
-    middle = project(after(third, early[-1]))
+    blocks = [after(slab_grads, *pieces)] + far
+    early = []
+    for block in blocks:
+        early.append(
+            reduce(jnp.dot(after(block, *early), basis, preferred_element_type=jnp.float32))
+        )
+    first = project(0, early[-1], store, where, index)
+    first += project(1, first)
+    early.append(reduce(jnp.concatenate([first, project(2, first)], 0)))
+    middle = project(3, early[-1])
     middle_totals = list(totals(halves(middle)))
     early.append(whiten(middle_totals[-1]))
     early = jnp.concatenate(early, 0)
     early = jnp.concatenate([early, swap(early, row_flip=0, feat_flip=1)], 1)
     early = [early] + [cross(early, flip) for flip in range(1, row_groups)]
 
-    late = project(after(moved[3], middle_totals[1]), *feature_cuts[:2])
-    late += project(after(moved[4], late, middle_totals[2]), *feature_cuts[1:3])
-    late += project(after(moved[5], late, early[0]), *feature_cuts[2:])
+    late = project(4, middle_totals[1])
+    late += project(5, late, early[0])
+    late += project(6, late)
     late = reduce(late)
     late = jnp.concatenate([late] + [cross(late, flip) for flip in range(1, row_groups)], 0)
     pair = swap(late, row_flip=0, feat_flip=1)
-    late = [
-        jnp.concatenate([late[f * tail : (f + 1) * tail], pair[f * tail : (f + 1) * tail]], 1)
-        for f in range(row_groups)
-    ]
-    columns = []
-    for flip in range(row_groups):
-        whole = jnp.concatenate([early[flip], late[flip]], 0)
-        order = [a ^ flip for a in range(row_groups)]
-        columns.append(
-            whole
-            if flip == 0
-            else jnp.concatenate([whole[i * rows : (i + 1) * rows] for i in order], 0)
-        )
-    whitened = jnp.concatenate(columns, 1)
-    return score(whitened, store, slab_index, row, first_column, row_groups)
+    return score(where, early, late, pair, store, index, rows, tail)
 
 
 def plain(slab_grads, basis, eigenvalues, store_rows, slab_index, *, row_groups, feat_groups):

time: 202 us -> 199 us (0.985)
    add x8, other arithmetic: 0.12 us -> 2.79 us  [totals(): total = total + swap(total, row_flip=0, feat_flip=bit | 1)]
    ppermute x26 -> x27, waiting for transfers between devices: 113 us -> 111 us  [exchange(): return lax.ppermute(value, ('rows', 'feat'), pairs)]
    ppermute x26 -> x27, starting transfers between devices: 35.3 us -> 35.2 us  [exchange(): return lax.ppermute(value, ('rows', 'feat'), pairs)]
    dot_general x7 -> x8, matrix products: 32.9 us -> 32.9 us  [the longest x7 25 us: project(): jnp.dot(after(moved[i], *needed), basis[f0:f1], preferred_element_type=jn...]
  transfers between devices with their start and end apart: 26 -> 27, of which waited for: 22 -> 23; matrix products, arithmetic and copies ran while one was open for 20% -> 21% of each run, Pallas kernels for 0% -> 0%
where the time goes in v2:
time: 199 us
  waiting for transfers between devices  111 us (56%)
  starting transfers between devices  35.2 us (18%)
  matrix products  32.9 us (17%)
  local copies, waits for them, and re-layouts  12.4 us (6%)
  other arithmetic  5.03 us (3%)
  Pallas kernels  2.49 us (1%)
    ppermute x27, waiting for transfers between devices, exchange(): return lax.ppermute(value, ('rows', 'feat'), pairs)  111 us
    ppermute x27, starting transfers between devices, exchange(): return lax.ppermute(value, ('rows', 'feat'), pairs)  35.2 us
    dot_general x7, matrix products, project(): jnp.dot(after(moved[i], *needed), basis[f0:f1], preferred_element_type=jn...  25 us
    slice x7, local copies, waits for them, and re-layouts, shards(): pieces.append(ready[r0:r1, f0:f1])  11.2 us
    dot_general x1, matrix products, shards(): jnp.dot(after(block, *early), basis, preferred_element_type=jnp.float32)  7.95 us
  transfers between devices with their start and end apart: 27, of which 23 were waited for; matrix products, arithmetic and copies ran while one was open for 21% of the time, Pallas kernels for 0%

profile of v2, /device:TPU:0, one launch (start us, length us, event | category | flops | bytes accessed | tf_op | source)
XLA Modules:
  0.0 199.2 jit_solution(13527953014775424535)
XLA Ops:
  0.0 1.8 slice.36
  1.9 2.5 %slice.37 = bf16[32,12288]{1,0:T(8,128)(2,1)} slice(bf16[224,16384]{1,0:T(8,128)(2,1)} %param.5), slice={[0:32], [4096:16384]} | slice | bytes 1572864 | tf_op jit(solution)/shard_map/slice | solution.py:122
  4.3 3.7 %slice.38 = bf16[96,16384]{1,0:T(8,128)(2,1)} slice(bf16[224,16384]{1,0:T(8,128)(2,1)} %param.5), slice={[32:128], [0:16384]} | slice | bytes 6291456 | tf_op jit(solution)/shard_map/slice | solution.py:122
  8.0 3.0 %collective-permute-start.6 = (bf16[96,16384]{1,0:T(8,128)(2,1)}, bf16[96,16384]{1,0:T(8,128)(2,1)}, u32[]{:S(2)}, u32[]{:S(2)}) collective-permute-start(bf16[96,16384]{1,0:T(8,128)(2,1)} %slice.38), channel_id=1, source_target_pairs={{0,16},{1,17},{2,18},{3,19},{4,20},{5,21},{6,22},{7,23},{8,24},{9,... | collective-permute-start | bytes 9437192 | tf_op jit(solution)/shard_map/ppermute | solution.py:30
  11.0 1.5 slice.39
  12.6 0.8 slice.40
  13.4 0.8 slice.41
  14.2 7.9 %fusion.22 = f32[224,512]{1,0:T(8,128)S(1)} fusion(bf16[224,16384]{1,0:T(8,128)(2,1)S(1)} %copy-done, bf16[16384,512]{1,0:T(8,128)(2,1)} %param.6), kind=kOutput, calls=%fused_computation.40 | convolution fusion | flops 3758096384 | bytes 24576000 | tf_op jit(solution)/shard_map/dot_general | solution.py:170
  22.3 1.5 collective-permute-done
  23.8 1.3 collective-permute-start.1
  25.2 0.5 collective-permute-start.4
  25.7 1.5 collective-permute-start.5
  27.2 0.5 collective-permute-start.11
  27.7 3.9 %collective-permute-done.1 = f32[224,256]{1,0:T(8,128)} collective-permute-done((f32[224,256]{1,0:T(8,128)S(1)}, f32[224,256]{1,0:T(8,128)}, u32[]{:S(2)}, u32[]{:S(2)}) %collective-permute-start.1) | collective-permute-done | bytes 229408 | tf_op jit(solution)/shard_map/ppermute | solution.py:30
  31.6 1.7 add.108
  33.2 1.6 collective-permute-start.2
  34.9 0.9 constant_dynamic-slice_fusion.5
  35.8 5.0 %collective-permute-done.2 = f32[224,256]{1,0:T(8,128)} collective-permute-done((f32[224,256]{1,0:T(8,128)}, f32[224,256]{1,0:T(8,128)}, u32[]{:S(2)}, u32[]{:S(2)}) %collective-permute-start.2) | collective-permute-done | bytes 229408 | tf_op jit(solution)/shard_map/ppermute | solution.py:30
  40.8 1.1 add.109
  41.9 3.0 %collective-permute-start.3 = (f32[224,256]{1,0:T(8,128)S(1)}, f32[224,256]{1,0:T(8,128)S(1)}, u32[]{:S(2)}, u32[]{:S(2)}) collective-permute-start(f32[224,256]{1,0:T(8,128)S(1)} %add.109), channel_id=1, source_target_pairs={{0,9},{1,8},{2,11},{3,10},{4,13},{5,12},{6,15},{7,14},{8,1},{9,0},... | collective-permute-start | bytes 688136 | tf_op jit(solution)/shard_map/ppermute | solution.py:30
  44.9 1.2 pad_maximum_fusion.refs_4_
  46.2 0.8 dynamic-slice_add_fusion.3
  47.0 8.4 %collective-permute-done.3 = f32[224,256]{1,0:T(8,128)S(1)} collective-permute-done((f32[224,256]{1,0:T(8,128)S(1)}, f32[224,256]{1,0:T(8,128)S(1)}, u32[]{:S(2)}, u32[]{:S(2)}) %collective-permute-start.3) | collective-permute-done | bytes 229408 | tf_op jit(solution)/shard_map/ppermute | solution.py:30
  55.4 30.5 %collective-permute-done.4 = bf16[32,4096]{1,0:T(8,128)(2,1)} collective-permute-done((bf16[32,4096]{1,0:T(8,128)(2,1)}, bf16[32,4096]{1,0:T(8,128)(2,1)}, u32[]{:S(2)}, u32[]{:S(2)}) %collective-permute-start.4) | collective-permute-done | bytes 262176 | tf_op jit(solution)/shard_map/ppermute | solution.py:30
  85.9 3.1 %fusion.6 = f32[32,512]{1,0:T(8,128)S(1)} fusion(bf16[32,4096]{1,0:T(8,128)(2,1)} %collective-permute-done.4, bf16[16384,512]{1,0:T(8,128)(2,1)} %param.6), kind=kOutput, calls=%fused_computation.6 | convolution fusion | flops 134217728 | bytes 4521984 | tf_op jit(solution)/shard_map/dot_general | solution.py:143
  89.0 13.8 %collective-permute-done.5 = bf16[32,12288]{1,0:T(8,128)(2,1)} collective-permute-done((bf16[32,12288]{1,0:T(8,128)(2,1)}, bf16[32,12288]{1,0:T(8,128)(2,1)}, u32[]{:S(2)}, u32[]{:S(2)}) %collective-permute-start.5) | collective-permute-done | bytes 786464 | tf_op jit(solution)/shard_map/ppermute | solution.py:30
  102.8 6.2 %fusion.16 = f32[32,512]{1,0:T(8,128)S(1)} fusion(f32[32,512]{1,0:T(8,128)S(1)} %fusion.6, bf16[32,12288]{1,0:T(8,128)(2,1)} %collective-permute-done.5, bf16[16384,512]{1,0:T(8,128)(2,1)} %param.6), kind=kOutput, calls=%fused_computation.12 | convolution fusion | flops 402669568 | bytes 13500416 | tf_op jit(solution)/shard_map/dot_general | solution.py:143
  109.0 9.6 %fusion.23 = f32[96,512]{1,0:T(8,128)S(1)} fusion(bf16[96,16384]{1,0:T(8,128)(2,1)} %collective-permute-done.6, bf16[16384,512]{1,0:T(8,128)(2,1)} %param.6), kind=kOutput, calls=%fused_computation.41 | convolution fusion | flops 1610612736 | bytes 20119552 | tf_op jit(solution)/shard_map/dot_general | solution.py:143
  118.7 1.3 collective-permute-done.7
  120.1 1.9 collective-permute-start.8
  121.9 3.6 %collective-permute-done.8 = f32[128,256]{1,0:T(8,128)S(1)} collective-permute-done((f32[128,256]{1,0:T(8,128)S(1)}, f32[128,256]{1,0:T(8,128)S(1)}, u32[]{:S(2)}, u32[]{:S(2)}) %collective-permute-start.8) | collective-permute-done | bytes 131104 | tf_op jit(solution)/shard_map/ppermute | solution.py:30
  125.5 2.3 %collective-permute-start.9 = (f32[128,256]{1,0:T(8,128)S(1)}, f32[128,256]{1,0:T(8,128)S(1)}, u32[]{:S(2)}, u32[]{:S(2)}) collective-permute-start(f32[128,256]{1,0:T(8,128)S(1)} %add.124), channel_id=1, source_target_pairs={{0,5},{1,4},{2,7},{3,6},{4,1},{5,0},{6,3},{7,2},{8,13},{9,12},{10,... | collective-permute-start | bytes 393224 | tf_op jit(solution)/shard_map/ppermute | solution.py:30
  127.8 3.8 %collective-permute-done.9 = f32[128,256]{1,0:T(8,128)S(1)} collective-permute-done((f32[128,256]{1,0:T(8,128)S(1)}, f32[128,256]{1,0:T(8,128)S(1)}, u32[]{:S(2)}, u32[]{:S(2)}) %collective-permute-start.9) | collective-permute-done | bytes 131104 | tf_op jit(solution)/shard_map/ppermute | solution.py:30
  131.6 2.8 %collective-permute-start.10 = (f32[128,256]{1,0:T(8,128)S(1)}, f32[128,256]{1,0:T(8,128)S(1)}, u32[]{:S(2)}, u32[]{:S(2)}) collective-permute-start(f32[128,256]{1,0:T(8,128)S(1)} %add.125), channel_id=1, source_target_pairs={{0,9},{1,8},{2,11},{3,10},{4,13},{5,12},{6,15},{7,14},{8,1},{9,0},... | collective-permute-start | bytes 393224 | tf_op jit(solution)/shard_map/ppermute | solution.py:30
  134.4 1.5 collective-permute-start.18
  135.9 4.9 %collective-permute-done.10 = f32[128,256]{1,0:T(8,128)S(1)} collective-permute-done((f32[128,256]{1,0:T(8,128)S(1)}, f32[128,256]{1,0:T(8,128)S(1)}, u32[]{:S(2)}, u32[]{:S(2)}) %collective-permute-start.10) | collective-permute-done | bytes 131104 | tf_op jit(solution)/shard_map/ppermute | solution.py:30
  140.8 6.8 %collective-permute-done.11 = bf16[64,16384]{1,0:T(8,128)(2,1)S(1)} collective-permute-done((bf16[64,16384]{1,0:T(8,128)(2,1)}, bf16[64,16384]{1,0:T(8,128)(2,1)S(1)}, u32[]{:S(2)}, u32[]{:S(2)}) %collective-permute-start.11) | collective-permute-done | bytes 2097184 | tf_op jit(solution)/shard_map/ppermute | solution.py:30
  147.6 3.0 %fusion.24 = f32[64,512]{1,0:T(8,128)S(1)} fusion(bf16[64,16384]{1,0:T(8,128)(2,1)S(1)} %collective-permute-done.11, bf16[16384,512]{1,0:T(8,128)(2,1)S(1)} %bitcast.14), kind=kOutput, calls=%fused_computation.42 | convolution fusion | flops 1073741824 | bytes 19005440 | tf_op jit(solution)/shard_map/dot_general | solution.py:143
  150.7 1.2 collective-permute-done.12
  152.0 1.9 collective-permute-start.13
  153.8 2.1 %collective-permute-done.13 = f32[64,256]{1,0:T(8,128)S(1)} collective-permute-done((f32[64,256]{1,0:T(8,128)S(1)}, f32[64,256]{1,0:T(8,128)S(1)}, u32[]{:S(2)}, u32[]{:S(2)}) %collective-permute-start.13) | collective-permute-done | bytes 65568 | tf_op jit(solution)/shard_map/ppermute | solution.py:30
  156.0 2.3 %collective-permute-start.14 = (f32[64,256]{1,0:T(8,128)S(1)}, f32[64,256]{1,0:T(8,128)S(1)}, u32[]{:S(2)}, u32[]{:S(2)}) collective-permute-start(f32[64,256]{1,0:T(8,128)S(1)} %add.128), channel_id=1, source_target_pairs={{0,5},{1,4},{2,7},{3,6},{4,1},{5,0},{6,3},{7,2},{8,13},{9,12},{10,... | collective-permute-start | bytes 196616 | tf_op jit(solution)/shard_map/ppermute | solution.py:30
  158.3 2.4 %collective-permute-done.14 = f32[64,256]{1,0:T(8,128)S(1)} collective-permute-done((f32[64,256]{1,0:T(8,128)S(1)}, f32[64,256]{1,0:T(8,128)S(1)}, u32[]{:S(2)}, u32[]{:S(2)}) %collective-permute-start.14) | collective-permute-done | bytes 65568 | tf_op jit(solution)/shard_map/ppermute | solution.py:30
  160.7 2.5 %collective-permute-start.15 = (f32[64,256]{1,0:T(8,128)S(1)}, f32[64,256]{1,0:T(8,128)S(1)}, u32[]{:S(2)}, u32[]{:S(2)}) collective-permute-start(f32[64,256]{1,0:T(8,128)S(1)} %add.129), channel_id=1, source_target_pairs={{0,9},{1,8},{2,11},{3,10},{4,13},{5,12},{6,15},{7,14},{8,1},{9,0},... | collective-permute-start | bytes 196616 | tf_op jit(solution)/shard_map/ppermute | solution.py:30
  163.2 1.5 collective-permute-start.19
  164.7 0.5 collective-permute-start.20
  165.2 2.0 collective-permute-done.15
  167.4 1.5 fusion.2
  169.0 6.2 %collective-permute-done.19 = bf16[32,6144]{1,0:T(8,128)(2,1)S(1)} collective-permute-done((bf16[32,6144]{1,0:T(8,128)(2,1)S(1)}, bf16[32,6144]{1,0:T(8,128)(2,1)S(1)}, u32[]{:S(2)}, u32[]{:S(2)}) %collective-permute-start.19) | collective-permute-done | bytes 393248 | tf_op jit(solution)/shard_map/ppermute | solution.py:30
  175.2 1.2 fusion.13
  176.3 0.7 collective-permute-done.20
  177.1 0.5 fusion.10
  177.6 1.2 collective-permute-done.21
  178.8 1.3 collective-permute-start.22
  180.1 2.1 %collective-permute-done.22 = f32[32,256]{1,0:T(8,128)S(1)} collective-permute-done((f32[32,256]{1,0:T(8,128)S(1)}, f32[32,256]{1,0:T(8,128)S(1)}, u32[]{:S(2)}, u32[]{:S(2)}) %collective-permute-start.22) | collective-permute-done | bytes 32800 | tf_op jit(solution)/shard_map/ppermute | solution.py:30
  182.2 1.3 collective-permute-start.23
  183.5 1.4 collective-permute-start.17
  185.0 0.6 collective-permute-done.23
  185.5 0.4 collective-permute-start.24
  185.9 3.9 %collective-permute-done.24 = f32[32,256]{1,0:T(8,128)S(1)} collective-permute-done((f32[32,256]{1,0:T(8,128)S(1)}, f32[32,256]{1,0:T(8,128)S(1)}, u32[]{:S(2)}, u32[]{:S(2)}) %collective-permute-start.24) | collective-permute-done | bytes 32800 | tf_op jit(solution)/shard_map/ppermute | solution.py:30
  189.8 1.3 collective-permute-start.25
  191.1 4.4 %collective-permute-done.25 = bf16[32,256]{1,0:T(8,128)(2,1)S(1)} collective-permute-done((bf16[32,256]{1,0:T(8,128)(2,1)S(1)}, bf16[32,256]{1,0:T(8,128)(2,1)S(1)}, u32[]{:S(2)}, u32[]{:S(2)}) %collective-permute-start.25) | collective-permute-done | bytes 16416 | tf_op jit(solution)/shard_map/ppermute | solution.py:30
  196.0 0.7 collective-permute-done.26.refs_3_
  196.7 2.5 %score.1 = f32[448,512]{1,0:T(8,128)} custom-call(s32[1]{0:T(128)} %bitcast._, bf16[416,512]{1,0:T(8,128)(2,1)S(1)} %pad_maximum_fusion.1.refs_0_, bf16[416,512]{1,0:T(8,128)(2,1)S(1)} %collective-permute-done.17.refs_1_, bf16[64,256]{1,0:T(8,128)(2,1)S(1)} %pad_maximum_fusion.3.refs_2_, bf16[64,256]{1,0:T(8,128)(2,1)S(1)} %collective-permute-done.26.refs_3_, ...), custom_call_target="tpu_custom_call" | custom-call | tf_op jit(solution)/shard_map/score/pallas_call | solution.py:77
  (53 shorter events, 1.4 us)
Async XLA Ops:
  0.0 11.0 %copy-start = (bf16[224,16384]{1,0:T(8,128)(2,1)S(1)}, bf16[224,16384]{1,0:T(8,128)(2,1)}, u32[]{:S(2)}) copy-start(bf16[224,16384]{1,0:T(8,128)(2,1)} %param.5) | copy-start | bytes 22020100
  8.0 100.9 %collective-permute-start.6 = (bf16[96,16384]{1,0:T(8,128)(2,1)}, bf16[96,16384]{1,0:T(8,128)(2,1)}, u32[]{:S(2)}, u32[]{:S(2)}) collective-permute-start(bf16[96,16384]{1,0:T(8,128)(2,1)} %slice.38), channel_id=1, source_target_pairs={{0,16},{1,17},{2,18},{3,19},{4,20},{5,21},{6,22},{7,23},{8,24},{9,... | collective-permute-start | bytes 9437192 | tf_op jit(solution)/shard_map/ppermute | solution.py:30
  14.2 20.7 %copy-start.1 = (bf16[512,1024]{1,0:T(8,128)(2,1)S(1)}, bf16[512,1024]{1,0:T(8,128)(2,1)}, u32[]{:S(2)}) copy-start(bf16[512,1024]{1,0:T(8,128)(2,1)} %param.8) | copy-start | bytes 3145732
  14.2 21.6 %copy-start.4 = (s32[448]{0:T(512)S(1)}, s32[448]{0:T(512)}, u32[]{:S(2)}) copy-start(s32[448]{0:T(512)} %param.9) | copy-start | bytes 5380
  22.2 1.6 collective-permute-start
  23.8 7.8 %collective-permute-start.1 = (f32[224,256]{1,0:T(8,128)S(1)}, f32[224,256]{1,0:T(8,128)}, u32[]{:S(2)}, u32[]{:S(2)}) collective-permute-start(f32[224,256]{1,0:T(8,128)S(1)} %dynamic-slice_add_fusion), channel_id=1, source_target_pairs={{0,3},{1,2},{2,1},{3,0},{4,7},{5,6},{6,5},{7,4},{8,11},{9,10},{10,... | collective-permute-start | bytes 688136 | tf_op jit(solution)/shard_map/ppermute | solution.py:30
  25.2 60.7 %collective-permute-start.4 = (bf16[32,4096]{1,0:T(8,128)(2,1)}, bf16[32,4096]{1,0:T(8,128)(2,1)}, u32[]{:S(2)}, u32[]{:S(2)}) collective-permute-start(bf16[32,4096]{1,0:T(8,128)(2,1)} %slice.36), channel_id=1, source_target_pairs={{0,16},{1,17},{2,18},{3,19},{4,20},{5,21},{6,22},{7,23},{8,24},{9,... | collective-permute-start | bytes 786440 | tf_op jit(solution)/shard_map/ppermute | solution.py:30
  25.7 77.0 %collective-permute-start.5 = (bf16[32,12288]{1,0:T(8,128)(2,1)}, bf16[32,12288]{1,0:T(8,128)(2,1)}, u32[]{:S(2)}, u32[]{:S(2)}) collective-permute-start(bf16[32,12288]{1,0:T(8,128)(2,1)} %slice.37), channel_id=1, source_target_pairs={{0,16},{1,17},{2,18},{3,19},{4,20},{5,21},{6,22},{7,23},{8,24},{9,... | collective-permute-start | bytes 2359304 | tf_op jit(solution)/shard_map/ppermute | solution.py:30
  27.2 120.4 %collective-permute-start.11 = (bf16[64,16384]{1,0:T(8,128)(2,1)}, bf16[64,16384]{1,0:T(8,128)(2,1)S(1)}, u32[]{:S(2)}, u32[]{:S(2)}) collective-permute-start(bf16[64,16384]{1,0:T(8,128)(2,1)} %slice.39), channel_id=1, source_target_pairs={{0,16},{1,17},{2,18},{3,19},{4,20},{5,21},{6,22},{7,23},{8,24},{9,... | collective-permute-start | bytes 6291464 | tf_op jit(solution)/shard_map/ppermute | solution.py:30
  33.2 7.6 %collective-permute-start.2 = (f32[224,256]{1,0:T(8,128)}, f32[224,256]{1,0:T(8,128)}, u32[]{:S(2)}, u32[]{:S(2)}) collective-permute-start(f32[224,256]{1,0:T(8,128)} %add.108), channel_id=1, source_target_pairs={{0,5},{1,4},{2,7},{3,6},{4,1},{5,0},{6,3},{7,2},{8,13},{9,12},{10,... | collective-permute-start | bytes 688136 | tf_op jit(solution)/shard_map/ppermute | solution.py:30
  41.9 13.5 %collective-permute-start.3 = (f32[224,256]{1,0:T(8,128)S(1)}, f32[224,256]{1,0:T(8,128)S(1)}, u32[]{:S(2)}, u32[]{:S(2)}) collective-permute-start(f32[224,256]{1,0:T(8,128)S(1)} %add.109), channel_id=1, source_target_pairs={{0,9},{1,8},{2,11},{3,10},{4,13},{5,12},{6,15},{7,14},{8,1},{9,0},... | collective-permute-start | bytes 688136 | tf_op jit(solution)/shard_map/ppermute | solution.py:30
  102.7 44.8 %slice-start = ((s8[16777216]{0:T(1024)(128)(4,1)}), s8[4194304]{0:T(1024)(128)(4,1)S(1)}, s32[]{:S(2)}) async-start(s8[16777216]{0:T(1024)(128)(4,1)} %bitcast.13), calls=%async_computation | async-start | bytes 8388608
  102.7 44.8 %slice-start.1 = ((s8[16777216]{0:T(1024)(128)(4,1)}), s8[4194304]{0:T(1024)(128)(4,1)S(1)}, s32[]{:S(2)}) async-start(s8[16777216]{0:T(1024)(128)(4,1)} %bitcast.13), calls=%async_computation.1 | async-start | bytes 8388608
  108.9 25.5 %copy-start.2 = (bf16[32,8192]{1,0:T(8,128)(2,1)S(1)}, bf16[32,8192]{1,0:T(8,128)(2,1)}, u32[]{:S(2)}) copy-start(bf16[32,8192]{1,0:T(8,128)(2,1)} %slice.40) | copy-start | bytes 1572868
  109.0 38.6 %slice-start.2 = ((s8[16777216]{0:T(1024)(128)(4,1)}), s8[4194304]{0:T(1024)(128)(4,1)S(1)}, s32[]{:S(2)}) async-start(s8[16777216]{0:T(1024)(128)(4,1)} %bitcast.13), calls=%async_computation.2 | async-start | bytes 8388608
  109.0 38.6 %slice-start.3 = ((s8[16777216]{0:T(1024)(128)(4,1)}), s8[4194304]{0:T(1024)(128)(4,1)S(1)}, s32[]{:S(2)}) async-start(s8[16777216]{0:T(1024)(128)(4,1)} %bitcast.13), calls=%async_computation.3 | async-start | bytes 8388608
  118.6 1.4 collective-permute-start.7
  120.1 5.4 %collective-permute-start.8 = (f32[128,256]{1,0:T(8,128)S(1)}, f32[128,256]{1,0:T(8,128)S(1)}, u32[]{:S(2)}, u32[]{:S(2)}) collective-permute-start(f32[128,256]{1,0:T(8,128)S(1)} %fusion.21), channel_id=1, source_target_pairs={{0,3},{1,2},{2,1},{3,0},{4,7},{5,6},{6,5},{7,4},{8,11},{9,10},{10,... | collective-permute-start | bytes 393224 | tf_op jit(solution)/shard_map/ppermute | solution.py:30
  125.5 6.1 %collective-permute-start.9 = (f32[128,256]{1,0:T(8,128)S(1)}, f32[128,256]{1,0:T(8,128)S(1)}, u32[]{:S(2)}, u32[]{:S(2)}) collective-permute-start(f32[128,256]{1,0:T(8,128)S(1)} %add.124), channel_id=1, source_target_pairs={{0,5},{1,4},{2,7},{3,6},{4,1},{5,0},{6,3},{7,2},{8,13},{9,12},{10,... | collective-permute-start | bytes 393224 | tf_op jit(solution)/shard_map/ppermute | solution.py:30
  131.6 9.1 %collective-permute-start.10 = (f32[128,256]{1,0:T(8,128)S(1)}, f32[128,256]{1,0:T(8,128)S(1)}, u32[]{:S(2)}, u32[]{:S(2)}) collective-permute-start(f32[128,256]{1,0:T(8,128)S(1)} %add.125), channel_id=1, source_target_pairs={{0,9},{1,8},{2,11},{3,10},{4,13},{5,12},{6,15},{7,14},{8,1},{9,0},... | collective-permute-start | bytes 393224 | tf_op jit(solution)/shard_map/ppermute | solution.py:30
  134.4 30.8 %collective-permute-start.18 = (bf16[32,8192]{1,0:T(8,128)(2,1)S(1)}, bf16[32,8192]{1,0:T(8,128)(2,1)S(1)}, u32[]{:S(2)}, u32[]{:S(2)}) collective-permute-start(bf16[32,8192]{1,0:T(8,128)(2,1)S(1)} %copy-done.2), channel_id=1, source_target_pairs={{0,16},{1,17},{2,18},{3,19},{4,20},{5,21},{6,22},{7,23},{8,24},{9,... | collective-permute-start | bytes 1572872 | tf_op jit(solution)/shard_map/ppermute | solution.py:30
  140.8 22.4 %copy-start.3 = (bf16[32,6144]{1,0:T(8,128)(2,1)S(1)}, bf16[32,6144]{1,0:T(8,128)(2,1)}, u32[]{:S(2)}) copy-start(bf16[32,6144]{1,0:T(8,128)(2,1)} %slice.41) | copy-start | bytes 1179652
  150.6 1.3 collective-permute-start.12
  152.0 4.0 %collective-permute-start.13 = (f32[64,256]{1,0:T(8,128)S(1)}, f32[64,256]{1,0:T(8,128)S(1)}, u32[]{:S(2)}, u32[]{:S(2)}) collective-permute-start(f32[64,256]{1,0:T(8,128)S(1)} %dynamic-slice_add_fusion.1), channel_id=1, source_target_pairs={{0,3},{1,2},{2,1},{3,0},{4,7},{5,6},{6,5},{7,4},{8,11},{9,10},{10,... | collective-permute-start | bytes 196616 | tf_op jit(solution)/shard_map/ppermute | solution.py:30
  156.0 4.7 %collective-permute-start.14 = (f32[64,256]{1,0:T(8,128)S(1)}, f32[64,256]{1,0:T(8,128)S(1)}, u32[]{:S(2)}, u32[]{:S(2)}) collective-permute-start(f32[64,256]{1,0:T(8,128)S(1)} %add.128), channel_id=1, source_target_pairs={{0,5},{1,4},{2,7},{3,6},{4,1},{5,0},{6,3},{7,2},{8,13},{9,12},{10,... | collective-permute-start | bytes 196616 | tf_op jit(solution)/shard_map/ppermute | solution.py:30
  160.7 6.5 %collective-permute-start.15 = (f32[64,256]{1,0:T(8,128)S(1)}, f32[64,256]{1,0:T(8,128)S(1)}, u32[]{:S(2)}, u32[]{:S(2)}) collective-permute-start(f32[64,256]{1,0:T(8,128)S(1)} %add.129), channel_id=1, source_target_pairs={{0,9},{1,8},{2,11},{3,10},{4,13},{5,12},{6,15},{7,14},{8,1},{9,0},... | collective-permute-start | bytes 196616 | tf_op jit(solution)/shard_map/ppermute | solution.py:30
  163.2 12.0 %collective-permute-start.19 = (bf16[32,6144]{1,0:T(8,128)(2,1)S(1)}, bf16[32,6144]{1,0:T(8,128)(2,1)S(1)}, u32[]{:S(2)}, u32[]{:S(2)}) collective-permute-start(bf16[32,6144]{1,0:T(8,128)(2,1)S(1)} %copy-done.3), channel_id=1, source_target_pairs={{0,16},{1,17},{2,18},{3,19},{4,20},{5,21},{6,22},{7,23},{8,24},{9,... | collective-permute-start | bytes 1179656 | tf_op jit(solution)/shard_map/ppermute | solution.py:30
  164.7 12.4 %collective-permute-start.20 = (bf16[32,2048]{1,0:T(8,128)(2,1)S(1)}, bf16[32,2048]{1,0:T(8,128)(2,1)S(1)}, u32[]{:S(2)}, u32[]{:S(2)}) collective-permute-start(bf16[32,2048]{1,0:T(8,128)(2,1)S(1)} %slice.42), channel_id=1, source_target_pairs={{0,16},{1,17},{2,18},{3,19},{4,20},{5,21},{6,22},{7,23},{8,24},{9,... | collective-permute-start | bytes 393224 | tf_op jit(solution)/shard_map/ppermute | solution.py:30
  167.2 1.7 collective-permute-start.16
  177.5 1.3 collective-permute-start.21
  178.8 3.3 %collective-permute-start.22 = (f32[32,256]{1,0:T(8,128)S(1)}, f32[32,256]{1,0:T(8,128)S(1)}, u32[]{:S(2)}, u32[]{:S(2)}) collective-permute-start(f32[32,256]{1,0:T(8,128)S(1)} %dynamic-slice_add_fusion.2), channel_id=1, source_target_pairs={{0,3},{1,2},{2,1},{3,0},{4,7},{5,6},{6,5},{7,4},{8,11},{9,10},{10,... | collective-permute-start | bytes 98312 | tf_op jit(solution)/shard_map/ppermute | solution.py:30
  182.2 3.3 %collective-permute-start.23 = (f32[32,256]{1,0:T(8,128)S(1)}, f32[32,256]{1,0:T(8,128)S(1)}, u32[]{:S(2)}, u32[]{:S(2)}) collective-permute-start(f32[32,256]{1,0:T(8,128)S(1)} %add.134), channel_id=1, source_target_pairs={{0,5},{1,4},{2,7},{3,6},{4,1},{5,0},{6,3},{7,2},{8,13},{9,12},{10,... | collective-permute-start | bytes 98312 | tf_op jit(solution)/shard_map/ppermute | solution.py:30
  183.5 13.2 %collective-permute-start.17 = (bf16[416,512]{1,0:T(8,128)(2,1)S(1)}, bf16[416,512]{1,0:T(8,128)(2,1)S(1)}, u32[]{:S(2)}, u32[]{:S(2)}) collective-permute-start(bf16[416,512]{1,0:T(8,128)(2,1)S(1)} %pad_maximum_fusion.1.refs_0_), channel_id=1, source_target_pairs={{0,17},{1,16},{2,19},{3,18},{4,21},{5,20},{6,23},{7,22},{8,25},{9,... | collective-permute-start | bytes 1277960 | tf_op jit(solution)/shard_map/ppermute | solution.py:30
  185.5 4.2 %collective-permute-start.24 = (f32[32,256]{1,0:T(8,128)S(1)}, f32[32,256]{1,0:T(8,128)S(1)}, u32[]{:S(2)}, u32[]{:S(2)}) collective-permute-start(f32[32,256]{1,0:T(8,128)S(1)} %add.135), channel_id=1, source_target_pairs={{0,9},{1,8},{2,11},{3,10},{4,13},{5,12},{6,15},{7,14},{8,1},{9,0},... | collective-permute-start | bytes 98312 | tf_op jit(solution)/shard_map/ppermute | solution.py:30
  189.8 5.7 %collective-permute-start.25 = (bf16[32,256]{1,0:T(8,128)(2,1)S(1)}, bf16[32,256]{1,0:T(8,128)(2,1)S(1)}, u32[]{:S(2)}, u32[]{:S(2)}) collective-permute-start(bf16[32,256]{1,0:T(8,128)(2,1)S(1)} %divide_convert_fusion.3), channel_id=1, source_target_pairs={{0,17},{1,16},{2,19},{3,18},{4,21},{5,20},{6,23},{7,22},{8,25},{9,... | collective-permute-start | bytes 49160 | tf_op jit(solution)/shard_map/ppermute | solution.py:30
  195.5 1.2 collective-permute-start.26

commit v3 on v2

--- a/solution.py
+++ b/solution.py
@@ -172,20 +172,20 @@
     first = project(0, early[-1], store, where, index)
     first += project(1, first)
     early.append(reduce(jnp.concatenate([first, project(2, first)], 0)))
-    middle = project(3, early[-1])
-    middle_totals = list(totals(halves(middle)))
-    early.append(whiten(middle_totals[-1]))
     early = jnp.concatenate(early, 0)
     early = jnp.concatenate([early, swap(early, row_flip=0, feat_flip=1)], 1)
     early = [early] + [cross(early, flip) for flip in range(1, row_groups)]
 
+    middle = project(3, early[0])
+    middle_totals = list(totals(halves(middle)))
+    middle = whiten(middle_totals[-1])
     late = project(4, middle_totals[1])
-    late += project(5, late, early[0])
+    late += project(5, late, middle)
     late += project(6, late)
-    late = reduce(late)
+    late = jnp.concatenate([middle, reduce(late)], 0)
     late = jnp.concatenate([late] + [cross(late, flip) for flip in range(1, row_groups)], 0)
     pair = swap(late, row_flip=0, feat_flip=1)
-    return score(where, early, late, pair, store, index, rows, tail)
+    return score(where, early, late, pair, store, index, rows, rows - near)
 
 
 def plain(slab_grads, basis, eigenvalues, store_rows, slab_index, *, row_groups, feat_groups):

time: 199 us -> 199 us (level)
  waiting for transfers between devices: 111 us -> 108 us
    ppermute x27, waiting for transfers between devices: 111 us -> 108 us  [exchange(): return lax.ppermute(value, ('rows', 'feat'), pairs)]
where the time goes in v3:
time: 199 us; the launch traced here: 198 us
  waiting for transfers between devices  108 us (54%)
  starting transfers between devices  36.3 us (18%)
  matrix products  32.9 us (17%)
  local copies, waits for them, and re-layouts  13.1 us (7%)
  other arithmetic  5.02 us (3%)
  Pallas kernels  2.58 us (1%)
    ppermute x27, waiting for transfers between devices, exchange(): return lax.ppermute(value, ('rows', 'feat'), pairs)  108 us
    ppermute x27, starting transfers between devices, exchange(): return lax.ppermute(value, ('rows', 'feat'), pairs)  36.3 us
    dot_general x7, matrix products, project(): jnp.dot(after(moved[i], *needed), basis[f0:f1], preferred_element_type=jn...  25 us
    slice x7, local copies, waits for them, and re-layouts, shards(): pieces.append(ready[r0:r1, f0:f1])  11.9 us
    dot_general x1, matrix products, shards(): jnp.dot(after(block, *early), basis, preferred_element_type=jnp.float32)  7.94 us
  transfers between devices with their start and end apart: 27, of which 23 were waited for; matrix products, arithmetic and copies ran while one was open for 21% of the time, Pallas kernels for 0%

profile of v3, /device:TPU:0, one launch (start us, length us, event | category | flops | bytes accessed | tf_op | source)
XLA Modules:
  0.0 198.2 jit_solution(4775775108993624056)
XLA Ops:
  0.0 1.8 slice.36
  1.8 2.5 %slice.37 = bf16[32,12288]{1,0:T(8,128)(2,1)} slice(bf16[224,16384]{1,0:T(8,128)(2,1)} %param.5), slice={[0:32], [4096:16384]} | slice | bytes 1572864 | tf_op jit(solution)/shard_map/slice | solution.py:122
  4.3 3.7 %slice.38 = bf16[96,16384]{1,0:T(8,128)(2,1)} slice(bf16[224,16384]{1,0:T(8,128)(2,1)} %param.5), slice={[32:128], [0:16384]} | slice | bytes 6291456 | tf_op jit(solution)/shard_map/slice | solution.py:122
  8.0 3.0 %collective-permute-start.6 = (bf16[96,16384]{1,0:T(8,128)(2,1)}, bf16[96,16384]{1,0:T(8,128)(2,1)}, u32[]{:S(2)}, u32[]{:S(2)}) collective-permute-start(bf16[96,16384]{1,0:T(8,128)(2,1)} %slice.38), channel_id=1, source_target_pairs={{0,16},{1,17},{2,18},{3,19},{4,20},{5,21},{6,22},{7,23},{8,24},{9,... | collective-permute-start | bytes 9437192 | tf_op jit(solution)/shard_map/ppermute | solution.py:30
  11.0 1.6 slice.39
  12.6 0.8 slice.40
  13.4 0.8 slice.41
  14.2 0.7 slice.42
  14.9 7.9 %fusion.22 = f32[224,512]{1,0:T(8,128)S(1)} fusion(bf16[224,16384]{1,0:T(8,128)(2,1)S(1)} %copy-done, bf16[16384,512]{1,0:T(8,128)(2,1)} %param.6), kind=kOutput, calls=%fused_computation.41 | convolution fusion | flops 3758096384 | bytes 24576000 | tf_op jit(solution)/shard_map/dot_general | solution.py:170
  23.0 1.5 collective-permute-done
  24.5 1.3 collective-permute-start.1
  25.8 0.5 collective-permute-start.4
  26.3 1.5 collective-permute-start.5
  27.8 0.5 collective-permute-start.13
  28.4 3.9 %collective-permute-done.1 = f32[224,256]{1,0:T(8,128)} collective-permute-done((f32[224,256]{1,0:T(8,128)S(1)}, f32[224,256]{1,0:T(8,128)}, u32[]{:S(2)}, u32[]{:S(2)}) %collective-permute-start.1) | collective-permute-done | bytes 229408 | tf_op jit(solution)/shard_map/ppermute | solution.py:30
  32.2 1.7 add.108
  33.9 1.6 collective-permute-start.2
  35.5 0.9 constant_dynamic-slice_fusion.5
  36.4 5.0 %collective-permute-done.2 = f32[224,256]{1,0:T(8,128)} collective-permute-done((f32[224,256]{1,0:T(8,128)}, f32[224,256]{1,0:T(8,128)}, u32[]{:S(2)}, u32[]{:S(2)}) %collective-permute-start.2) | collective-permute-done | bytes 229408 | tf_op jit(solution)/shard_map/ppermute | solution.py:30
  41.5 1.1 add.109
  42.5 3.0 %collective-permute-start.3 = (f32[224,256]{1,0:T(8,128)S(1)}, f32[224,256]{1,0:T(8,128)S(1)}, u32[]{:S(2)}, u32[]{:S(2)}) collective-permute-start(f32[224,256]{1,0:T(8,128)S(1)} %add.109), channel_id=1, source_target_pairs={{0,9},{1,8},{2,11},{3,10},{4,13},{5,12},{6,15},{7,14},{8,1},{9,0},... | collective-permute-start | bytes 688136 | tf_op jit(solution)/shard_map/ppermute | solution.py:30
  45.6 1.2 pad_maximum_fusion.refs_4_
  46.8 0.8 dynamic-slice_add_fusion.3
  47.6 8.4 %collective-permute-done.3 = f32[224,256]{1,0:T(8,128)S(1)} collective-permute-done((f32[224,256]{1,0:T(8,128)S(1)}, f32[224,256]{1,0:T(8,128)S(1)}, u32[]{:S(2)}, u32[]{:S(2)}) %collective-permute-start.3) | collective-permute-done | bytes 229408 | tf_op jit(solution)/shard_map/ppermute | solution.py:30
  56.1 29.8 %collective-permute-done.4 = bf16[32,4096]{1,0:T(8,128)(2,1)} collective-permute-done((bf16[32,4096]{1,0:T(8,128)(2,1)}, bf16[32,4096]{1,0:T(8,128)(2,1)}, u32[]{:S(2)}, u32[]{:S(2)}) %collective-permute-start.4) | collective-permute-done | bytes 262176 | tf_op jit(solution)/shard_map/ppermute | solution.py:30
  85.9 3.1 %fusion.6 = f32[32,512]{1,0:T(8,128)S(1)} fusion(bf16[32,4096]{1,0:T(8,128)(2,1)} %collective-permute-done.4, bf16[16384,512]{1,0:T(8,128)(2,1)} %param.6), kind=kOutput, calls=%fused_computation.6 | convolution fusion | flops 134217728 | bytes 4521984 | tf_op jit(solution)/shard_map/dot_general | solution.py:143
  89.0 13.8 %collective-permute-done.5 = bf16[32,12288]{1,0:T(8,128)(2,1)} collective-permute-done((bf16[32,12288]{1,0:T(8,128)(2,1)}, bf16[32,12288]{1,0:T(8,128)(2,1)}, u32[]{:S(2)}, u32[]{:S(2)}) %collective-permute-start.5) | collective-permute-done | bytes 786464 | tf_op jit(solution)/shard_map/ppermute | solution.py:30
  102.8 6.2 %fusion.16 = f32[32,512]{1,0:T(8,128)S(1)} fusion(f32[32,512]{1,0:T(8,128)S(1)} %fusion.6, bf16[32,12288]{1,0:T(8,128)(2,1)} %collective-permute-done.5, bf16[16384,512]{1,0:T(8,128)(2,1)} %param.6), kind=kOutput, calls=%fused_computation.12 | convolution fusion | flops 402669568 | bytes 13500416 | tf_op jit(solution)/shard_map/dot_general | solution.py:143
  109.0 9.6 %fusion.23 = f32[96,512]{1,0:T(8,128)S(1)} fusion(bf16[96,16384]{1,0:T(8,128)(2,1)} %collective-permute-done.6, bf16[16384,512]{1,0:T(8,128)(2,1)} %param.6), kind=kOutput, calls=%fused_computation.42 | convolution fusion | flops 1610612736 | bytes 20119552 | tf_op jit(solution)/shard_map/dot_general | solution.py:143
  118.7 1.3 collective-permute-done.7
  120.1 1.9 collective-permute-start.8
  121.9 3.6 %collective-permute-done.8 = f32[128,256]{1,0:T(8,128)S(1)} collective-permute-done((f32[128,256]{1,0:T(8,128)S(1)}, f32[128,256]{1,0:T(8,128)S(1)}, u32[]{:S(2)}, u32[]{:S(2)}) %collective-permute-start.8) | collective-permute-done | bytes 131104 | tf_op jit(solution)/shard_map/ppermute | solution.py:30
  125.5 2.3 %collective-permute-start.9 = (f32[128,256]{1,0:T(8,128)S(1)}, f32[128,256]{1,0:T(8,128)S(1)}, u32[]{:S(2)}, u32[]{:S(2)}) collective-permute-start(f32[128,256]{1,0:T(8,128)S(1)} %add.124), channel_id=1, source_target_pairs={{0,5},{1,4},{2,7},{3,6},{4,1},{5,0},{6,3},{7,2},{8,13},{9,12},{10,... | collective-permute-start | bytes 393224 | tf_op jit(solution)/shard_map/ppermute | solution.py:30
  127.9 3.8 %collective-permute-done.9 = f32[128,256]{1,0:T(8,128)S(1)} collective-permute-done((f32[128,256]{1,0:T(8,128)S(1)}, f32[128,256]{1,0:T(8,128)S(1)}, u32[]{:S(2)}, u32[]{:S(2)}) %collective-permute-start.9) | collective-permute-done | bytes 131104 | tf_op jit(solution)/shard_map/ppermute | solution.py:30
  131.7 2.8 %collective-permute-start.10 = (f32[128,256]{1,0:T(8,128)S(1)}, f32[128,256]{1,0:T(8,128)S(1)}, u32[]{:S(2)}, u32[]{:S(2)}) collective-permute-start(f32[128,256]{1,0:T(8,128)S(1)} %add.125), channel_id=1, source_target_pairs={{0,9},{1,8},{2,11},{3,10},{4,13},{5,12},{6,15},{7,14},{8,1},{9,0},... | collective-permute-start | bytes 393224 | tf_op jit(solution)/shard_map/ppermute | solution.py:30
  134.4 6.3 %collective-permute-done.10 = f32[128,256]{1,0:T(8,128)S(1)} collective-permute-done((f32[128,256]{1,0:T(8,128)S(1)}, f32[128,256]{1,0:T(8,128)S(1)}, u32[]{:S(2)}, u32[]{:S(2)}) %collective-permute-start.10) | collective-permute-done | bytes 131104 | tf_op jit(solution)/shard_map/ppermute | solution.py:30
  141.2 1.5 collective-permute-start.18
  142.8 4.8 %collective-permute-done.13 = bf16[64,16384]{1,0:T(8,128)(2,1)S(1)} collective-permute-done((bf16[64,16384]{1,0:T(8,128)(2,1)}, bf16[64,16384]{1,0:T(8,128)(2,1)S(1)}, u32[]{:S(2)}, u32[]{:S(2)}) %collective-permute-start.13) | collective-permute-done | bytes 2097184 | tf_op jit(solution)/shard_map/ppermute | solution.py:30
  147.6 3.0 %fusion.24 = f32[64,512]{1,0:T(8,128)S(1)} fusion(bf16[64,16384]{1,0:T(8,128)(2,1)S(1)} %collective-permute-done.13, bf16[16384,512]{1,0:T(8,128)(2,1)S(1)} %bitcast.14), kind=kOutput, calls=%fused_computation.43 | convolution fusion | flops 1073741824 | bytes 19005440 | tf_op jit(solution)/shard_map/dot_general | solution.py:143
  150.7 1.2 collective-permute-done.14
  152.0 1.9 collective-permute-start.15
  153.9 2.1 %collective-permute-done.15 = f32[64,256]{1,0:T(8,128)S(1)} collective-permute-done((f32[64,256]{1,0:T(8,128)S(1)}, f32[64,256]{1,0:T(8,128)S(1)}, u32[]{:S(2)}, u32[]{:S(2)}) %collective-permute-start.15) | collective-permute-done | bytes 65568 | tf_op jit(solution)/shard_map/ppermute | solution.py:30
  156.0 2.3 %collective-permute-start.16 = (f32[64,256]{1,0:T(8,128)S(1)}, f32[64,256]{1,0:T(8,128)S(1)}, u32[]{:S(2)}, u32[]{:S(2)}) collective-permute-start(f32[64,256]{1,0:T(8,128)S(1)} %add.128), channel_id=1, source_target_pairs={{0,5},{1,4},{2,7},{3,6},{4,1},{5,0},{6,3},{7,2},{8,13},{9,12},{10,... | collective-permute-start | bytes 196616 | tf_op jit(solution)/shard_map/ppermute | solution.py:30
  158.3 1.5 collective-permute-start.19
  159.8 0.5 collective-permute-start.20
  160.7 2.5 %collective-permute-start.17 = (f32[64,256]{1,0:T(8,128)S(1)}, f32[64,256]{1,0:T(8,128)S(1)}, u32[]{:S(2)}, u32[]{:S(2)}) collective-permute-start(f32[64,256]{1,0:T(8,128)S(1)} %add.129), channel_id=1, source_target_pairs={{0,9},{1,8},{2,11},{3,10},{4,13},{5,12},{6,15},{7,14},{8,1},{9,0},... | collective-permute-start | bytes 196616 | tf_op jit(solution)/shard_map/ppermute | solution.py:30
  163.2 1.5 fusion.2
  164.7 1.1 collective-permute-done.17
  165.8 4.5 %collective-permute-done.19 = bf16[32,6144]{1,0:T(8,128)(2,1)S(1)} collective-permute-done((bf16[32,6144]{1,0:T(8,128)(2,1)S(1)}, bf16[32,6144]{1,0:T(8,128)(2,1)S(1)}, u32[]{:S(2)}, u32[]{:S(2)}) %collective-permute-start.19) | collective-permute-done | bytes 393248 | tf_op jit(solution)/shard_map/ppermute | solution.py:30
  170.3 1.2 fusion.13
  171.5 0.7 collective-permute-done.20
  172.2 0.5 fusion.10
  172.8 1.2 collective-permute-done.21
  174.0 1.3 collective-permute-start.22
  175.3 2.1 %collective-permute-done.22 = f32[32,256]{1,0:T(8,128)S(1)} collective-permute-done((f32[32,256]{1,0:T(8,128)S(1)}, f32[32,256]{1,0:T(8,128)S(1)}, u32[]{:S(2)}, u32[]{:S(2)}) %collective-permute-start.22) | collective-permute-done | bytes 32800 | tf_op jit(solution)/shard_map/ppermute | solution.py:30
  177.5 3.1 %collective-permute-done.23 = f32[32,256]{1,0:T(8,128)S(1)} collective-permute-done((f32[32,256]{1,0:T(8,128)S(1)}, f32[32,256]{1,0:T(8,128)S(1)}, u32[]{:S(2)}, u32[]{:S(2)}) %collective-permute-start.23) | collective-permute-done | bytes 32800 | tf_op jit(solution)/shard_map/ppermute | solution.py:30
  180.7 2.4 %collective-permute-start.24 = (f32[32,256]{1,0:T(8,128)S(1)}, f32[32,256]{1,0:T(8,128)S(1)}, u32[]{:S(2)}, u32[]{:S(2)}) collective-permute-start(f32[32,256]{1,0:T(8,128)S(1)} %add.135), channel_id=1, source_target_pairs={{0,9},{1,8},{2,11},{3,10},{4,13},{5,12},{6,15},{7,14},{8,1},{9,0},... | collective-permute-start | bytes 98312 | tf_op jit(solution)/shard_map/ppermute | solution.py:30
  183.0 1.4 collective-permute-start.12
  184.5 1.3 collective-permute-done.24
  185.8 1.3 collective-permute-start.25
  187.1 7.2 %collective-permute-done.25 = bf16[96,256]{1,0:T(8,128)(2,1)S(1)} collective-permute-done((bf16[96,256]{1,0:T(8,128)(2,1)S(1)}, bf16[96,256]{1,0:T(8,128)(2,1)S(1)}, u32[]{:S(2)}, u32[]{:S(2)}) %collective-permute-start.25) | collective-permute-done | bytes 49184 | tf_op jit(solution)/shard_map/ppermute | solution.py:30
  194.3 0.4 collective-permute-start.26
  194.9 0.8 collective-permute-done.26.refs_3_
  195.7 2.6 %score.1 = f32[448,512]{1,0:T(8,128)} custom-call(s32[1]{0:T(128)} %bitcast._, bf16[352,512]{1,0:T(8,128)(2,1)S(1)} %pad_maximum_fusion.1.refs_0_, bf16[352,512]{1,0:T(8,128)(2,1)S(1)} %collective-permute-done.12.refs_1_, bf16[192,256]{1,0:T(8,128)(2,1)S(1)} %pad_maximum_fusion.3.refs_2_, bf16[192,256]{1,0:T(8,128)(2,1)S(1)} %collective-permute-done.26.refs_3_, ...), custom_call_target="tpu_custom_call" | custom-call | tf_op jit(solution)/shard_map/score/pallas_call | solution.py:77
  (56 shorter events, 1.7 us)
Async XLA Ops:
  0.0 11.0 %copy-start = (bf16[224,16384]{1,0:T(8,128)(2,1)S(1)}, bf16[224,16384]{1,0:T(8,128)(2,1)}, u32[]{:S(2)}) copy-start(bf16[224,16384]{1,0:T(8,128)(2,1)} %param.5) | copy-start | bytes 22020100
  8.0 100.9 %collective-permute-start.6 = (bf16[96,16384]{1,0:T(8,128)(2,1)}, bf16[96,16384]{1,0:T(8,128)(2,1)}, u32[]{:S(2)}, u32[]{:S(2)}) collective-permute-start(bf16[96,16384]{1,0:T(8,128)(2,1)} %slice.38), channel_id=1, source_target_pairs={{0,16},{1,17},{2,18},{3,19},{4,20},{5,21},{6,22},{7,23},{8,24},{9,... | collective-permute-start | bytes 9437192 | tf_op jit(solution)/shard_map/ppermute | solution.py:30
  14.9 20.6 %copy-start.1 = (bf16[512,1024]{1,0:T(8,128)(2,1)S(1)}, bf16[512,1024]{1,0:T(8,128)(2,1)}, u32[]{:S(2)}) copy-start(bf16[512,1024]{1,0:T(8,128)(2,1)} %param.8) | copy-start | bytes 3145732
  14.9 21.6 %copy-start.5 = (s32[448]{0:T(512)S(1)}, s32[448]{0:T(512)}, u32[]{:S(2)}) copy-start(s32[448]{0:T(512)} %param.9) | copy-start | bytes 5380
  22.9 1.6 collective-permute-start
  24.5 7.8 %collective-permute-start.1 = (f32[224,256]{1,0:T(8,128)S(1)}, f32[224,256]{1,0:T(8,128)}, u32[]{:S(2)}, u32[]{:S(2)}) collective-permute-start(f32[224,256]{1,0:T(8,128)S(1)} %dynamic-slice_add_fusion), channel_id=1, source_target_pairs={{0,3},{1,2},{2,1},{3,0},{4,7},{5,6},{6,5},{7,4},{8,11},{9,10},{10,... | collective-permute-start | bytes 688136 | tf_op jit(solution)/shard_map/ppermute | solution.py:30
  25.8 60.1 %collective-permute-start.4 = (bf16[32,4096]{1,0:T(8,128)(2,1)}, bf16[32,4096]{1,0:T(8,128)(2,1)}, u32[]{:S(2)}, u32[]{:S(2)}) collective-permute-start(bf16[32,4096]{1,0:T(8,128)(2,1)} %slice.36), channel_id=1, source_target_pairs={{0,16},{1,17},{2,18},{3,19},{4,20},{5,21},{6,22},{7,23},{8,24},{9,... | collective-permute-start | bytes 786440 | tf_op jit(solution)/shard_map/ppermute | solution.py:30
  26.3 76.4 %collective-permute-start.5 = (bf16[32,12288]{1,0:T(8,128)(2,1)}, bf16[32,12288]{1,0:T(8,128)(2,1)}, u32[]{:S(2)}, u32[]{:S(2)}) collective-permute-start(bf16[32,12288]{1,0:T(8,128)(2,1)} %slice.37), channel_id=1, source_target_pairs={{0,16},{1,17},{2,18},{3,19},{4,20},{5,21},{6,22},{7,23},{8,24},{9,... | collective-permute-start | bytes 2359304 | tf_op jit(solution)/shard_map/ppermute | solution.py:30
  27.8 119.8 %collective-permute-start.13 = (bf16[64,16384]{1,0:T(8,128)(2,1)}, bf16[64,16384]{1,0:T(8,128)(2,1)S(1)}, u32[]{:S(2)}, u32[]{:S(2)}) collective-permute-start(bf16[64,16384]{1,0:T(8,128)(2,1)} %slice.39), channel_id=1, source_target_pairs={{0,16},{1,17},{2,18},{3,19},{4,20},{5,21},{6,22},{7,23},{8,24},{9,... | collective-permute-start | bytes 6291464 | tf_op jit(solution)/shard_map/ppermute | solution.py:30
  33.9 7.6 %collective-permute-start.2 = (f32[224,256]{1,0:T(8,128)}, f32[224,256]{1,0:T(8,128)}, u32[]{:S(2)}, u32[]{:S(2)}) collective-permute-start(f32[224,256]{1,0:T(8,128)} %add.108), channel_id=1, source_target_pairs={{0,5},{1,4},{2,7},{3,6},{4,1},{5,0},{6,3},{7,2},{8,13},{9,12},{10,... | collective-permute-start | bytes 688136 | tf_op jit(solution)/shard_map/ppermute | solution.py:30
  42.5 13.5 %collective-permute-start.3 = (f32[224,256]{1,0:T(8,128)S(1)}, f32[224,256]{1,0:T(8,128)S(1)}, u32[]{:S(2)}, u32[]{:S(2)}) collective-permute-start(f32[224,256]{1,0:T(8,128)S(1)} %add.109), channel_id=1, source_target_pairs={{0,9},{1,8},{2,11},{3,10},{4,13},{5,12},{6,15},{7,14},{8,1},{9,0},... | collective-permute-start | bytes 688136 | tf_op jit(solution)/shard_map/ppermute | solution.py:30
  102.8 44.8 %slice-start = ((s8[16777216]{0:T(1024)(128)(4,1)}), s8[4194304]{0:T(1024)(128)(4,1)S(1)}, s32[]{:S(2)}) async-start(s8[16777216]{0:T(1024)(128)(4,1)} %bitcast.13), calls=%async_computation | async-start | bytes 8388608
  102.8 44.8 %slice-start.1 = ((s8[16777216]{0:T(1024)(128)(4,1)}), s8[4194304]{0:T(1024)(128)(4,1)S(1)}, s32[]{:S(2)}) async-start(s8[16777216]{0:T(1024)(128)(4,1)} %bitcast.13), calls=%async_computation.1 | async-start | bytes 8388608
  108.9 32.3 %copy-start.2 = (bf16[32,8192]{1,0:T(8,128)(2,1)S(1)}, bf16[32,8192]{1,0:T(8,128)(2,1)}, u32[]{:S(2)}) copy-start(bf16[32,8192]{1,0:T(8,128)(2,1)} %slice.40) | copy-start | bytes 1572868
  109.0 38.6 %slice-start.2 = ((s8[16777216]{0:T(1024)(128)(4,1)}), s8[4194304]{0:T(1024)(128)(4,1)S(1)}, s32[]{:S(2)}) async-start(s8[16777216]{0:T(1024)(128)(4,1)} %bitcast.13), calls=%async_computation.2 | async-start | bytes 8388608
  109.0 38.6 %slice-start.3 = ((s8[16777216]{0:T(1024)(128)(4,1)}), s8[4194304]{0:T(1024)(128)(4,1)S(1)}, s32[]{:S(2)}) async-start(s8[16777216]{0:T(1024)(128)(4,1)} %bitcast.13), calls=%async_computation.3 | async-start | bytes 8388608
  118.6 1.4 collective-permute-start.7
  120.1 5.4 %collective-permute-start.8 = (f32[128,256]{1,0:T(8,128)S(1)}, f32[128,256]{1,0:T(8,128)S(1)}, u32[]{:S(2)}, u32[]{:S(2)}) collective-permute-start(f32[128,256]{1,0:T(8,128)S(1)} %fusion.21), channel_id=1, source_target_pairs={{0,3},{1,2},{2,1},{3,0},{4,7},{5,6},{6,5},{7,4},{8,11},{9,10},{10,... | collective-permute-start | bytes 393224 | tf_op jit(solution)/shard_map/ppermute | solution.py:30
  125.5 6.1 %collective-permute-start.9 = (f32[128,256]{1,0:T(8,128)S(1)}, f32[128,256]{1,0:T(8,128)S(1)}, u32[]{:S(2)}, u32[]{:S(2)}) collective-permute-start(f32[128,256]{1,0:T(8,128)S(1)} %add.124), channel_id=1, source_target_pairs={{0,5},{1,4},{2,7},{3,6},{4,1},{5,0},{6,3},{7,2},{8,13},{9,12},{10,... | collective-permute-start | bytes 393224 | tf_op jit(solution)/shard_map/ppermute | solution.py:30
  131.7 9.1 %collective-permute-start.10 = (f32[128,256]{1,0:T(8,128)S(1)}, f32[128,256]{1,0:T(8,128)S(1)}, u32[]{:S(2)}, u32[]{:S(2)}) collective-permute-start(f32[128,256]{1,0:T(8,128)S(1)} %add.125), channel_id=1, source_target_pairs={{0,9},{1,8},{2,11},{3,10},{4,13},{5,12},{6,15},{7,14},{8,1},{9,0},... | collective-permute-start | bytes 393224 | tf_op jit(solution)/shard_map/ppermute | solution.py:30
  140.8 1.9 collective-permute-start.11
  141.2 19.2 %collective-permute-start.18 = (bf16[32,8192]{1,0:T(8,128)(2,1)S(1)}, bf16[32,8192]{1,0:T(8,128)(2,1)S(1)}, u32[]{:S(2)}, u32[]{:S(2)}) collective-permute-start(bf16[32,8192]{1,0:T(8,128)(2,1)S(1)} %copy-done.2), channel_id=1, source_target_pairs={{0,16},{1,17},{2,18},{3,19},{4,20},{5,21},{6,22},{7,23},{8,24},{9,... | collective-permute-start | bytes 1572872 | tf_op jit(solution)/shard_map/ppermute | solution.py:30
  142.7 15.6 %copy-start.3 = (bf16[32,6144]{1,0:T(8,128)(2,1)S(1)}, bf16[32,6144]{1,0:T(8,128)(2,1)}, u32[]{:S(2)}) copy-start(bf16[32,6144]{1,0:T(8,128)(2,1)} %slice.41) | copy-start | bytes 1179652
  142.8 17.1 %copy-start.4 = (bf16[32,2048]{1,0:T(8,128)(2,1)S(1)}, bf16[32,2048]{1,0:T(8,128)(2,1)}, u32[]{:S(2)}) copy-start(bf16[32,2048]{1,0:T(8,128)(2,1)} %slice.42) | copy-start | bytes 393220
  150.6 1.3 collective-permute-start.14
  152.0 4.0 %collective-permute-start.15 = (f32[64,256]{1,0:T(8,128)S(1)}, f32[64,256]{1,0:T(8,128)S(1)}, u32[]{:S(2)}, u32[]{:S(2)}) collective-permute-start(f32[64,256]{1,0:T(8,128)S(1)} %dynamic-slice_add_fusion.1), channel_id=1, source_target_pairs={{0,3},{1,2},{2,1},{3,0},{4,7},{5,6},{6,5},{7,4},{8,11},{9,10},{10,... | collective-permute-start | bytes 196616 | tf_op jit(solution)/shard_map/ppermute | solution.py:30
  156.0 4.7 %collective-permute-start.16 = (f32[64,256]{1,0:T(8,128)S(1)}, f32[64,256]{1,0:T(8,128)S(1)}, u32[]{:S(2)}, u32[]{:S(2)}) collective-permute-start(f32[64,256]{1,0:T(8,128)S(1)} %add.128), channel_id=1, source_target_pairs={{0,5},{1,4},{2,7},{3,6},{4,1},{5,0},{6,3},{7,2},{8,13},{9,12},{10,... | collective-permute-start | bytes 196616 | tf_op jit(solution)/shard_map/ppermute | solution.py:30
  158.3 12.0 %collective-permute-start.19 = (bf16[32,6144]{1,0:T(8,128)(2,1)S(1)}, bf16[32,6144]{1,0:T(8,128)(2,1)S(1)}, u32[]{:S(2)}, u32[]{:S(2)}) collective-permute-start(bf16[32,6144]{1,0:T(8,128)(2,1)S(1)} %copy-done.3), channel_id=1, source_target_pairs={{0,16},{1,17},{2,18},{3,19},{4,20},{5,21},{6,22},{7,23},{8,24},{9,... | collective-permute-start | bytes 1179656 | tf_op jit(solution)/shard_map/ppermute | solution.py:30
  159.8 12.4 %collective-permute-start.20 = (bf16[32,2048]{1,0:T(8,128)(2,1)S(1)}, bf16[32,2048]{1,0:T(8,128)(2,1)S(1)}, u32[]{:S(2)}, u32[]{:S(2)}) collective-permute-start(bf16[32,2048]{1,0:T(8,128)(2,1)S(1)} %copy-done.4), channel_id=1, source_target_pairs={{0,16},{1,17},{2,18},{3,19},{4,20},{5,21},{6,22},{7,23},{8,24},{9,... | collective-permute-start | bytes 393224 | tf_op jit(solution)/shard_map/ppermute | solution.py:30
  160.7 5.1 %collective-permute-start.17 = (f32[64,256]{1,0:T(8,128)S(1)}, f32[64,256]{1,0:T(8,128)S(1)}, u32[]{:S(2)}, u32[]{:S(2)}) collective-permute-start(f32[64,256]{1,0:T(8,128)S(1)} %add.129), channel_id=1, source_target_pairs={{0,9},{1,8},{2,11},{3,10},{4,13},{5,12},{6,15},{7,14},{8,1},{9,0},... | collective-permute-start | bytes 196616 | tf_op jit(solution)/shard_map/ppermute | solution.py:30
  172.7 1.3 collective-permute-start.21
  174.0 3.3 %collective-permute-start.22 = (f32[32,256]{1,0:T(8,128)S(1)}, f32[32,256]{1,0:T(8,128)S(1)}, u32[]{:S(2)}, u32[]{:S(2)}) collective-permute-start(f32[32,256]{1,0:T(8,128)S(1)} %dynamic-slice_add_fusion.2), channel_id=1, source_target_pairs={{0,3},{1,2},{2,1},{3,0},{4,7},{5,6},{6,5},{7,4},{8,11},{9,10},{10,... | collective-permute-start | bytes 98312 | tf_op jit(solution)/shard_map/ppermute | solution.py:30
  177.3 3.3 %collective-permute-start.23 = (f32[32,256]{1,0:T(8,128)S(1)}, f32[32,256]{1,0:T(8,128)S(1)}, u32[]{:S(2)}, u32[]{:S(2)}) collective-permute-start(f32[32,256]{1,0:T(8,128)S(1)} %add.134), channel_id=1, source_target_pairs={{0,5},{1,4},{2,7},{3,6},{4,1},{5,0},{6,3},{7,2},{8,13},{9,12},{10,... | collective-permute-start | bytes 98312 | tf_op jit(solution)/shard_map/ppermute | solution.py:30
  180.7 5.1 %collective-permute-start.24 = (f32[32,256]{1,0:T(8,128)S(1)}, f32[32,256]{1,0:T(8,128)S(1)}, u32[]{:S(2)}, u32[]{:S(2)}) collective-permute-start(f32[32,256]{1,0:T(8,128)S(1)} %add.135), channel_id=1, source_target_pairs={{0,9},{1,8},{2,11},{3,10},{4,13},{5,12},{6,15},{7,14},{8,1},{9,0},... | collective-permute-start | bytes 98312 | tf_op jit(solution)/shard_map/ppermute | solution.py:30
  183.0 11.8 %collective-permute-start.12 = (bf16[352,512]{1,0:T(8,128)(2,1)S(1)}, bf16[352,512]{1,0:T(8,128)(2,1)S(1)}, u32[]{:S(2)}, u32[]{:S(2)}) collective-permute-start(bf16[352,512]{1,0:T(8,128)(2,1)S(1)} %pad_maximum_fusion.1.refs_0_), channel_id=1, source_target_pairs={{0,17},{1,16},{2,19},{3,18},{4,21},{5,20},{6,23},{7,22},{8,25},{9,... | collective-permute-start | bytes 1081352 | tf_op jit(solution)/shard_map/ppermute | solution.py:30
  185.8 8.5 %collective-permute-start.25 = (bf16[96,256]{1,0:T(8,128)(2,1)S(1)}, bf16[96,256]{1,0:T(8,128)(2,1)S(1)}, u32[]{:S(2)}, u32[]{:S(2)}) collective-permute-start(bf16[96,256]{1,0:T(8,128)(2,1)S(1)} %pad_maximum_fusion.4), channel_id=1, source_target_pairs={{0,17},{1,16},{2,19},{3,18},{4,21},{5,20},{6,23},{7,22},{8,25},{9,... | collective-permute-start | bytes 147464 | tf_op jit(solution)/shard_map/ppermute | solution.py:30
  194.3 1.4 collective-permute-start.26

commit v4 on v3

--- a/solution.py
+++ b/solution.py
@@ -4,7 +4,6 @@
 import jax.numpy as jnp
 from jax import lax
 from jax.experimental import pallas as pl
-from jax.experimental.pallas import tpu as pltpu
 from jax.sharding import PartitionSpec as P
 
 
@@ -34,58 +33,68 @@
     return lax.optimization_barrier((value, *needed))[0]
 
 
-def score_kernel(row_groups, rows, tail, _, *refs):
-    early = refs[:row_groups]
-    late_ref, pair_ref, store_ref, index_ref, out_ref = refs[row_groups:]
-    half = late_ref.shape[1]
-    same = index_ref[...] == lax.broadcasted_iota(jnp.int32, out_ref.shape, 1)
-
-    def dot(block, flip, part, size):
-        spot = (2 * flip + part) * half
-        return lax.dot_general(
-            block,
-            store_ref[:, spot : spot + size],
-            CONTRACT_LAST,
-            preferred_element_type=jnp.float32,
+def score(row, early, late, pair, store, same, rows, tail):
+    row_groups = len(early)
+    columns = []
+    for flip in range(row_groups):
+        spot = flip * tail
+        whole = jnp.concatenate(
+            [
+                early[flip],
+                jnp.concatenate([late[spot : spot + tail], pair[spot : spot + tail]], 1),
+            ],
+            0,
         )
-
-    for place in range(row_groups):
-
-        @pl.when(pl.program_id(0) == place)
-        def _():
-            head, foot = 0.0, 0.0
-            for flip in range(row_groups):
-                block = (place ^ flip) * rows
-                head += dot(early[flip][block : block + rows - tail, :], flip, 0, 2 * half)
-                if place ^ flip == row_groups - 1:
-                    spot = flip * tail
-                    foot += dot(late_ref[spot : spot + tail, :], flip, 0, half)
-                    foot += dot(pair_ref[spot : spot + tail, :], flip, 1, half)
-                else:
-                    foot += dot(
-                        early[flip][block + rows - tail : block + rows, :], flip, 0, 2 * half
-                    )
-            product = jnp.concatenate([head, foot], 0)
-            out_ref[...] = jnp.where(same, jnp.zeros_like(product), product)
-
-
-def score(where, early, late, pair, store, slab_index, rows, tail):
-    row_groups, count = len(early), store.shape[0]
-    whole = [
-        pl.BlockSpec(a.shape, lambda a, where: (0, 0)) for a in (*early, late, pair, store)
-    ]
+        columns.append([whole[i * rows : (i + 1) * rows] for i in range(row_groups)])
+    blocks = [
+        jnp.concatenate([columns[flip][place ^ flip] for flip in range(row_groups)], 1)
+        for place in range(row_groups)
+    ]
+    bit = 1
+    while bit < row_groups:
+        moved = (row & bit) != 0
+        blocks = [
+            jnp.where(moved, blocks[place ^ bit], blocks[place]) for place in range(row_groups)
+        ]
+        bit *= 2
+    product = lax.dot_general(
+        jnp.concatenate(blocks, 0), store, CONTRACT_LAST, preferred_element_type=jnp.float32
+    )
+    return jnp.where(same(product.shape), jnp.zeros_like(product), product)
+
+
+def dot_kernel(left_ref, right_ref, out_ref):
+    term = jnp.dot(left_ref[...], right_ref[...], preferred_element_type=jnp.float32)
+
+    @pl.when(pl.program_id(0) == 0)
+    def _():
+        out_ref[...] = term
+
+    @pl.when(pl.program_id(0) > 0)
+    def _():
+        out_ref[...] += term
+
+
+def dot(left, right):
+    depth = left.shape[1]
+    block = depth // 16 if depth % 2048 == 0 else depth
+    rows, columns = left.shape[0], right.shape[1]
     return pl.pallas_call(
-        functools.partial(score_kernel, row_groups, rows, tail),
-        out_shape=jax.ShapeDtypeStruct((rows * row_groups, count), jnp.float32),
-        grid_spec=pltpu.PrefetchScalarGridSpec(
-            num_scalar_prefetch=1,
-            grid=(row_groups,),
-            in_specs=whole + [pl.BlockSpec((rows, 1), lambda a, where: (a ^ where[0], 0))],
-            out_specs=pl.BlockSpec((rows, count), lambda a, where: (a ^ where[0], 0)),
+        dot_kernel,
+        out_shape=jax.ShapeDtypeStruct((rows, columns), jnp.float32),
+        grid=(depth // block,),
+        in_specs=[
+            pl.BlockSpec((rows, block), lambda k: (0, k)),
+            pl.BlockSpec((block, columns), lambda k: (k, 0)),
+        ],
+        out_specs=pl.BlockSpec((rows, columns), lambda k: (0, 0)),
+        cost_estimate=pl.CostEstimate(
+            flops=2 * rows * depth * columns,
+            bytes_accessed=2 * depth * (rows + columns) + 4 * rows * columns,
+            transcendentals=0,
         ),
-        compiler_params=pltpu.CompilerParams(vmem_limit_bytes=24 << 20),
-        name="score",
-    )(where, *early, late, pair, store, slab_index)
+        name="dot",
+    )(left, right)
 
 
 def shards(slab_grads, basis, eigenvalues, store_rows, slab_index, *, row_groups, feat_groups):
@@ -101,18 +110,19 @@
     def cross(value, flip):
         return swap(value, row_flip=flip, feat_flip=bin(flip).count("1") & 1)
 
-    tail = max(rows // 7 // 16 * 16, 16)
-    near = (rows - tail) * 2 // 3 // 16 * 16
-    lead = min(32, near // 2)
-    quarter = features // 4
+    ends = [rows * 43 // 100, rows * 68 // 100, rows * 90 // 100, rows]
+    ends = [end // 8 * 8 for end in ends]
+    lead = min(32, ends[0] // 16 * 8)
+    unit = features // 8
+    plan = [
+        (0, lead, (0, 2 * unit, features)),
+        (lead, ends[0], (0, features)),
+        (ends[0], ends[1], (0, features)),
+        (ends[1], ends[2], (0, 6 * unit, features)),
+        (ends[2], ends[3], (0, 4 * unit, 7 * unit, features)),
+    ]
     cuts = [
-        (0, lead, 0, quarter),
-        (0, lead, quarter, features),
-        (lead, near, 0, features),
-        (near, rows - tail, 0, features),
-        (rows - tail, rows, 0, 2 * quarter),
-        (rows - tail, rows, 2 * quarter, features - quarter // 2),
-        (rows - tail, rows, features - quarter // 2, features),
+        (r0, r1, f0, f1) for r0, r1, marks in plan for f0, f1 in zip(marks[:-1], marks[1:])
     ]
 
     last = row_groups - 1
@@ -120,7 +130,7 @@
     pieces, ready = [], slab_grads
     for i, (r0, r1, f0, f1) in enumerate(cuts):
         pieces.append(ready[r0:r1, f0:f1])
-        if i < 2:
+        if i < 3:
             ready = after(slab_grads, pieces[-1])
     moved = []
     for piece in pieces:
@@ -135,8 +145,9 @@
         for part in (side, 1 - side):
             order.append(lax.dynamic_slice_in_dim(store_rows, base + part * half, half, 1))
     store = jnp.concatenate(order, 1)
-    where = row.astype(jnp.int32).reshape(1)
-    index = slab_index[:, None] - first_column
+
+    def same(shape):
+        return slab_index[:, None] == first_column + lax.broadcasted_iota(jnp.int32, shape, 1)
 
     def project(i, *needed):
         _, _, f0, f1 = cuts[i]
@@ -166,26 +177,27 @@
     blocks = [after(slab_grads, *pieces)] + far
     early = []
     for block in blocks:
-        early.append(
-            reduce(jnp.dot(after(block, *early), basis, preferred_element_type=jnp.float32))
-        )
-    first = project(0, early[-1], store, where, index)
+        value = dot(after(block, *early), basis)
+        early.append(reduce(value))
+    first = project(0, early[-1], store)
     first += project(1, first)
     early.append(reduce(jnp.concatenate([first, project(2, first)], 0)))
+    early.append(reduce(project(3, early[-1])))
     early = jnp.concatenate(early, 0)
     early = jnp.concatenate([early, swap(early, row_flip=0, feat_flip=1)], 1)
     early = [early] + [cross(early, flip) for flip in range(1, row_groups)]
 
-    middle = project(3, early[0])
+    middle = project(4, early[0])
+    middle += project(5, middle)
     middle_totals = list(totals(halves(middle)))
     middle = whiten(middle_totals[-1])
-    late = project(4, middle_totals[1])
-    late += project(5, late, middle)
-    late += project(6, late)
+    late = project(6, middle_totals[1])
+    late += project(7, late, middle_totals[2])
+    late += project(8, late, middle)
     late = jnp.concatenate([middle, reduce(late)], 0)
     late = jnp.concatenate([late] + [cross(late, flip) for flip in range(1, row_groups)], 0)
     pair = swap(late, row_flip=0, feat_flip=1)
-    return score(where, early, late, pair, store, index, rows, rows - near)
+    return score(row, early, late, pair, store, same, rows, rows - ends[1])
 
 
 def plain(slab_grads, basis, eigenvalues, store_rows, slab_index, *, row_groups, feat_groups):

time: 199 us -> 224 us (1.13)
  starting transfers between devices: 36.3 us -> 50.5 us
  Pallas kernels: 2.58 us -> 16.6 us
  local copies, waits for them, and re-layouts: 13.1 us -> 19.1 us
  waiting for transfers between devices: 108 us -> 102 us
  matrix products: 32.9 us -> 29.9 us
    ppermute x27 -> x33, starting transfers between devices: 36.3 us -> 50.5 us  [exchange(): return lax.ppermute(value, ('rows', 'feat'), pairs)]
    pallas_call x1, Pallas kernels: 2.58 us -> 16.6 us  [dot(): pl.pallas_call(dot_kernel, out_shape=jax.ShapeDtypeStruct((rows, columns)...]
    dot_general x1, matrix products: 7.94 us -> 1.6 us  [score(): lax.dot_general(jnp.concatenate(blocks, 0), store, CONTRACT_LAST, preferr...]
    ppermute x27 -> x33, waiting for transfers between devices: 108 us -> 102 us  [exchange(): return lax.ppermute(value, ('rows', 'feat'), pairs)]
    slice x7 -> x9, local copies, waits for them, and re-layouts: 11.9 us -> 17.2 us  [shards(): pieces.append(ready[r0:r1, f0:f1])]
    dot_general x7 -> x9, matrix products: 25 us -> 28.3 us  [project(): jnp.dot(after(moved[i], *needed), basis[f0:f1], preferred_element_type=jn...]
  transfers between devices with their start and end apart: 27 -> 33, of which waited for: 23 -> 26; matrix products, arithmetic and copies ran while one was open for 21% -> 14% of each run, Pallas kernels for 0% -> 0%
where the time goes in v4:
time: 224 us; the launch traced here: 223 us
  waiting for transfers between devices  102 us (46%)
  starting transfers between devices  50.5 us (23%)
  matrix products  29.9 us (13%)
  local copies, waits for them, and re-layouts  19.1 us (9%)
  Pallas kernels  16.6 us (7%)
  other arithmetic  4.18 us (2%)
    ppermute x33, waiting for transfers between devices, exchange(): return lax.ppermute(value, ('rows', 'feat'), pairs)  102 us
    ppermute x33, starting transfers between devices, exchange(): return lax.ppermute(value, ('rows', 'feat'), pairs)  50.5 us
    dot_general x9, matrix products, project(): jnp.dot(after(moved[i], *needed), basis[f0:f1], preferred_element_type=jn...  28.3 us
    slice x9, local copies, waits for them, and re-layouts, shards(): pieces.append(ready[r0:r1, f0:f1])  17.2 us
    pallas_call x1, Pallas kernels, dot(): pl.pallas_call(dot_kernel, out_shape=jax.ShapeDtypeStruct((rows, columns)...  16.6 us
  transfers between devices with their start and end apart: 33, of which 26 were waited for; matrix products, arithmetic and copies ran while one was open for 14% of the time, Pallas kernels for 0%

profile of v4, /device:TPU:0, one launch (start us, length us, event | category | flops | bytes accessed | tf_op | source)
XLA Modules:
  0.0 222.7 jit_solution(448932470135716489)
XLA Ops:
  0.0 1.7 slice.66
  1.7 2.1 slice.67
  3.8 3.1 %slice.68 = bf16[64,16384]{1,0:T(8,128)(2,1)} slice(bf16[224,16384]{1,0:T(8,128)(2,1)} %left_ref), slice={[32:96], [0:16384]} | slice | bytes 4194304 | tf_op jit(solution)/shard_map/slice | solution.py:132
  6.8 2.8 %slice.69 = bf16[56,16384]{1,0:T(8,128)(2,1)} slice(bf16[224,16384]{1,0:T(8,128)(2,1)} %left_ref), slice={[96:152], [0:16384]} | slice | bytes 3670016 | tf_op jit(solution)/shard_map/slice | solution.py:132
  9.7 1.3 slice.70
  11.0 1.8 slice.71
  12.8 1.8 slice.72
  14.5 1.7 slice.73
  17.2 16.6 %dot.1 = f32[224,512]{1,0:T(8,128)} custom-call(bf16[224,16384]{1,0:T(8,128)(2,1)} %left_ref, bf16[16384,512]{1,0:T(8,128)(2,1)} %right_ref.1), custom_call_target="tpu_custom_call" | custom-call | flops 3758096384 | bytes 24576000 | tf_op jit(solution)/shard_map/dot/pallas_call | solution.py:82
  33.7 1.6 constant_dynamic-slice_fusion.7
  35.9 2.5 %collective-permute-start.6 = (bf16[64,16384]{1,0:T(8,128)(2,1)}, bf16[64,16384]{1,0:T(8,128)(2,1)S(1)}, u32[]{:S(2)}, u32[]{:S(2)}) collective-permute-start(bf16[64,16384]{1,0:T(8,128)(2,1)} %slice.68), channel_id=1, source_target_pairs={{0,16},{1,17},{2,18},{3,19},{4,20},{5,21},{6,22},{7,23},{8,24},{9,... | collective-permute-start | bytes 6291464 | tf_op jit(solution)/shard_map/ppermute | solution.py:29
  38.4 1.1 dynamic-slice_add_fusion
  39.4 1.7 collective-permute-start.1
  41.1 5.9 %collective-permute-done.1 = f32[224,256]{1,0:T(8,128)S(1)} collective-permute-done((f32[224,256]{1,0:T(8,128)S(1)}, f32[224,256]{1,0:T(8,128)S(1)}, u32[]{:S(2)}, u32[]{:S(2)}) %collective-permute-start.1) | collective-permute-done | bytes 229408 | tf_op jit(solution)/shard_map/ppermute | solution.py:29
  47.0 2.1 collective-permute-start.2
  49.1 5.8 %collective-permute-done.2 = f32[224,256]{1,0:T(8,128)S(1)} collective-permute-done((f32[224,256]{1,0:T(8,128)S(1)}, f32[224,256]{1,0:T(8,128)S(1)}, u32[]{:S(2)}, u32[]{:S(2)}) %collective-permute-start.2) | collective-permute-done | bytes 229408 | tf_op jit(solution)/shard_map/ppermute | solution.py:29
  55.6 2.8 %collective-permute-start.3 = (f32[224,256]{1,0:T(8,128)}, f32[224,256]{1,0:T(8,128)}, u32[]{:S(2)}, u32[]{:S(2)}) collective-permute-start(f32[224,256]{1,0:T(8,128)} %add.136), channel_id=1, source_target_pairs={{0,9},{1,8},{2,11},{3,10},{4,13},{5,12},{6,15},{7,14},{8,1},{9,0},... | collective-permute-start | bytes 688136 | tf_op jit(solution)/shard_map/ppermute | solution.py:29
  58.5 1.5 collective-permute-start.5
  60.5 1.5 collective-permute-start.11
  62.7 6.6 %collective-permute-done.3 = f32[224,256]{1,0:T(8,128)} collective-permute-done((f32[224,256]{1,0:T(8,128)}, f32[224,256]{1,0:T(8,128)}, u32[]{:S(2)}, u32[]{:S(2)}) %collective-permute-start.3) | collective-permute-done | bytes 229408 | tf_op jit(solution)/shard_map/ppermute | solution.py:29
  69.4 1.1 divide_convert_fusion
  70.4 37.2 %collective-permute-done.4 = bf16[32,4096]{1,0:T(8,128)(2,1)} collective-permute-done((bf16[32,4096]{1,0:T(8,128)(2,1)}, bf16[32,4096]{1,0:T(8,128)(2,1)}, u32[]{:S(2)}, u32[]{:S(2)}) %collective-permute-start.4) | collective-permute-done | bytes 262176 | tf_op jit(solution)/shard_map/ppermute | solution.py:29
  107.6 3.1 %fusion.10 = f32[32,512]{1,0:T(8,128)S(1)} fusion(bf16[32,4096]{1,0:T(8,128)(2,1)} %collective-permute-done.4, bf16[16384,512]{1,0:T(8,128)(2,1)} %right_ref.1), kind=kOutput, calls=%fused_computation.10 | convolution fusion | flops 134217728 | bytes 4521984 | tf_op jit(solution)/shard_map/dot_general | solution.py:154
  110.7 6.2 %fusion.17 = f32[32,512]{1,0:T(8,128)S(1)} fusion(f32[32,512]{1,0:T(8,128)S(1)} %fusion.10, bf16[32,12288]{1,0:T(8,128)(2,1)} %collective-permute-done.5, bf16[16384,512]{1,0:T(8,128)(2,1)} %right_ref.1), kind=kOutput, calls=%fused_computation.16 | convolution fusion | flops 402669568 | bytes 13500416 | tf_op jit(solution)/shard_map/dot_general | solution.py:154
  117.0 8.9 %fusion.37 = f32[64,512]{1,0:T(8,128)S(1)} fusion(bf16[64,16384]{1,0:T(8,128)(2,1)S(1)} %collective-permute-done.6, bf16[16384,512]{1,0:T(8,128)(2,1)} %right_ref.1), kind=kOutput, calls=%fused_computation.67 | convolution fusion | flops 1073741824 | bytes 19005440 | tf_op jit(solution)/shard_map/dot_general | solution.py:154
  126.0 1.3 collective-permute-done.7
  127.3 1.9 collective-permute-start.8
  129.2 2.9 %collective-permute-done.8 = f32[96,256]{1,0:T(8,128)S(1)} collective-permute-done((f32[96,256]{1,0:T(8,128)S(1)}, f32[96,256]{1,0:T(8,128)S(1)}, u32[]{:S(2)}, u32[]{:S(2)}) %collective-permute-start.8) | collective-permute-done | bytes 98336 | tf_op jit(solution)/shard_map/ppermute | solution.py:29
  132.1 2.4 %collective-permute-start.9 = (f32[96,256]{1,0:T(8,128)S(1)}, f32[96,256]{1,0:T(8,128)S(1)}, u32[]{:S(2)}, u32[]{:S(2)}) collective-permute-start(f32[96,256]{1,0:T(8,128)S(1)} %add.150), channel_id=1, source_target_pairs={{0,5},{1,4},{2,7},{3,6},{4,1},{5,0},{6,3},{7,2},{8,13},{9,12},{10,... | collective-permute-start | bytes 294920 | tf_op jit(solution)/shard_map/ppermute | solution.py:29
  134.5 3.1 %collective-permute-done.9 = f32[96,256]{1,0:T(8,128)S(1)} collective-permute-done((f32[96,256]{1,0:T(8,128)S(1)}, f32[96,256]{1,0:T(8,128)S(1)}, u32[]{:S(2)}, u32[]{:S(2)}) %collective-permute-start.9) | collective-permute-done | bytes 98336 | tf_op jit(solution)/shard_map/ppermute | solution.py:29
  137.6 2.7 %collective-permute-start.10 = (f32[96,256]{1,0:T(8,128)S(1)}, f32[96,256]{1,0:T(8,128)S(1)}, u32[]{:S(2)}, u32[]{:S(2)}) collective-permute-start(f32[96,256]{1,0:T(8,128)S(1)} %add.151), channel_id=1, source_target_pairs={{0,9},{1,8},{2,11},{3,10},{4,13},{5,12},{6,15},{7,14},{8,1},{9,0},... | collective-permute-start | bytes 294920 | tf_op jit(solution)/shard_map/ppermute | solution.py:29
  140.3 1.5 collective-permute-start.17
  141.8 3.3 %collective-permute-done.10 = f32[96,256]{1,0:T(8,128)S(1)} collective-permute-done((f32[96,256]{1,0:T(8,128)S(1)}, f32[96,256]{1,0:T(8,128)S(1)}, u32[]{:S(2)}, u32[]{:S(2)}) %collective-permute-start.10) | collective-permute-done | bytes 98336 | tf_op jit(solution)/shard_map/ppermute | solution.py:29
  145.2 1.7 collective-permute-done.11
  147.0 4.3 %fusion.38 = f32[56,512]{1,0:T(8,128)S(1)} fusion(bf16[56,16384]{1,0:T(8,128)(2,1)} %collective-permute-done.11, bf16[16384,512]{1,0:T(8,128)(2,1)S(1)} %bitcast.12), kind=kOutput, calls=%fused_computation.68 | convolution fusion | flops 939524096 | bytes 18726912 | tf_op jit(solution)/shard_map/dot_general | solution.py:154
  151.4 1.2 collective-permute-done.12
  152.6 1.9 collective-permute-start.13
  154.5 2.0 collective-permute-done.13
  156.5 2.3 %collective-permute-start.14 = (f32[56,256]{1,0:T(8,128)S(1)}, f32[56,256]{1,0:T(8,128)S(1)}, u32[]{:S(2)}, u32[]{:S(2)}) collective-permute-start(f32[56,256]{1,0:T(8,128)S(1)} %add.154), channel_id=1, source_target_pairs={{0,5},{1,4},{2,7},{3,6},{4,1},{5,0},{6,3},{7,2},{8,13},{9,12},{10,... | collective-permute-start | bytes 172040 | tf_op jit(solution)/shard_map/ppermute | solution.py:29
  158.8 2.2 collective-permute-done.14
  161.0 2.8 %collective-permute-start.15 = (f32[56,256]{1,0:T(8,128)S(1)}, f32[56,256]{1,0:T(8,128)S(1)}, u32[]{:S(2)}, u32[]{:S(2)}) collective-permute-start(f32[56,256]{1,0:T(8,128)S(1)} %add.155), channel_id=1, source_target_pairs={{0,9},{1,8},{2,11},{3,10},{4,13},{5,12},{6,15},{7,14},{8,1},{9,0},... | collective-permute-start | bytes 172040 | tf_op jit(solution)/shard_map/ppermute | solution.py:29
  163.8 2.0 collective-permute-done.15
  165.8 1.6 collective-permute-start.16
  167.4 1.5 collective-permute-start.18
  169.5 2.6 %collective-permute-done.17 = bf16[48,12288]{1,0:T(8,128)(2,1)S(1)} collective-permute-done((bf16[48,12288]{1,0:T(8,128)(2,1)S(1)}, bf16[48,12288]{1,0:T(8,128)(2,1)S(1)}, u32[]{:S(2)}, u32[]{:S(2)}) %collective-permute-start.17) | collective-permute-done | bytes 1179680 | tf_op jit(solution)/shard_map/ppermute | solution.py:29
  172.1 2.5 %fusion = f32[48,512]{1,0:T(8,128)S(1)} fusion(bf16[48,12288]{1,0:T(8,128)(2,1)S(1)} %collective-permute-done.17, bf16[16384,512]{1,0:T(8,128)(2,1)S(1)} %bitcast.12), kind=kOutput, calls=%fused_computation | convolution fusion | flops 603979776 | bytes 13860864 | tf_op jit(solution)/shard_map/dot_general | solution.py:154
  174.6 6.0 %collective-permute-done.18 = bf16[48,4096]{1,0:T(8,128)(2,1)S(1)} collective-permute-done((bf16[48,4096]{1,0:T(8,128)(2,1)S(1)}, bf16[48,4096]{1,0:T(8,128)(2,1)S(1)}, u32[]{:S(2)}, u32[]{:S(2)}) %collective-permute-start.18) | collective-permute-done | bytes 393248 | tf_op jit(solution)/shard_map/ppermute | solution.py:29
  181.5 1.2 collective-permute-done.19
  182.7 1.9 collective-permute-start.20
  184.6 1.5 collective-permute-start.24
  186.6 2.1 collective-permute-start.21
  189.0 1.2 fusion.4
  190.8 2.9 %collective-permute-start.22 = (f32[48,256]{1,0:T(8,128)S(1)}, f32[48,256]{1,0:T(8,128)S(1)}, u32[]{:S(2)}, u32[]{:S(2)}) collective-permute-start(f32[48,256]{1,0:T(8,128)S(1)} %add.160), channel_id=1, source_target_pairs={{0,9},{1,8},{2,11},{3,10},{4,13},{5,12},{6,15},{7,14},{8,1},{9,0},... | collective-permute-start | bytes 147464 | tf_op jit(solution)/shard_map/ppermute | solution.py:29
  193.6 1.7 collective-permute-done.24
  197.7 1.2 collective-permute-done.26
  198.9 1.5 collective-permute-start.27
  200.4 1.7 collective-permute-done.27
  202.1 1.6 collective-permute-start.28
  203.7 1.7 collective-permute-done.28
  205.4 2.6 %collective-permute-start.29 = (f32[24,256]{1,0:T(8,128)S(1)}, f32[24,256]{1,0:T(8,128)S(1)}, u32[]{:S(2)}, u32[]{:S(2)}) collective-permute-start(f32[24,256]{1,0:T(8,128)S(1)} %add.166), channel_id=1, source_target_pairs={{0,9},{1,8},{2,11},{3,10},{4,13},{5,12},{6,15},{7,14},{8,1},{9,0},... | collective-permute-start | bytes 73736 | tf_op jit(solution)/shard_map/ppermute | solution.py:29
  208.0 1.4 collective-permute-start.32
  209.6 1.6 collective-permute-start.30
  211.3 8.2 %collective-permute-done.30 = bf16[72,256]{1,0:T(8,128)(2,1)S(1)} collective-permute-done((bf16[72,256]{1,0:T(8,128)(2,1)S(1)}, bf16[72,256]{1,0:T(8,128)(2,1)S(1)}, u32[]{:S(2)}, u32[]{:S(2)}) %collective-permute-start.30) | collective-permute-done | bytes 36896 | tf_op jit(solution)/shard_map/ppermute | solution.py:29
  221.1 1.6 convolution_select_fusion
  (78 shorter events, 10.8 us)
Async XLA Ops:
  35.4 3.0 %collective-permute-start = (f32[224,256]{1,0:T(8,128)}, f32[224,256]{1,0:T(8,128)}, u32[]{:S(2)}, u32[]{:S(2)}) collective-permute-start(f32[224,256]{1,0:T(8,128)} %constant_dynamic-slice_fusion.7), channel_id=1, source_target_pairs={{0,1},{1,0},{2,3},{3,2},{4,5},{5,4},{6,7},{7,6},{8,9},{9,8},{10,11... | collective-permute-start | bytes 688136 | tf_op jit(solution)/shard_map/ppermute | solution.py:29
  35.9 81.1 %collective-permute-start.6 = (bf16[64,16384]{1,0:T(8,128)(2,1)}, bf16[64,16384]{1,0:T(8,128)(2,1)S(1)}, u32[]{:S(2)}, u32[]{:S(2)}) collective-permute-start(bf16[64,16384]{1,0:T(8,128)(2,1)} %slice.68), channel_id=1, source_target_pairs={{0,16},{1,17},{2,18},{3,19},{4,20},{5,21},{6,22},{7,23},{8,24},{9,... | collective-permute-start | bytes 6291464 | tf_op jit(solution)/shard_map/ppermute | solution.py:29
  39.4 7.6 %collective-permute-start.1 = (f32[224,256]{1,0:T(8,128)S(1)}, f32[224,256]{1,0:T(8,128)S(1)}, u32[]{:S(2)}, u32[]{:S(2)}) collective-permute-start(f32[224,256]{1,0:T(8,128)S(1)} %dynamic-slice_add_fusion), channel_id=1, source_target_pairs={{0,3},{1,2},{2,1},{3,0},{4,7},{5,6},{6,5},{7,4},{8,11},{9,10},{10,... | collective-permute-start | bytes 688136 | tf_op jit(solution)/shard_map/ppermute | solution.py:29
  47.0 7.9 %collective-permute-start.2 = (f32[224,256]{1,0:T(8,128)S(1)}, f32[224,256]{1,0:T(8,128)S(1)}, u32[]{:S(2)}, u32[]{:S(2)}) collective-permute-start(f32[224,256]{1,0:T(8,128)S(1)} %add.135), channel_id=1, source_target_pairs={{0,5},{1,4},{2,7},{3,6},{4,1},{5,0},{6,3},{7,2},{8,13},{9,12},{10,... | collective-permute-start | bytes 688136 | tf_op jit(solution)/shard_map/ppermute | solution.py:29
  55.6 13.7 %collective-permute-start.3 = (f32[224,256]{1,0:T(8,128)}, f32[224,256]{1,0:T(8,128)}, u32[]{:S(2)}, u32[]{:S(2)}) collective-permute-start(f32[224,256]{1,0:T(8,128)} %add.136), channel_id=1, source_target_pairs={{0,9},{1,8},{2,11},{3,10},{4,13},{5,12},{6,15},{7,14},{8,1},{9,0},... | collective-permute-start | bytes 688136 | tf_op jit(solution)/shard_map/ppermute | solution.py:29
  58.5 52.2 %collective-permute-start.5 = (bf16[32,12288]{1,0:T(8,128)(2,1)}, bf16[32,12288]{1,0:T(8,128)(2,1)}, u32[]{:S(2)}, u32[]{:S(2)}) collective-permute-start(bf16[32,12288]{1,0:T(8,128)(2,1)} %slice.67), channel_id=1, source_target_pairs={{0,16},{1,17},{2,18},{3,19},{4,20},{5,21},{6,22},{7,23},{8,24},{9,... | collective-permute-start | bytes 2359304 | tf_op jit(solution)/shard_map/ppermute | solution.py:29
  60.0 47.7 %collective-permute-start.4 = (bf16[32,4096]{1,0:T(8,128)(2,1)}, bf16[32,4096]{1,0:T(8,128)(2,1)}, u32[]{:S(2)}, u32[]{:S(2)}) collective-permute-start(bf16[32,4096]{1,0:T(8,128)(2,1)} %slice.66), channel_id=1, source_target_pairs={{0,16},{1,17},{2,18},{3,19},{4,20},{5,21},{6,22},{7,23},{8,24},{9,... | collective-permute-start | bytes 786440 | tf_op jit(solution)/shard_map/ppermute | solution.py:29
  60.5 86.4 %collective-permute-start.11 = (bf16[56,16384]{1,0:T(8,128)(2,1)}, bf16[56,16384]{1,0:T(8,128)(2,1)}, u32[]{:S(2)}, u32[]{:S(2)}) collective-permute-start(bf16[56,16384]{1,0:T(8,128)(2,1)} %slice.69), channel_id=1, source_target_pairs={{0,16},{1,17},{2,18},{3,19},{4,20},{5,21},{6,22},{7,23},{8,24},{9,... | collective-permute-start | bytes 5505032 | tf_op jit(solution)/shard_map/ppermute | solution.py:29
  110.7 36.2 %slice-start = ((s8[16777216]{0:T(1024)(128)(4,1)}), s8[4194304]{0:T(1024)(128)(4,1)S(1)}, s32[]{:S(2)}) async-start(s8[16777216]{0:T(1024)(128)(4,1)} %bitcast.11), calls=%async_computation | async-start | bytes 8388608
  110.7 36.2 %slice-start.1 = ((s8[16777216]{0:T(1024)(128)(4,1)}), s8[4194304]{0:T(1024)(128)(4,1)S(1)}, s32[]{:S(2)}) async-start(s8[16777216]{0:T(1024)(128)(4,1)} %bitcast.11), calls=%async_computation.1 | async-start | bytes 8388608
  116.9 30.0 %slice-start.2 = ((s8[16777216]{0:T(1024)(128)(4,1)}), s8[4194304]{0:T(1024)(128)(4,1)S(1)}, s32[]{:S(2)}) async-start(s8[16777216]{0:T(1024)(128)(4,1)} %bitcast.11), calls=%async_computation.2 | async-start | bytes 8388608
  117.0 30.0 %slice-start.3 = ((s8[16777216]{0:T(1024)(128)(4,1)}), s8[4194304]{0:T(1024)(128)(4,1)S(1)}, s32[]{:S(2)}) async-start(s8[16777216]{0:T(1024)(128)(4,1)} %bitcast.11), calls=%async_computation.3 | async-start | bytes 8388608
  125.9 1.4 collective-permute-start.7
  127.3 4.7 %collective-permute-start.8 = (f32[96,256]{1,0:T(8,128)S(1)}, f32[96,256]{1,0:T(8,128)S(1)}, u32[]{:S(2)}, u32[]{:S(2)}) collective-permute-start(f32[96,256]{1,0:T(8,128)S(1)} %fusion.34), channel_id=1, source_target_pairs={{0,3},{1,2},{2,1},{3,0},{4,7},{5,6},{6,5},{7,4},{8,11},{9,10},{10,... | collective-permute-start | bytes 294920 | tf_op jit(solution)/shard_map/ppermute | solution.py:29
  132.1 5.5 %collective-permute-start.9 = (f32[96,256]{1,0:T(8,128)S(1)}, f32[96,256]{1,0:T(8,128)S(1)}, u32[]{:S(2)}, u32[]{:S(2)}) collective-permute-start(f32[96,256]{1,0:T(8,128)S(1)} %add.150), channel_id=1, source_target_pairs={{0,5},{1,4},{2,7},{3,6},{4,1},{5,0},{6,3},{7,2},{8,13},{9,12},{10,... | collective-permute-start | bytes 294920 | tf_op jit(solution)/shard_map/ppermute | solution.py:29
  137.6 7.6 %collective-permute-start.10 = (f32[96,256]{1,0:T(8,128)S(1)}, f32[96,256]{1,0:T(8,128)S(1)}, u32[]{:S(2)}, u32[]{:S(2)}) collective-permute-start(f32[96,256]{1,0:T(8,128)S(1)} %add.151), channel_id=1, source_target_pairs={{0,9},{1,8},{2,11},{3,10},{4,13},{5,12},{6,15},{7,14},{8,1},{9,0},... | collective-permute-start | bytes 294920 | tf_op jit(solution)/shard_map/ppermute | solution.py:29
  140.3 31.8 %collective-permute-start.17 = (bf16[48,12288]{1,0:T(8,128)(2,1)S(1)}, bf16[48,12288]{1,0:T(8,128)(2,1)S(1)}, u32[]{:S(2)}, u32[]{:S(2)}) collective-permute-start(bf16[48,12288]{1,0:T(8,128)(2,1)S(1)} %slice.70), channel_id=1, source_target_pairs={{0,16},{1,17},{2,18},{3,19},{4,20},{5,21},{6,22},{7,23},{8,24},{9,... | collective-permute-start | bytes 3538952 | tf_op jit(solution)/shard_map/ppermute | solution.py:29
  145.2 22.3 %copy-start.2 = (bf16[48,4096]{1,0:T(8,128)(2,1)S(1)}, bf16[48,4096]{1,0:T(8,128)(2,1)}, u32[]{:S(2)}) copy-start(bf16[48,4096]{1,0:T(8,128)(2,1)} %slice.71) | copy-start | bytes 1179652
  145.2 23.7 %copy-start.1 = (bf16[24,8192]{1,0:T(8,128)(2,1)S(1)}, bf16[24,8192]{1,0:T(8,128)(2,1)}, u32[]{:S(2)}) copy-start(bf16[24,8192]{1,0:T(8,128)(2,1)} %slice.72) | copy-start | bytes 1179652
  151.3 1.3 collective-permute-start.12
  152.6 3.9 %collective-permute-start.13 = (f32[56,256]{1,0:T(8,128)S(1)}, f32[56,256]{1,0:T(8,128)S(1)}, u32[]{:S(2)}, u32[]{:S(2)}) collective-permute-start(f32[56,256]{1,0:T(8,128)S(1)} %dynamic-slice_add_fusion.1), channel_id=1, source_target_pairs={{0,3},{1,2},{2,1},{3,0},{4,7},{5,6},{6,5},{7,4},{8,11},{9,10},{10,... | collective-permute-start | bytes 172040 | tf_op jit(solution)/shard_map/ppermute | solution.py:29
  156.5 4.5 %collective-permute-start.14 = (f32[56,256]{1,0:T(8,128)S(1)}, f32[56,256]{1,0:T(8,128)S(1)}, u32[]{:S(2)}, u32[]{:S(2)}) collective-permute-start(f32[56,256]{1,0:T(8,128)S(1)} %add.154), channel_id=1, source_target_pairs={{0,5},{1,4},{2,7},{3,6},{4,1},{5,0},{6,3},{7,2},{8,13},{9,12},{10,... | collective-permute-start | bytes 172040 | tf_op jit(solution)/shard_map/ppermute | solution.py:29
  161.0 4.8 %collective-permute-start.15 = (f32[56,256]{1,0:T(8,128)S(1)}, f32[56,256]{1,0:T(8,128)S(1)}, u32[]{:S(2)}, u32[]{:S(2)}) collective-permute-start(f32[56,256]{1,0:T(8,128)S(1)} %add.155), channel_id=1, source_target_pairs={{0,9},{1,8},{2,11},{3,10},{4,13},{5,12},{6,15},{7,14},{8,1},{9,0},... | collective-permute-start | bytes 172040 | tf_op jit(solution)/shard_map/ppermute | solution.py:29
  165.8 3.6 %collective-permute-start.16 = (bf16[376,256]{1,0:T(8,128)(2,1)S(1)}, bf16[376,256]{1,0:T(8,128)(2,1)S(1)}, u32[]{:S(2)}, u32[]{:S(2)}) collective-permute-start(bf16[376,256]{1,0:T(8,128)(2,1)S(1)} %pad_maximum_fusion.9), channel_id=1, source_target_pairs={{0,1},{1,0},{2,3},{3,2},{4,5},{5,4},{6,7},{7,6},{8,9},{9,8},{10,11... | collective-permute-start | bytes 577544 | tf_op jit(solution)/shard_map/ppermute | solution.py:29
  167.4 13.1 %collective-permute-start.18 = (bf16[48,4096]{1,0:T(8,128)(2,1)S(1)}, bf16[48,4096]{1,0:T(8,128)(2,1)S(1)}, u32[]{:S(2)}, u32[]{:S(2)}) collective-permute-start(bf16[48,4096]{1,0:T(8,128)(2,1)S(1)} %copy-done.2), channel_id=1, source_target_pairs={{0,16},{1,17},{2,18},{3,19},{4,20},{5,21},{6,22},{7,23},{8,24},{9,... | collective-permute-start | bytes 1179656 | tf_op jit(solution)/shard_map/ppermute | solution.py:29
  168.9 20.0 %collective-permute-start.23 = (bf16[24,8192]{1,0:T(8,128)(2,1)S(1)}, bf16[24,8192]{1,0:T(8,128)(2,1)S(1)}, u32[]{:S(2)}, u32[]{:S(2)}) collective-permute-start(bf16[24,8192]{1,0:T(8,128)(2,1)S(1)} %copy-done.1), channel_id=1, source_target_pairs={{0,16},{1,17},{2,18},{3,19},{4,20},{5,21},{6,22},{7,23},{8,24},{9,... | collective-permute-start | bytes 1179656 | tf_op jit(solution)/shard_map/ppermute | solution.py:29
  174.6 10.0 %copy-start.3 = (bf16[24,6144]{1,0:T(8,128)(2,1)S(1)}, bf16[24,6144]{1,0:T(8,128)(2,1)}, u32[]{:S(2)}) copy-start(bf16[24,6144]{1,0:T(8,128)(2,1)} %slice.73) | copy-start | bytes 884740
  181.4 1.3 collective-permute-start.19
  182.7 3.9 %collective-permute-start.20 = (f32[48,256]{1,0:T(8,128)S(1)}, f32[48,256]{1,0:T(8,128)S(1)}, u32[]{:S(2)}, u32[]{:S(2)}) collective-permute-start(f32[48,256]{1,0:T(8,128)S(1)} %dynamic-slice_add_fusion.2), channel_id=1, source_target_pairs={{0,3},{1,2},{2,1},{3,0},{4,7},{5,6},{6,5},{7,4},{8,11},{9,10},{10,... | collective-permute-start | bytes 147464 | tf_op jit(solution)/shard_map/ppermute | solution.py:29
  184.6 10.7 %collective-permute-start.24 = (bf16[24,6144]{1,0:T(8,128)(2,1)S(1)}, bf16[24,6144]{1,0:T(8,128)(2,1)S(1)}, u32[]{:S(2)}, u32[]{:S(2)}) collective-permute-start(bf16[24,6144]{1,0:T(8,128)(2,1)S(1)} %copy-done.3), channel_id=1, source_target_pairs={{0,16},{1,17},{2,18},{3,19},{4,20},{5,21},{6,22},{7,23},{8,24},{9,... | collective-permute-start | bytes 884744 | tf_op jit(solution)/shard_map/ppermute | solution.py:29
  186.1 11.1 %collective-permute-start.25 = (bf16[24,2048]{1,0:T(8,128)(2,1)S(1)}, bf16[24,2048]{1,0:T(8,128)(2,1)S(1)}, u32[]{:S(2)}, u32[]{:S(2)}) collective-permute-start(bf16[24,2048]{1,0:T(8,128)(2,1)S(1)} %slice.74), channel_id=1, source_target_pairs={{0,16},{1,17},{2,18},{3,19},{4,20},{5,21},{6,22},{7,23},{8,24},{9,... | collective-permute-start | bytes 294920 | tf_op jit(solution)/shard_map/ppermute | solution.py:29
  186.6 4.1 %collective-permute-start.21 = (f32[48,256]{1,0:T(8,128)S(1)}, f32[48,256]{1,0:T(8,128)S(1)}, u32[]{:S(2)}, u32[]{:S(2)}) collective-permute-start(f32[48,256]{1,0:T(8,128)S(1)} %add.159), channel_id=1, source_target_pairs={{0,5},{1,4},{2,7},{3,6},{4,1},{5,0},{6,3},{7,2},{8,13},{9,12},{10,... | collective-permute-start | bytes 147464 | tf_op jit(solution)/shard_map/ppermute | solution.py:29
  190.7 20.4 %copy-start = (bf16[512,1024]{1,0:T(8,128)(2,1)S(1)}, bf16[512,1024]{1,0:T(8,128)(2,1)}, u32[]{:S(2)}) copy-start(bf16[512,1024]{1,0:T(8,128)(2,1)} %param.8) | copy-start | bytes 3145732
  190.8 5.5 %collective-permute-start.22 = (f32[48,256]{1,0:T(8,128)S(1)}, f32[48,256]{1,0:T(8,128)S(1)}, u32[]{:S(2)}, u32[]{:S(2)}) collective-permute-start(f32[48,256]{1,0:T(8,128)S(1)} %add.160), channel_id=1, source_target_pairs={{0,9},{1,8},{2,11},{3,10},{4,13},{5,12},{6,15},{7,14},{8,1},{9,0},... | collective-permute-start | bytes 147464 | tf_op jit(solution)/shard_map/ppermute | solution.py:29
  197.6 23.5 %copy-start.4 = (s32[448]{0:T(512)S(1)}, s32[448]{0:T(512)}, u32[]{:S(2)}) copy-start(s32[448]{0:T(512)} %param.9) | copy-start | bytes 5380
  197.6 1.3 collective-permute-start.26
  198.9 3.3 %collective-permute-start.27 = (f32[24,256]{1,0:T(8,128)S(1)}, f32[24,256]{1,0:T(8,128)S(1)}, u32[]{:S(2)}, u32[]{:S(2)}) collective-permute-start(f32[24,256]{1,0:T(8,128)S(1)} %dynamic-slice_add_fusion.3), channel_id=1, source_target_pairs={{0,3},{1,2},{2,1},{3,0},{4,7},{5,6},{6,5},{7,4},{8,11},{9,10},{10,... | collective-permute-start | bytes 73736 | tf_op jit(solution)/shard_map/ppermute | solution.py:29
  202.1 3.3 %collective-permute-start.28 = (f32[24,256]{1,0:T(8,128)S(1)}, f32[24,256]{1,0:T(8,128)S(1)}, u32[]{:S(2)}, u32[]{:S(2)}) collective-permute-start(f32[24,256]{1,0:T(8,128)S(1)} %add.165), channel_id=1, source_target_pairs={{0,5},{1,4},{2,7},{3,6},{4,1},{5,0},{6,3},{7,2},{8,13},{9,12},{10,... | collective-permute-start | bytes 73736 | tf_op jit(solution)/shard_map/ppermute | solution.py:29
  205.4 4.2 %collective-permute-start.29 = (f32[24,256]{1,0:T(8,128)S(1)}, f32[24,256]{1,0:T(8,128)S(1)}, u32[]{:S(2)}, u32[]{:S(2)}) collective-permute-start(f32[24,256]{1,0:T(8,128)S(1)} %add.166), channel_id=1, source_target_pairs={{0,9},{1,8},{2,11},{3,10},{4,13},{5,12},{6,15},{7,14},{8,1},{9,0},... | collective-permute-start | bytes 73736 | tf_op jit(solution)/shard_map/ppermute | solution.py:29
  208.0 11.9 %collective-permute-start.32 = (bf16[376,512]{1,0:T(8,128)(2,1)S(1)}, bf16[376,512]{1,0:T(8,128)(2,1)S(1)}, u32[]{:S(2)}, u32[]{:S(2)}) collective-permute-start(bf16[376,512]{1,0:T(8,128)(2,1)S(1)} %pad_maximum_fusion.8), channel_id=1, source_target_pairs={{0,17},{1,16},{2,19},{3,18},{4,21},{5,20},{6,23},{7,22},{8,25},{9,... | collective-permute-start | bytes 1155080 | tf_op jit(solution)/shard_map/ppermute | solution.py:29
  209.6 9.9 %collective-permute-start.30 = (bf16[72,256]{1,0:T(8,128)(2,1)S(1)}, bf16[72,256]{1,0:T(8,128)(2,1)S(1)}, u32[]{:S(2)}, u32[]{:S(2)}) collective-permute-start(bf16[72,256]{1,0:T(8,128)(2,1)S(1)} %pad_maximum_fusion.11), channel_id=1, source_target_pairs={{0,17},{1,16},{2,19},{3,18},{4,21},{5,20},{6,23},{7,22},{8,25},{9,... | collective-permute-start | bytes 110600 | tf_op jit(solution)/shard_map/ppermute | solution.py:29
  219.5 1.3 collective-permute-start.31

commit v5 on v4

--- a/solution.py
+++ b/solution.py
@@ -4,6 +4,7 @@
 import jax.numpy as jnp
 from jax import lax
 from jax.experimental import pallas as pl
+from jax.experimental.pallas import tpu as pltpu
 from jax.sharding import PartitionSpec as P
 
 
@@ -73,6 +74,25 @@
     @pl.when(pl.program_id(0) > 0)
     def _():
         out_ref[...] += term
+
+
+def head_kernel(rows, columns, whole_ref, out_ref, arrived):
+    copy = pltpu.make_async_copy(
+        whole_ref.at[pl.ds(0, rows), pl.ds(0, columns)], out_ref, arrived
+    )
+    copy.start()
+    copy.wait()
+
+
+def head(whole, rows, columns):
+    return pl.pallas_call(
+        functools.partial(head_kernel, rows, columns),
+        out_shape=pltpu.VMEM((rows, columns), whole.dtype),
+        in_specs=[pl.BlockSpec(memory_space=pl.ANY)],
+        out_specs=pl.BlockSpec(memory_space=pltpu.VMEM),
+        scratch_shapes=[pltpu.SemaphoreType.DMA],
+        name="head",
+    )(whole)
 
 
 def dot(left, right):
@@ -129,7 +149,7 @@
     far = [swap(slab_grads, row_flip=flip, feat_flip=0) for flip in range(1, last)]
     pieces, ready = [], slab_grads
     for i, (r0, r1, f0, f1) in enumerate(cuts):
-        pieces.append(ready[r0:r1, f0:f1])
+        pieces.append(head(ready, r1, f1) if i == 0 else ready[r0:r1, f0:f1])
         if i < 3:
             ready = after(slab_grads, pieces[-1])
     moved = []
@@ -174,7 +194,7 @@
     def reduce(partial_value):
         return whiten(list(totals(halves(partial_value)))[-1])
 
-    blocks = [after(slab_grads, *pieces)] + far
+    blocks = [after(slab_grads, moved[0], *pieces)] + far
     early = []
     for block in blocks:
         value = dot(after(block, *early), basis)

time: 224 us -> 219 us (0.978)
  starting transfers between devices: 50.5 us -> 42 us
  waiting for transfers between devices: 102 us -> 107 us
    ppermute x33, starting transfers between devices: 50.5 us -> 42 us  [exchange(): return lax.ppermute(value, ('rows', 'feat'), pairs)]
    ppermute x33, waiting for transfers between devices: 102 us -> 107 us  [exchange(): return lax.ppermute(value, ('rows', 'feat'), pairs)]
    slice x9 -> x8, local copies, waits for them, and re-layouts: 17.2 us -> 15.5 us  [shards(): pieces.append(head(ready, r1, f1) if i == 0 else ready[r0:r1, f0:f1])]
  transfers between devices with their start and end apart: 33 -> 33, of which waited for: 26 -> 27; matrix products, arithmetic and copies ran while one was open for 14% -> 22% of each run, Pallas kernels for 0% -> 0%
where the time goes in v5:
time: 219 us; the launch traced here: 218 us
  waiting for transfers between devices  107 us (49%)
  starting transfers between devices  42 us (19%)
  matrix products  29.9 us (14%)
  Pallas kernels  17.6 us (8%)
  local copies, waits for them, and re-layouts  17.4 us (8%)
  other arithmetic  4.15 us (2%)
    ppermute x33, waiting for transfers between devices, exchange(): return lax.ppermute(value, ('rows', 'feat'), pairs)  107 us
    ppermute x33, starting transfers between devices, exchange(): return lax.ppermute(value, ('rows', 'feat'), pairs)  42 us
    dot_general x9, matrix products, project(): jnp.dot(after(moved[i], *needed), basis[f0:f1], preferred_element_type=jn...  28.3 us
    pallas_call x1, Pallas kernels, dot(): pl.pallas_call(dot_kernel, out_shape=jax.ShapeDtypeStruct((rows, columns)...  16.7 us
    slice x8, local copies, waits for them, and re-layouts, shards(): pieces.append(head(ready, r1, f1) if i == 0 else ready[r0:r1, f0:f1])  15.5 us
  transfers between devices with their start and end apart: 33, of which 27 were waited for; matrix products, arithmetic and copies ran while one was open for 22% of the time, Pallas kernels for 0%

profile of v5, /device:TPU:0, one launch (start us, length us, event | category | flops | bytes accessed | tf_op | source)
XLA Modules:
  0.0 218.0 jit_solution(2018658739864836979)
XLA Ops:
  0.0 1.0 head.1
  1.0 3.0 %collective-permute-start = (bf16[32,4096]{1,0:T(8,128)(2,1)S(1)}, bf16[32,4096]{1,0:T(8,128)(2,1)S(1)}, u32[]{:S(2)}, u32[]{:S(2)}) collective-permute-start(bf16[32,4096]{1,0:T(8,128)(2,1)S(1)} %head.1), channel_id=1, source_target_pairs={{0,16},{1,17},{2,18},{3,19},{4,20},{5,21},{6,22},{7,23},{8,24},{9,... | collective-permute-start | bytes 786440 | tf_op jit(solution)/shard_map/ppermute | solution.py:30
  4.0 2.1 slice.63
  6.1 3.1 %slice.64 = bf16[64,16384]{1,0:T(8,128)(2,1)} slice(bf16[224,16384]{1,0:T(8,128)(2,1)} %left_ref), slice={[32:96], [0:16384]} | slice | bytes 4194304 | tf_op jit(solution)/shard_map/slice | solution.py:152
  9.1 2.9 %slice.65 = bf16[56,16384]{1,0:T(8,128)(2,1)} slice(bf16[224,16384]{1,0:T(8,128)(2,1)} %left_ref), slice={[96:152], [0:16384]} | slice | bytes 3670016 | tf_op jit(solution)/shard_map/slice | solution.py:152
  12.0 1.3 slice.66
  13.3 1.8 slice.67
  15.1 1.8 slice.68
  16.9 1.7 slice.69
  18.6 0.9 slice.70
  19.5 16.7 %dot.1 = f32[224,512]{1,0:T(8,128)} custom-call(bf16[224,16384]{1,0:T(8,128)(2,1)} %left_ref, bf16[16384,512]{1,0:T(8,128)(2,1)} %right_ref.1), custom_call_target="tpu_custom_call" | custom-call | flops 3758096384 | bytes 24576000 | tf_op jit(solution)/shard_map/dot/pallas_call | solution.py:102
  36.2 1.7 constant_dynamic-slice_fusion.7
  37.9 1.8 collective-permute-done.1
  39.7 1.1 dynamic-slice_add_fusion
  40.8 1.3 collective-permute-start.2
  42.1 6.3 %collective-permute-done.2 = f32[224,256]{1,0:T(8,128)S(1)} collective-permute-done((f32[224,256]{1,0:T(8,128)S(1)}, f32[224,256]{1,0:T(8,128)S(1)}, u32[]{:S(2)}, u32[]{:S(2)}) %collective-permute-start.2) | collective-permute-done | bytes 229408 | tf_op jit(solution)/shard_map/ppermute | solution.py:30
  48.4 1.7 collective-permute-start.3
  50.1 5.7 %collective-permute-done.3 = f32[224,256]{1,0:T(8,128)S(1)} collective-permute-done((f32[224,256]{1,0:T(8,128)S(1)}, f32[224,256]{1,0:T(8,128)S(1)}, u32[]{:S(2)}, u32[]{:S(2)}) %collective-permute-start.3) | collective-permute-done | bytes 229408 | tf_op jit(solution)/shard_map/ppermute | solution.py:30
  56.5 2.9 %collective-permute-start.4 = (f32[224,256]{1,0:T(8,128)}, f32[224,256]{1,0:T(8,128)}, u32[]{:S(2)}, u32[]{:S(2)}) collective-permute-start(f32[224,256]{1,0:T(8,128)} %add.136), channel_id=1, source_target_pairs={{0,9},{1,8},{2,11},{3,10},{4,13},{5,12},{6,15},{7,14},{8,1},{9,0},... | collective-permute-start | bytes 688136 | tf_op jit(solution)/shard_map/ppermute | solution.py:30
  60.0 1.5 collective-permute-start.11
  62.2 8.0 %collective-permute-done.4 = f32[224,256]{1,0:T(8,128)} collective-permute-done((f32[224,256]{1,0:T(8,128)}, f32[224,256]{1,0:T(8,128)}, u32[]{:S(2)}, u32[]{:S(2)}) %collective-permute-start.4) | collective-permute-done | bytes 229408 | tf_op jit(solution)/shard_map/ppermute | solution.py:30
  70.2 1.1 divide_convert_fusion
  71.3 3.1 %fusion.10 = f32[32,512]{1,0:T(8,128)S(1)} fusion(bf16[32,4096]{1,0:T(8,128)(2,1)} %copy-done.4, bf16[16384,512]{1,0:T(8,128)(2,1)} %right_ref.1), kind=kOutput, calls=%fused_computation.10 | convolution fusion | flops 134217728 | bytes 4521984 | tf_op jit(solution)/shard_map/dot_general | solution.py:174
  74.4 29.1 %collective-permute-done.5 = bf16[32,12288]{1,0:T(8,128)(2,1)} collective-permute-done((bf16[32,12288]{1,0:T(8,128)(2,1)}, bf16[32,12288]{1,0:T(8,128)(2,1)}, u32[]{:S(2)}, u32[]{:S(2)}) %collective-permute-start.5) | collective-permute-done | bytes 786464 | tf_op jit(solution)/shard_map/ppermute | solution.py:30
  103.5 6.2 %fusion.17 = f32[32,512]{1,0:T(8,128)S(1)} fusion(f32[32,512]{1,0:T(8,128)S(1)} %fusion.10, bf16[32,12288]{1,0:T(8,128)(2,1)} %collective-permute-done.5, bf16[16384,512]{1,0:T(8,128)(2,1)} %right_ref.1), kind=kOutput, calls=%fused_computation.16 | convolution fusion | flops 402669568 | bytes 13500416 | tf_op jit(solution)/shard_map/dot_general | solution.py:174
  109.8 8.9 %fusion.37 = f32[64,512]{1,0:T(8,128)S(1)} fusion(bf16[64,16384]{1,0:T(8,128)(2,1)S(1)} %collective-permute-done.6, bf16[16384,512]{1,0:T(8,128)(2,1)} %right_ref.1), kind=kOutput, calls=%fused_computation.67 | convolution fusion | flops 1073741824 | bytes 19005440 | tf_op jit(solution)/shard_map/dot_general | solution.py:174
  118.8 1.3 collective-permute-done.7
  120.1 1.3 collective-permute-start.8
  121.4 3.5 %collective-permute-done.8 = f32[96,256]{1,0:T(8,128)S(1)} collective-permute-done((f32[96,256]{1,0:T(8,128)S(1)}, f32[96,256]{1,0:T(8,128)S(1)}, u32[]{:S(2)}, u32[]{:S(2)}) %collective-permute-start.8) | collective-permute-done | bytes 98336 | tf_op jit(solution)/shard_map/ppermute | solution.py:30
  124.9 1.8 collective-permute-start.9
  126.7 2.6 %collective-permute-done.9 = f32[96,256]{1,0:T(8,128)S(1)} collective-permute-done((f32[96,256]{1,0:T(8,128)S(1)}, f32[96,256]{1,0:T(8,128)S(1)}, u32[]{:S(2)}, u32[]{:S(2)}) %collective-permute-start.9) | collective-permute-done | bytes 98336 | tf_op jit(solution)/shard_map/ppermute | solution.py:30
  129.4 3.2 %collective-permute-start.10 = (f32[96,256]{1,0:T(8,128)S(1)}, f32[96,256]{1,0:T(8,128)S(1)}, u32[]{:S(2)}, u32[]{:S(2)}) collective-permute-start(f32[96,256]{1,0:T(8,128)S(1)} %add.151), channel_id=1, source_target_pairs={{0,9},{1,8},{2,11},{3,10},{4,13},{5,12},{6,15},{7,14},{8,1},{9,0},... | collective-permute-start | bytes 294920 | tf_op jit(solution)/shard_map/ppermute | solution.py:30
  133.1 4.3 %collective-permute-done.10 = f32[96,256]{1,0:T(8,128)S(1)} collective-permute-done((f32[96,256]{1,0:T(8,128)S(1)}, f32[96,256]{1,0:T(8,128)S(1)}, u32[]{:S(2)}, u32[]{:S(2)}) %collective-permute-start.10) | collective-permute-done | bytes 98336 | tf_op jit(solution)/shard_map/ppermute | solution.py:30
  137.5 5.4 %collective-permute-done.11 = bf16[56,16384]{1,0:T(8,128)(2,1)} collective-permute-done((bf16[56,16384]{1,0:T(8,128)(2,1)}, bf16[56,16384]{1,0:T(8,128)(2,1)}, u32[]{:S(2)}, u32[]{:S(2)}) %collective-permute-start.11) | collective-permute-done | bytes 1835040 | tf_op jit(solution)/shard_map/ppermute | solution.py:30
  142.9 4.3 %fusion.38 = f32[56,512]{1,0:T(8,128)S(1)} fusion(bf16[56,16384]{1,0:T(8,128)(2,1)} %collective-permute-done.11, bf16[16384,512]{1,0:T(8,128)(2,1)S(1)} %bitcast.12), kind=kOutput, calls=%fused_computation.68 | convolution fusion | flops 939524096 | bytes 18726912 | tf_op jit(solution)/shard_map/dot_general | solution.py:174
  147.3 1.2 collective-permute-done.12
  148.5 1.3 collective-permute-start.13
  149.9 2.6 %collective-permute-done.13 = f32[56,256]{1,0:T(8,128)S(1)} collective-permute-done((f32[56,256]{1,0:T(8,128)S(1)}, f32[56,256]{1,0:T(8,128)S(1)}, u32[]{:S(2)}, u32[]{:S(2)}) %collective-permute-start.13) | collective-permute-done | bytes 57376 | tf_op jit(solution)/shard_map/ppermute | solution.py:30
  152.5 1.7 collective-permute-start.14
  154.2 2.0 collective-permute-done.14
  156.2 3.0 %collective-permute-start.15 = (f32[56,256]{1,0:T(8,128)S(1)}, f32[56,256]{1,0:T(8,128)S(1)}, u32[]{:S(2)}, u32[]{:S(2)}) collective-permute-start(f32[56,256]{1,0:T(8,128)S(1)} %add.155), channel_id=1, source_target_pairs={{0,9},{1,8},{2,11},{3,10},{4,13},{5,12},{6,15},{7,14},{8,1},{9,0},... | collective-permute-start | bytes 172040 | tf_op jit(solution)/shard_map/ppermute | solution.py:30
  159.2 1.9 collective-permute-done.15
  161.1 1.7 collective-permute-start.16
  163.4 1.5 collective-permute-start.23
  164.9 3.1 %collective-permute-done.17 = bf16[48,12288]{1,0:T(8,128)(2,1)S(1)} collective-permute-done((bf16[48,12288]{1,0:T(8,128)(2,1)S(1)}, bf16[48,12288]{1,0:T(8,128)(2,1)S(1)}, u32[]{:S(2)}, u32[]{:S(2)}) %collective-permute-start.17) | collective-permute-done | bytes 1179680 | tf_op jit(solution)/shard_map/ppermute | solution.py:30
  168.0 2.5 %fusion = f32[48,512]{1,0:T(8,128)S(1)} fusion(bf16[48,12288]{1,0:T(8,128)(2,1)S(1)} %collective-permute-done.17, bf16[16384,512]{1,0:T(8,128)(2,1)S(1)} %bitcast.12), kind=kOutput, calls=%fused_computation | convolution fusion | flops 603979776 | bytes 13860864 | tf_op jit(solution)/shard_map/dot_general | solution.py:174
  170.5 6.0 %collective-permute-done.18 = bf16[48,4096]{1,0:T(8,128)(2,1)S(1)} collective-permute-done((bf16[48,4096]{1,0:T(8,128)(2,1)S(1)}, bf16[48,4096]{1,0:T(8,128)(2,1)S(1)}, u32[]{:S(2)}, u32[]{:S(2)}) %collective-permute-start.18) | collective-permute-done | bytes 393248 | tf_op jit(solution)/shard_map/ppermute | solution.py:30
  177.4 1.2 collective-permute-done.19
  178.6 1.3 collective-permute-start.20
  180.5 1.5 collective-permute-start.25
  182.4 1.7 collective-permute-start.21
  184.9 1.2 fusion.4
  186.1 2.9 %collective-permute-start.22 = (f32[48,256]{1,0:T(8,128)S(1)}, f32[48,256]{1,0:T(8,128)S(1)}, u32[]{:S(2)}, u32[]{:S(2)}) collective-permute-start(f32[48,256]{1,0:T(8,128)S(1)} %add.160), channel_id=1, source_target_pairs={{0,9},{1,8},{2,11},{3,10},{4,13},{5,12},{6,15},{7,14},{8,1},{9,0},... | collective-permute-start | bytes 147464 | tf_op jit(solution)/shard_map/ppermute | solution.py:30
  189.0 2.2 %collective-permute-done.24 = bf16[24,6144]{1,0:T(8,128)(2,1)S(1)} collective-permute-done((bf16[24,6144]{1,0:T(8,128)(2,1)S(1)}, bf16[24,6144]{1,0:T(8,128)(2,1)S(1)}, u32[]{:S(2)}, u32[]{:S(2)}) %collective-permute-start.24) | collective-permute-done | bytes 294944 | tf_op jit(solution)/shard_map/ppermute | solution.py:30
  191.2 0.9 fusion.23
  193.3 1.2 collective-permute-done.26
  194.5 1.3 collective-permute-start.27
  195.8 2.0 collective-permute-done.27
  197.8 1.3 collective-permute-start.28
  199.1 1.9 collective-permute-done.28
  201.0 2.4 %collective-permute-start.29 = (f32[24,256]{1,0:T(8,128)S(1)}, f32[24,256]{1,0:T(8,128)S(1)}, u32[]{:S(2)}, u32[]{:S(2)}) collective-permute-start(f32[24,256]{1,0:T(8,128)S(1)} %add.166), channel_id=1, source_target_pairs={{0,9},{1,8},{2,11},{3,10},{4,13},{5,12},{6,15},{7,14},{8,1},{9,0},... | collective-permute-start | bytes 73736 | tf_op jit(solution)/shard_map/ppermute | solution.py:30
  203.9 1.3 collective-permute-done.29
  205.6 9.3 %collective-permute-done.30 = bf16[72,256]{1,0:T(8,128)(2,1)S(1)} collective-permute-done((bf16[72,256]{1,0:T(8,128)(2,1)S(1)}, bf16[72,256]{1,0:T(8,128)(2,1)S(1)}, u32[]{:S(2)}, u32[]{:S(2)}) %collective-permute-start.30) | collective-permute-done | bytes 36896 | tf_op jit(solution)/shard_map/ppermute | solution.py:30
  216.4 1.6 convolution_select_fusion
  (80 shorter events, 9.7 us)
Async XLA Ops:
  1.0 18.5 %collective-permute-start = (bf16[32,4096]{1,0:T(8,128)(2,1)S(1)}, bf16[32,4096]{1,0:T(8,128)(2,1)S(1)}, u32[]{:S(2)}, u32[]{:S(2)}) collective-permute-start(bf16[32,4096]{1,0:T(8,128)(2,1)S(1)} %head.1), channel_id=1, source_target_pairs={{0,16},{1,17},{2,18},{3,19},{4,20},{5,21},{6,22},{7,23},{8,24},{9,... | collective-permute-start | bytes 786440 | tf_op jit(solution)/shard_map/ppermute | solution.py:30
  19.5 16.7 %copy-start.4 = (bf16[32,4096]{1,0:T(8,128)(2,1)}, bf16[32,4096]{1,0:T(8,128)(2,1)S(1)}, u32[]{:S(2)}) copy-start(bf16[32,4096]{1,0:T(8,128)(2,1)S(1)} %collective-permute-done) | copy-start | bytes 786436
  37.9 1.8 collective-permute-start.1
  37.9 71.9 %collective-permute-start.6 = (bf16[64,16384]{1,0:T(8,128)(2,1)}, bf16[64,16384]{1,0:T(8,128)(2,1)S(1)}, u32[]{:S(2)}, u32[]{:S(2)}) collective-permute-start(bf16[64,16384]{1,0:T(8,128)(2,1)} %slice.64), channel_id=1, source_target_pairs={{0,16},{1,17},{2,18},{3,19},{4,20},{5,21},{6,22},{7,23},{8,24},{9,... | collective-permute-start | bytes 6291464 | tf_op jit(solution)/shard_map/ppermute | solution.py:30
  40.8 7.7 %collective-permute-start.2 = (f32[224,256]{1,0:T(8,128)S(1)}, f32[224,256]{1,0:T(8,128)S(1)}, u32[]{:S(2)}, u32[]{:S(2)}) collective-permute-start(f32[224,256]{1,0:T(8,128)S(1)} %dynamic-slice_add_fusion), channel_id=1, source_target_pairs={{0,3},{1,2},{2,1},{3,0},{4,7},{5,6},{6,5},{7,4},{8,11},{9,10},{10,... | collective-permute-start | bytes 688136 | tf_op jit(solution)/shard_map/ppermute | solution.py:30
  48.4 7.4 %collective-permute-start.3 = (f32[224,256]{1,0:T(8,128)S(1)}, f32[224,256]{1,0:T(8,128)S(1)}, u32[]{:S(2)}, u32[]{:S(2)}) collective-permute-start(f32[224,256]{1,0:T(8,128)S(1)} %add.135), channel_id=1, source_target_pairs={{0,5},{1,4},{2,7},{3,6},{4,1},{5,0},{6,3},{7,2},{8,13},{9,12},{10,... | collective-permute-start | bytes 688136 | tf_op jit(solution)/shard_map/ppermute | solution.py:30
  56.5 13.7 %collective-permute-start.4 = (f32[224,256]{1,0:T(8,128)}, f32[224,256]{1,0:T(8,128)}, u32[]{:S(2)}, u32[]{:S(2)}) collective-permute-start(f32[224,256]{1,0:T(8,128)} %add.136), channel_id=1, source_target_pairs={{0,9},{1,8},{2,11},{3,10},{4,13},{5,12},{6,15},{7,14},{8,1},{9,0},... | collective-permute-start | bytes 688136 | tf_op jit(solution)/shard_map/ppermute | solution.py:30
  59.5 44.1 %collective-permute-start.5 = (bf16[32,12288]{1,0:T(8,128)(2,1)}, bf16[32,12288]{1,0:T(8,128)(2,1)}, u32[]{:S(2)}, u32[]{:S(2)}) collective-permute-start(bf16[32,12288]{1,0:T(8,128)(2,1)} %slice.63), channel_id=1, source_target_pairs={{0,16},{1,17},{2,18},{3,19},{4,20},{5,21},{6,22},{7,23},{8,24},{9,... | collective-permute-start | bytes 2359304 | tf_op jit(solution)/shard_map/ppermute | solution.py:30
  60.0 82.9 %collective-permute-start.11 = (bf16[56,16384]{1,0:T(8,128)(2,1)}, bf16[56,16384]{1,0:T(8,128)(2,1)}, u32[]{:S(2)}, u32[]{:S(2)}) collective-permute-start(bf16[56,16384]{1,0:T(8,128)(2,1)} %slice.65), channel_id=1, source_target_pairs={{0,16},{1,17},{2,18},{3,19},{4,20},{5,21},{6,22},{7,23},{8,24},{9,... | collective-permute-start | bytes 5505032 | tf_op jit(solution)/shard_map/ppermute | solution.py:30
  103.5 39.3 %slice-start = ((s8[16777216]{0:T(1024)(128)(4,1)}), s8[4194304]{0:T(1024)(128)(4,1)S(1)}, s32[]{:S(2)}) async-start(s8[16777216]{0:T(1024)(128)(4,1)} %bitcast.11), calls=%async_computation | async-start | bytes 8388608
  103.5 39.3 %slice-start.1 = ((s8[16777216]{0:T(1024)(128)(4,1)}), s8[4194304]{0:T(1024)(128)(4,1)S(1)}, s32[]{:S(2)}) async-start(s8[16777216]{0:T(1024)(128)(4,1)} %bitcast.11), calls=%async_computation.1 | async-start | bytes 8388608
  109.7 33.1 %slice-start.2 = ((s8[16777216]{0:T(1024)(128)(4,1)}), s8[4194304]{0:T(1024)(128)(4,1)S(1)}, s32[]{:S(2)}) async-start(s8[16777216]{0:T(1024)(128)(4,1)} %bitcast.11), calls=%async_computation.2 | async-start | bytes 8388608
  109.7 33.1 %slice-start.3 = ((s8[16777216]{0:T(1024)(128)(4,1)}), s8[4194304]{0:T(1024)(128)(4,1)S(1)}, s32[]{:S(2)}) async-start(s8[16777216]{0:T(1024)(128)(4,1)} %bitcast.11), calls=%async_computation.3 | async-start | bytes 8388608
  118.7 1.4 collective-permute-start.7
  120.1 4.8 %collective-permute-start.8 = (f32[96,256]{1,0:T(8,128)S(1)}, f32[96,256]{1,0:T(8,128)S(1)}, u32[]{:S(2)}, u32[]{:S(2)}) collective-permute-start(f32[96,256]{1,0:T(8,128)S(1)} %fusion.34), channel_id=1, source_target_pairs={{0,3},{1,2},{2,1},{3,0},{4,7},{5,6},{6,5},{7,4},{8,11},{9,10},{10,... | collective-permute-start | bytes 294920 | tf_op jit(solution)/shard_map/ppermute | solution.py:30
  124.9 4.4 %collective-permute-start.9 = (f32[96,256]{1,0:T(8,128)S(1)}, f32[96,256]{1,0:T(8,128)S(1)}, u32[]{:S(2)}, u32[]{:S(2)}) collective-permute-start(f32[96,256]{1,0:T(8,128)S(1)} %add.150), channel_id=1, source_target_pairs={{0,5},{1,4},{2,7},{3,6},{4,1},{5,0},{6,3},{7,2},{8,13},{9,12},{10,... | collective-permute-start | bytes 294920 | tf_op jit(solution)/shard_map/ppermute | solution.py:30
  129.4 8.1 %collective-permute-start.10 = (f32[96,256]{1,0:T(8,128)S(1)}, f32[96,256]{1,0:T(8,128)S(1)}, u32[]{:S(2)}, u32[]{:S(2)}) collective-permute-start(f32[96,256]{1,0:T(8,128)S(1)} %add.151), channel_id=1, source_target_pairs={{0,9},{1,8},{2,11},{3,10},{4,13},{5,12},{6,15},{7,14},{8,1},{9,0},... | collective-permute-start | bytes 294920 | tf_op jit(solution)/shard_map/ppermute | solution.py:30
  132.6 35.4 %collective-permute-start.17 = (bf16[48,12288]{1,0:T(8,128)(2,1)S(1)}, bf16[48,12288]{1,0:T(8,128)(2,1)S(1)}, u32[]{:S(2)}, u32[]{:S(2)}) collective-permute-start(bf16[48,12288]{1,0:T(8,128)(2,1)S(1)} %slice.66), channel_id=1, source_target_pairs={{0,16},{1,17},{2,18},{3,19},{4,20},{5,21},{6,22},{7,23},{8,24},{9,... | collective-permute-start | bytes 3538952 | tf_op jit(solution)/shard_map/ppermute | solution.py:30
  137.4 25.4 %copy-start.2 = (bf16[48,4096]{1,0:T(8,128)(2,1)S(1)}, bf16[48,4096]{1,0:T(8,128)(2,1)}, u32[]{:S(2)}) copy-start(bf16[48,4096]{1,0:T(8,128)(2,1)} %slice.67) | copy-start | bytes 1179652
  137.5 25.9 %copy-start.1 = (bf16[24,8192]{1,0:T(8,128)(2,1)S(1)}, bf16[24,8192]{1,0:T(8,128)(2,1)}, u32[]{:S(2)}) copy-start(bf16[24,8192]{1,0:T(8,128)(2,1)} %slice.68) | copy-start | bytes 1179652
  147.2 1.3 collective-permute-start.12
  148.5 3.9 %collective-permute-start.13 = (f32[56,256]{1,0:T(8,128)S(1)}, f32[56,256]{1,0:T(8,128)S(1)}, u32[]{:S(2)}, u32[]{:S(2)}) collective-permute-start(f32[56,256]{1,0:T(8,128)S(1)} %dynamic-slice_add_fusion.1), channel_id=1, source_target_pairs={{0,3},{1,2},{2,1},{3,0},{4,7},{5,6},{6,5},{7,4},{8,11},{9,10},{10,... | collective-permute-start | bytes 172040 | tf_op jit(solution)/shard_map/ppermute | solution.py:30
  152.5 3.7 %collective-permute-start.14 = (f32[56,256]{1,0:T(8,128)S(1)}, f32[56,256]{1,0:T(8,128)S(1)}, u32[]{:S(2)}, u32[]{:S(2)}) collective-permute-start(f32[56,256]{1,0:T(8,128)S(1)} %add.154), channel_id=1, source_target_pairs={{0,5},{1,4},{2,7},{3,6},{4,1},{5,0},{6,3},{7,2},{8,13},{9,12},{10,... | collective-permute-start | bytes 172040 | tf_op jit(solution)/shard_map/ppermute | solution.py:30
  156.2 4.9 %collective-permute-start.15 = (f32[56,256]{1,0:T(8,128)S(1)}, f32[56,256]{1,0:T(8,128)S(1)}, u32[]{:S(2)}, u32[]{:S(2)}) collective-permute-start(f32[56,256]{1,0:T(8,128)S(1)} %add.155), channel_id=1, source_target_pairs={{0,9},{1,8},{2,11},{3,10},{4,13},{5,12},{6,15},{7,14},{8,1},{9,0},... | collective-permute-start | bytes 172040 | tf_op jit(solution)/shard_map/ppermute | solution.py:30
  161.1 3.8 %collective-permute-start.16 = (bf16[376,256]{1,0:T(8,128)(2,1)S(1)}, bf16[376,256]{1,0:T(8,128)(2,1)S(1)}, u32[]{:S(2)}, u32[]{:S(2)}) collective-permute-start(bf16[376,256]{1,0:T(8,128)(2,1)S(1)} %pad_maximum_fusion.9), channel_id=1, source_target_pairs={{0,1},{1,0},{2,3},{3,2},{4,5},{5,4},{6,7},{7,6},{8,9},{9,8},{10,11... | collective-permute-start | bytes 577544 | tf_op jit(solution)/shard_map/ppermute | solution.py:30
  162.8 13.6 %collective-permute-start.18 = (bf16[48,4096]{1,0:T(8,128)(2,1)S(1)}, bf16[48,4096]{1,0:T(8,128)(2,1)S(1)}, u32[]{:S(2)}, u32[]{:S(2)}) collective-permute-start(bf16[48,4096]{1,0:T(8,128)(2,1)S(1)} %copy-done.2), channel_id=1, source_target_pairs={{0,16},{1,17},{2,18},{3,19},{4,20},{5,21},{6,22},{7,23},{8,24},{9,... | collective-permute-start | bytes 1179656 | tf_op jit(solution)/shard_map/ppermute | solution.py:30
  163.4 21.5 %collective-permute-start.23 = (bf16[24,8192]{1,0:T(8,128)(2,1)S(1)}, bf16[24,8192]{1,0:T(8,128)(2,1)S(1)}, u32[]{:S(2)}, u32[]{:S(2)}) collective-permute-start(bf16[24,8192]{1,0:T(8,128)(2,1)S(1)} %copy-done.1), channel_id=1, source_target_pairs={{0,16},{1,17},{2,18},{3,19},{4,20},{5,21},{6,22},{7,23},{8,24},{9,... | collective-permute-start | bytes 1179656 | tf_op jit(solution)/shard_map/ppermute | solution.py:30
  170.5 9.5 %copy-start.3 = (bf16[24,6144]{1,0:T(8,128)(2,1)S(1)}, bf16[24,6144]{1,0:T(8,128)(2,1)}, u32[]{:S(2)}) copy-start(bf16[24,6144]{1,0:T(8,128)(2,1)} %slice.69) | copy-start | bytes 884740
  177.3 1.3 collective-permute-start.19
  178.6 3.8 %collective-permute-start.20 = (f32[48,256]{1,0:T(8,128)S(1)}, f32[48,256]{1,0:T(8,128)S(1)}, u32[]{:S(2)}, u32[]{:S(2)}) collective-permute-start(f32[48,256]{1,0:T(8,128)S(1)} %dynamic-slice_add_fusion.2), channel_id=1, source_target_pairs={{0,3},{1,2},{2,1},{3,0},{4,7},{5,6},{6,5},{7,4},{8,11},{9,10},{10,... | collective-permute-start | bytes 147464 | tf_op jit(solution)/shard_map/ppermute | solution.py:30
  180.0 11.2 %collective-permute-start.24 = (bf16[24,6144]{1,0:T(8,128)(2,1)S(1)}, bf16[24,6144]{1,0:T(8,128)(2,1)S(1)}, u32[]{:S(2)}, u32[]{:S(2)}) collective-permute-start(bf16[24,6144]{1,0:T(8,128)(2,1)S(1)} %copy-done.3), channel_id=1, source_target_pairs={{0,16},{1,17},{2,18},{3,19},{4,20},{5,21},{6,22},{7,23},{8,24},{9,... | collective-permute-start | bytes 884744 | tf_op jit(solution)/shard_map/ppermute | solution.py:30
  180.5 12.3 %collective-permute-start.25 = (bf16[24,2048]{1,0:T(8,128)(2,1)S(1)}, bf16[24,2048]{1,0:T(8,128)(2,1)S(1)}, u32[]{:S(2)}, u32[]{:S(2)}) collective-permute-start(bf16[24,2048]{1,0:T(8,128)(2,1)S(1)} %slice.70), channel_id=1, source_target_pairs={{0,16},{1,17},{2,18},{3,19},{4,20},{5,21},{6,22},{7,23},{8,24},{9,... | collective-permute-start | bytes 294920 | tf_op jit(solution)/shard_map/ppermute | solution.py:30
  182.4 3.7 %collective-permute-start.21 = (f32[48,256]{1,0:T(8,128)S(1)}, f32[48,256]{1,0:T(8,128)S(1)}, u32[]{:S(2)}, u32[]{:S(2)}) collective-permute-start(f32[48,256]{1,0:T(8,128)S(1)} %add.159), channel_id=1, source_target_pairs={{0,5},{1,4},{2,7},{3,6},{4,1},{5,0},{6,3},{7,2},{8,13},{9,12},{10,... | collective-permute-start | bytes 147464 | tf_op jit(solution)/shard_map/ppermute | solution.py:30
  186.1 19.4 %copy-start = (bf16[512,1024]{1,0:T(8,128)(2,1)S(1)}, bf16[512,1024]{1,0:T(8,128)(2,1)}, u32[]{:S(2)}) copy-start(bf16[512,1024]{1,0:T(8,128)(2,1)} %param.8) | copy-start | bytes 3145732
  186.1 6.0 %collective-permute-start.22 = (f32[48,256]{1,0:T(8,128)S(1)}, f32[48,256]{1,0:T(8,128)S(1)}, u32[]{:S(2)}, u32[]{:S(2)}) collective-permute-start(f32[48,256]{1,0:T(8,128)S(1)} %add.160), channel_id=1, source_target_pairs={{0,9},{1,8},{2,11},{3,10},{4,13},{5,12},{6,15},{7,14},{8,1},{9,0},... | collective-permute-start | bytes 147464 | tf_op jit(solution)/shard_map/ppermute | solution.py:30
  193.2 23.2 %copy-start.5 = (s32[448]{0:T(512)S(1)}, s32[448]{0:T(512)}, u32[]{:S(2)}) copy-start(s32[448]{0:T(512)} %param.9) | copy-start | bytes 5380
  193.2 1.3 collective-permute-start.26
  194.5 3.3 %collective-permute-start.27 = (f32[24,256]{1,0:T(8,128)S(1)}, f32[24,256]{1,0:T(8,128)S(1)}, u32[]{:S(2)}, u32[]{:S(2)}) collective-permute-start(f32[24,256]{1,0:T(8,128)S(1)} %dynamic-slice_add_fusion.3), channel_id=1, source_target_pairs={{0,3},{1,2},{2,1},{3,0},{4,7},{5,6},{6,5},{7,4},{8,11},{9,10},{10,... | collective-permute-start | bytes 73736 | tf_op jit(solution)/shard_map/ppermute | solution.py:30
  197.8 3.3 %collective-permute-start.28 = (f32[24,256]{1,0:T(8,128)S(1)}, f32[24,256]{1,0:T(8,128)S(1)}, u32[]{:S(2)}, u32[]{:S(2)}) collective-permute-start(f32[24,256]{1,0:T(8,128)S(1)} %add.165), channel_id=1, source_target_pairs={{0,5},{1,4},{2,7},{3,6},{4,1},{5,0},{6,3},{7,2},{8,13},{9,12},{10,... | collective-permute-start | bytes 73736 | tf_op jit(solution)/shard_map/ppermute | solution.py:30
  201.0 4.2 %collective-permute-start.29 = (f32[24,256]{1,0:T(8,128)S(1)}, f32[24,256]{1,0:T(8,128)S(1)}, u32[]{:S(2)}, u32[]{:S(2)}) collective-permute-start(f32[24,256]{1,0:T(8,128)S(1)} %add.166), channel_id=1, source_target_pairs={{0,9},{1,8},{2,11},{3,10},{4,13},{5,12},{6,15},{7,14},{8,1},{9,0},... | collective-permute-start | bytes 73736 | tf_op jit(solution)/shard_map/ppermute | solution.py:30
  203.4 11.9 %collective-permute-start.32 = (bf16[376,512]{1,0:T(8,128)(2,1)S(1)}, bf16[376,512]{1,0:T(8,128)(2,1)S(1)}, u32[]{:S(2)}, u32[]{:S(2)}) collective-permute-start(bf16[376,512]{1,0:T(8,128)(2,1)S(1)} %pad_maximum_fusion.8), channel_id=1, source_target_pairs={{0,17},{1,16},{2,19},{3,18},{4,21},{5,20},{6,23},{7,22},{8,25},{9,... | collective-permute-start | bytes 1155080 | tf_op jit(solution)/shard_map/ppermute | solution.py:30
  205.2 9.7 %collective-permute-start.30 = (bf16[72,256]{1,0:T(8,128)(2,1)S(1)}, bf16[72,256]{1,0:T(8,128)(2,1)S(1)}, u32[]{:S(2)}, u32[]{:S(2)}) collective-permute-start(bf16[72,256]{1,0:T(8,128)(2,1)S(1)} %pad_maximum_fusion.11), channel_id=1, source_target_pairs={{0,17},{1,16},{2,19},{3,18},{4,21},{5,20},{6,23},{7,22},{8,25},{9,... | collective-permute-start | bytes 110600 | tf_op jit(solution)/shard_map/ppermute | solution.py:30
  214.9 1.3 collective-permute-start.31

commit v6 on v5

--- a/solution.py
+++ b/solution.py
@@ -34,34 +34,108 @@
     return lax.optimization_barrier((value, *needed))[0]
 
 
-def score(row, early, late, pair, store, same, rows, tail):
-    row_groups = len(early)
-    columns = []
-    for flip in range(row_groups):
-        spot = flip * tail
-        whole = jnp.concatenate(
-            [
-                early[flip],
-                jnp.concatenate([late[spot : spot + tail], pair[spot : spot + tail]], 1),
-            ],
-            0,
-        )
-        columns.append([whole[i * rows : (i + 1) * rows] for i in range(row_groups)])
-    blocks = [
-        jnp.concatenate([columns[flip][place ^ flip] for flip in range(row_groups)], 1)
-        for place in range(row_groups)
-    ]
-    bit = 1
+def place(row, blocks):
+    row_groups, bit = len(blocks), 1
     while bit < row_groups:
         moved = (row & bit) != 0
-        blocks = [
-            jnp.where(moved, blocks[place ^ bit], blocks[place]) for place in range(row_groups)
-        ]
+        blocks = [jnp.where(moved, blocks[a ^ bit], blocks[a]) for a in range(row_groups)]
         bit *= 2
-    product = lax.dot_general(
-        jnp.concatenate(blocks, 0), store, CONTRACT_LAST, preferred_element_type=jnp.float32
-    )
-    return jnp.where(same(product.shape), jnp.zeros_like(product), product)
+    return jnp.concatenate(blocks, 0)
+
+
+def product(left, right):
+    return lax.dot_general(left, right, CONTRACT_LAST, preferred_element_type=jnp.float32)
+
+
+def arrange(row, early, rows, tail):
+    row_groups, width = len(early), early[0].shape[1]
+    blocks = []
+    for a in range(row_groups):
+        parts = []
+        for flip in range(row_groups):
+            spot = (a ^ flip) * rows
+            if a ^ flip == row_groups - 1:
+                part = early[flip][spot : spot + rows - tail]
+                part = jnp.concatenate([part, jnp.zeros((tail, width), part.dtype)], 0)
+            else:
+                part = early[flip][spot : spot + rows]
+            parts.append(part)
+        blocks.append(jnp.concatenate(parts, 1))
+    return place(row, blocks)
+
+
+def partial_scores(early, store, rows, tail):
+    row_groups, width = len(early), early[0].shape[1]
+    values = []
+    for a in range(row_groups):
+        total = 0.0
+        for flip in range(row_groups):
+            end = ((a ^ flip) + 1) * rows
+            if a ^ flip != row_groups - 1:
+                total += product(
+                    early[flip][end - tail : end], store[:, flip * width : (flip + 1) * width]
+                )
+        values.append(total)
+    return jnp.concatenate(values, 0)
+
+
+def masked_product(whitened, store, slab_index):
+    value = product(whitened, store)
+    columns = lax.broadcasted_iota(jnp.int32, value.shape, 1)
+    return jnp.where(slab_index[:, None] == columns, jnp.zeros_like(value), value)
+
+
+def score_late_kernel(
+    row_groups, rows, row_ref, late_ref, pair_ref, store_ref, partial_ref, index_ref, _, out_ref,
+    held, sent
+):
+    tail, half = late_ref.shape[0] // row_groups, late_ref.shape[1]
+    copies = []
+    for a in range(row_groups):
+        flip = (row_groups - 1) ^ a
+        spot, column = flip * tail, 2 * flip * half
+        value = partial_ref[a * tail : (a + 1) * tail, :]
+        value += product(
+            late_ref[spot : spot + tail, :], store_ref[:, column : column + half]
+        )
+        value += product(
+            pair_ref[spot : spot + tail, :], store_ref[:, column + half : column + 2 * half]
+        )
+        block = row_ref[0] ^ a
+        index = index_ref[pl.ds(pl.multiple_of(block * tail, 8), tail), :]
+        columns = lax.broadcasted_iota(jnp.int32, value.shape, 1)
+        held[a * tail : (a + 1) * tail, :] = jnp.where(
+            index == columns, jnp.zeros_like(value), value
+        )
+        copy = pltpu.make_async_copy(
+            held.at[pl.ds(a * tail, tail)],
+            out_ref.at[pl.ds(pl.multiple_of(block * rows + rows - tail, 8), tail)],
+            sent.at[a],
+        )
+        copy.start()
+        copies.append(copy)
+    for copy in copies:
+        copy.wait()
+
+
+def score_late(row, late, pair, store, partial_value, index, value, row_groups):
+    rows = value.shape[0] // row_groups
+    vmem = pl.BlockSpec(memory_space=pltpu.VMEM)
+    return pl.pallas_call(
+        functools.partial(score_late_kernel, row_groups, rows),
+        out_shape=jax.ShapeDtypeStruct(value.shape, value.dtype),
+        in_specs=[pl.BlockSpec(memory_space=pltpu.SMEM)]
+        + [vmem] * 5
+        + [pl.BlockSpec(memory_space=pl.ANY)],
+        out_specs=pl.BlockSpec(memory_space=pl.ANY),
+        scratch_shapes=[
+            pltpu.VMEM(partial_value.shape, jnp.float32),
+            pltpu.SemaphoreType.DMA((row_groups,)),
+        ],
+        input_output_aliases={6: 0},
+        compiler_params=pltpu.CompilerParams(vmem_limit_bytes=16 << 20),
+        name="score_late",
+    )(row.astype(jnp.int32).reshape(1), late, pair, store, partial_value, index, value)
 
 
 def dot_kernel(left_ref, right_ref, out_ref):
@@ -166,8 +240,9 @@
             order.append(lax.dynamic_slice_in_dim(store_rows, base + part * half, half, 1))
     store = jnp.concatenate(order, 1)
 
-    def same(shape):
-        return slab_index[:, None] == first_column + lax.broadcasted_iota(jnp.int32, shape, 1)
+    tail = rows - ends[1]
+    shifted = slab_index - first_column
+    index = shifted.reshape(row_groups, rows)[:, rows - tail :].reshape(row_groups * tail, 1)
 
     def project(i, *needed):
         _, _, f0, f1 = cuts[i]
@@ -199,7 +274,7 @@
     for block in blocks:
         value = dot(after(block, *early), basis)
         early.append(reduce(value))
-    first = project(0, early[-1], store)
+    first = project(0, early[-1])
     first += project(1, first)
     early.append(reduce(jnp.concatenate([first, project(2, first)], 0)))
     early.append(reduce(project(3, early[-1])))
@@ -214,10 +289,18 @@
     late = project(6, middle_totals[1])
     late += project(7, late, middle_totals[2])
     late += project(8, late, middle)
-    late = jnp.concatenate([middle, reduce(late)], 0)
-    late = jnp.concatenate([late] + [cross(late, flip) for flip in range(1, row_groups)], 0)
-    pair = swap(late, row_flip=0, feat_flip=1)
-    return score(row, early, late, pair, store, same, rows, rows - ends[1])
+    late_totals = list(totals(halves(late)))
+    late = whiten(after(late_totals[-1], *early[1:]))
+    others = [after(part, late) for part in early[1:]]
+    whitened = arrange(row, [early[0]] + others, rows, tail)
+    value = masked_product(whitened, store, shifted)
+    others = [after(part, value) for part in early]
+    partial_value = partial_scores(others, store, rows, tail)
+    late = jnp.concatenate([middle, late], 0)
+    others = [cross(late, flip) for flip in range(1, row_groups)]
+    late = jnp.concatenate([late] + others, 0)
+    pair = swap(after(late, value), row_flip=0, feat_flip=1)
+    return score_late(row, late, pair, store, partial_value, index, value, row_groups)
 
 
 def plain(slab_grads, basis, eigenvalues, store_rows, slab_index, *, row_groups, feat_groups):

time: 219 us -> 215 us (0.982)
  waiting for transfers between devices: 107 us -> 98.9 us
    ppermute x33, waiting for transfers between devices: 107 us -> 98.9 us  [exchange(): return lax.ppermute(value, ('rows', 'feat'), pairs)]
where the time goes in v6:
time: 215 us; the launch traced here: 214 us
  waiting for transfers between devices  98.9 us (46%)
  starting transfers between devices  43.8 us (20%)
  matrix products  30.6 us (14%)
  Pallas kernels  18.8 us (9%)
  local copies, waits for them, and re-layouts  18.3 us (9%)
  other arithmetic  3.35 us (2%)
    ppermute x33, waiting for transfers between devices, exchange(): return lax.ppermute(value, ('rows', 'feat'), pairs)  98.9 us
    ppermute x33, starting transfers between devices, exchange(): return lax.ppermute(value, ('rows', 'feat'), pairs)  43.8 us
    dot_general x9, matrix products, project(): jnp.dot(after(moved[i], *needed), basis[f0:f1], preferred_element_type=jn...  28.5 us
    pallas_call x1, Pallas kernels, dot(): pl.pallas_call(dot_kernel, out_shape=jax.ShapeDtypeStruct((rows, columns)...  16.7 us
    slice x8, local copies, waits for them, and re-layouts, shards(): pieces.append(head(ready, r1, f1) if i == 0 else ready[r0:r1, f0:f1])  16.1 us
  transfers between devices with their start and end apart: 33, of which 27 were waited for; matrix products, arithmetic and copies ran while one was open for 22% of the time, Pallas kernels for 0%

profile of v6, /device:TPU:0, one launch (start us, length us, event | category | flops | bytes accessed | tf_op | source)
XLA Modules:
  0.0 214.3 jit_solution(16872471793123923764)
XLA Ops:
  0.0 1.0 head.1
  1.0 3.0 %collective-permute-start.1 = (bf16[32,4096]{1,0:T(8,128)(2,1)S(1)}, bf16[32,4096]{1,0:T(8,128)(2,1)S(1)}, u32[]{:S(2)}, u32[]{:S(2)}) collective-permute-start(bf16[32,4096]{1,0:T(8,128)(2,1)S(1)} %head.1), channel_id=1, source_target_pairs={{0,16},{1,17},{2,18},{3,19},{4,20},{5,21},{6,22},{7,23},{8,24},{9,... | collective-permute-start | bytes 786440 | tf_op jit(solution)/shard_map/ppermute | solution.py:30
  4.0 2.1 slice.70
  6.1 3.1 %slice.71 = bf16[64,16384]{1,0:T(8,128)(2,1)} slice(bf16[224,16384]{1,0:T(8,128)(2,1)} %left_ref), slice={[32:96], [0:16384]} | slice | bytes 4194304 | tf_op jit(solution)/shard_map/slice | solution.py:226
  9.1 2.9 %slice.73 = bf16[56,16384]{1,0:T(8,128)(2,1)} slice(bf16[224,16384]{1,0:T(8,128)(2,1)} %left_ref), slice={[96:152], [0:16384]} | slice | bytes 3670016 | tf_op jit(solution)/shard_map/slice | solution.py:226
  12.0 1.3 slice.72
  13.3 1.8 slice.74
  15.1 1.8 slice.75
  16.9 1.7 slice.76
  18.6 1.5 slice.77
  20.1 16.7 %dot.1 = f32[224,512]{1,0:T(8,128)} custom-call(bf16[224,16384]{1,0:T(8,128)(2,1)} %left_ref, bf16[16384,512]{1,0:T(8,128)(2,1)} %right_ref.1), custom_call_target="tpu_custom_call" | custom-call | flops 3758096384 | bytes 24576000 | tf_op jit(solution)/shard_map/dot/pallas_call | solution.py:176
  36.8 1.6 constant_dynamic-slice_fusion.7
  38.5 1.7 collective-permute-done.2
  40.1 1.0 dynamic-slice_add_fusion
  41.1 1.3 collective-permute-start.3
  42.4 6.3 %collective-permute-done.3 = f32[224,256]{1,0:T(8,128)S(1)} collective-permute-done((f32[224,256]{1,0:T(8,128)S(1)}, f32[224,256]{1,0:T(8,128)S(1)}, u32[]{:S(2)}, u32[]{:S(2)}) %collective-permute-start.3) | collective-permute-done | bytes 229408 | tf_op jit(solution)/shard_map/ppermute | solution.py:30
  48.8 1.7 collective-permute-start.4
  50.5 5.7 %collective-permute-done.4 = f32[224,256]{1,0:T(8,128)S(1)} collective-permute-done((f32[224,256]{1,0:T(8,128)S(1)}, f32[224,256]{1,0:T(8,128)S(1)}, u32[]{:S(2)}, u32[]{:S(2)}) %collective-permute-start.4) | collective-permute-done | bytes 229408 | tf_op jit(solution)/shard_map/ppermute | solution.py:30
  56.2 3.0 %collective-permute-start.5 = (f32[224,256]{1,0:T(8,128)S(1)}, f32[224,256]{1,0:T(8,128)}, u32[]{:S(2)}, u32[]{:S(2)}) collective-permute-start(f32[224,256]{1,0:T(8,128)S(1)} %add.130), channel_id=1, source_target_pairs={{0,9},{1,8},{2,11},{3,10},{4,13},{5,12},{6,15},{7,14},{8,1},{9,0},... | collective-permute-start | bytes 688136 | tf_op jit(solution)/shard_map/ppermute | solution.py:30
  59.7 1.5 collective-permute-start.12
  62.0 7.8 %collective-permute-done.5 = f32[224,256]{1,0:T(8,128)} collective-permute-done((f32[224,256]{1,0:T(8,128)S(1)}, f32[224,256]{1,0:T(8,128)}, u32[]{:S(2)}, u32[]{:S(2)}) %collective-permute-start.5) | collective-permute-done | bytes 229408 | tf_op jit(solution)/shard_map/ppermute | solution.py:30
  69.7 1.0 divide_convert_fusion
  70.7 3.1 %fusion.10 = f32[32,512]{1,0:T(8,128)S(1)} fusion(bf16[32,4096]{1,0:T(8,128)(2,1)} %copy-done.6, bf16[16384,512]{1,0:T(8,128)(2,1)} %right_ref.1), kind=kOutput, calls=%fused_computation.10 | convolution fusion | flops 134217728 | bytes 4521984 | tf_op jit(solution)/shard_map/dot_general | solution.py:249
  73.8 30.3 %collective-permute-done.6 = bf16[32,12288]{1,0:T(8,128)(2,1)} collective-permute-done((bf16[32,12288]{1,0:T(8,128)(2,1)}, bf16[32,12288]{1,0:T(8,128)(2,1)}, u32[]{:S(2)}, u32[]{:S(2)}) %collective-permute-start.6) | collective-permute-done | bytes 786464 | tf_op jit(solution)/shard_map/ppermute | solution.py:30
  104.1 6.2 %fusion.17 = f32[32,512]{1,0:T(8,128)S(1)} fusion(f32[32,512]{1,0:T(8,128)S(1)} %fusion.10, bf16[32,12288]{1,0:T(8,128)(2,1)} %collective-permute-done.6, bf16[16384,512]{1,0:T(8,128)(2,1)} %right_ref.1), kind=kOutput, calls=%fused_computation.16 | convolution fusion | flops 402669568 | bytes 13500416 | tf_op jit(solution)/shard_map/dot_general | solution.py:249
  110.3 8.9 %fusion.49 = f32[64,512]{1,0:T(8,128)S(1)} fusion(bf16[64,16384]{1,0:T(8,128)(2,1)S(1)} %collective-permute-done.7, bf16[16384,512]{1,0:T(8,128)(2,1)} %right_ref.1), kind=kOutput, calls=%fused_computation.76 | convolution fusion | flops 1073741824 | bytes 19005440 | tf_op jit(solution)/shard_map/dot_general | solution.py:249
  119.4 1.3 collective-permute-done.8
  120.7 1.3 collective-permute-start.9
  122.0 3.5 %collective-permute-done.9 = f32[96,256]{1,0:T(8,128)S(1)} collective-permute-done((f32[96,256]{1,0:T(8,128)S(1)}, f32[96,256]{1,0:T(8,128)S(1)}, u32[]{:S(2)}, u32[]{:S(2)}) %collective-permute-start.9) | collective-permute-done | bytes 98336 | tf_op jit(solution)/shard_map/ppermute | solution.py:30
  125.5 1.8 collective-permute-start.10
  127.3 2.6 %collective-permute-done.10 = f32[96,256]{1,0:T(8,128)S(1)} collective-permute-done((f32[96,256]{1,0:T(8,128)S(1)}, f32[96,256]{1,0:T(8,128)S(1)}, u32[]{:S(2)}, u32[]{:S(2)}) %collective-permute-start.10) | collective-permute-done | bytes 98336 | tf_op jit(solution)/shard_map/ppermute | solution.py:30
  130.0 3.2 %collective-permute-start.11 = (f32[96,256]{1,0:T(8,128)S(1)}, f32[96,256]{1,0:T(8,128)S(1)}, u32[]{:S(2)}, u32[]{:S(2)}) collective-permute-start(f32[96,256]{1,0:T(8,128)S(1)} %add.139), channel_id=1, source_target_pairs={{0,9},{1,8},{2,11},{3,10},{4,13},{5,12},{6,15},{7,14},{8,1},{9,0},... | collective-permute-start | bytes 294920 | tf_op jit(solution)/shard_map/ppermute | solution.py:30
  133.7 4.3 %collective-permute-done.11 = f32[96,256]{1,0:T(8,128)S(1)} collective-permute-done((f32[96,256]{1,0:T(8,128)S(1)}, f32[96,256]{1,0:T(8,128)S(1)}, u32[]{:S(2)}, u32[]{:S(2)}) %collective-permute-start.11) | collective-permute-done | bytes 98336 | tf_op jit(solution)/shard_map/ppermute | solution.py:30
  138.0 5.4 %collective-permute-done.12 = bf16[56,16384]{1,0:T(8,128)(2,1)} collective-permute-done((bf16[56,16384]{1,0:T(8,128)(2,1)}, bf16[56,16384]{1,0:T(8,128)(2,1)}, u32[]{:S(2)}, u32[]{:S(2)}) %collective-permute-start.12) | collective-permute-done | bytes 1835040 | tf_op jit(solution)/shard_map/ppermute | solution.py:30
  143.5 4.3 %fusion.50 = f32[56,512]{1,0:T(8,128)S(1)} fusion(bf16[56,16384]{1,0:T(8,128)(2,1)} %collective-permute-done.12, bf16[16384,512]{1,0:T(8,128)(2,1)S(1)} %bitcast.13), kind=kOutput, calls=%fused_computation.77 | convolution fusion | flops 939524096 | bytes 18726912 | tf_op jit(solution)/shard_map/dot_general | solution.py:249
  147.9 1.2 collective-permute-done.13
  149.1 1.4 collective-permute-start.14
  150.5 2.6 %collective-permute-done.14 = f32[56,256]{1,0:T(8,128)S(1)} collective-permute-done((f32[56,256]{1,0:T(8,128)S(1)}, f32[56,256]{1,0:T(8,128)S(1)}, u32[]{:S(2)}, u32[]{:S(2)}) %collective-permute-start.14) | collective-permute-done | bytes 57376 | tf_op jit(solution)/shard_map/ppermute | solution.py:30
  153.1 1.7 collective-permute-start.15
  154.8 2.0 collective-permute-done.15
  156.8 3.0 %collective-permute-start.16 = (f32[56,256]{1,0:T(8,128)S(1)}, f32[56,256]{1,0:T(8,128)S(1)}, u32[]{:S(2)}, u32[]{:S(2)}) collective-permute-start(f32[56,256]{1,0:T(8,128)S(1)} %add.143), channel_id=1, source_target_pairs={{0,9},{1,8},{2,11},{3,10},{4,13},{5,12},{6,15},{7,14},{8,1},{9,0},... | collective-permute-start | bytes 172040 | tf_op jit(solution)/shard_map/ppermute | solution.py:30
  159.8 1.9 collective-permute-done.16
  161.7 1.7 collective-permute-start.17
  163.9 1.5 collective-permute-start.23
  165.5 3.1 %collective-permute-done = bf16[48,12288]{1,0:T(8,128)(2,1)S(1)} collective-permute-done((bf16[48,12288]{1,0:T(8,128)(2,1)S(1)}, bf16[48,12288]{1,0:T(8,128)(2,1)S(1)}, u32[]{:S(2)}, u32[]{:S(2)}) %collective-permute-start) | collective-permute-done | bytes 1179680 | tf_op jit(solution)/shard_map/ppermute | solution.py:30
  168.6 2.6 %fusion = f32[48,512]{1,0:T(8,128)S(1)} fusion(bf16[48,12288]{1,0:T(8,128)(2,1)S(1)} %collective-permute-done, bf16[16384,512]{1,0:T(8,128)(2,1)S(1)} %bitcast.13), kind=kOutput, calls=%fused_computation | convolution fusion | flops 603979776 | bytes 13860864 | tf_op jit(solution)/shard_map/dot_general | solution.py:249
  171.3 5.8 %collective-permute-done.18 = bf16[48,4096]{1,0:T(8,128)(2,1)S(1)} collective-permute-done((bf16[48,4096]{1,0:T(8,128)(2,1)S(1)}, bf16[48,4096]{1,0:T(8,128)(2,1)S(1)}, u32[]{:S(2)}, u32[]{:S(2)}) %collective-permute-start.18) | collective-permute-done | bytes 393248 | tf_op jit(solution)/shard_map/ppermute | solution.py:30
  178.0 1.2 collective-permute-done.19
  179.2 1.3 collective-permute-start.20
  181.1 1.5 collective-permute-start.25
  183.0 1.7 collective-permute-start.21
  185.5 1.2 fusion.4
  186.7 2.9 %collective-permute-start.22 = (f32[48,256]{1,0:T(8,128)S(1)}, f32[48,256]{1,0:T(8,128)S(1)}, u32[]{:S(2)}, u32[]{:S(2)}) collective-permute-start(f32[48,256]{1,0:T(8,128)S(1)} %add.148), channel_id=1, source_target_pairs={{0,9},{1,8},{2,11},{3,10},{4,13},{5,12},{6,15},{7,14},{8,1},{9,0},... | collective-permute-start | bytes 147464 | tf_op jit(solution)/shard_map/ppermute | solution.py:30
  189.6 2.2 %collective-permute-done.24 = bf16[24,6144]{1,0:T(8,128)(2,1)S(1)} collective-permute-done((bf16[24,6144]{1,0:T(8,128)(2,1)S(1)}, bf16[24,6144]{1,0:T(8,128)(2,1)S(1)}, u32[]{:S(2)}, u32[]{:S(2)}) %collective-permute-start.24) | collective-permute-done | bytes 294944 | tf_op jit(solution)/shard_map/ppermute | solution.py:30
  195.1 1.3 collective-permute-start.27
  196.4 2.0 collective-permute-done.27
  198.3 1.6 collective-permute-start.28
  200.1 1.5 collective-permute-done.28
  201.6 2.9 %collective-permute-start.29 = (f32[24,256]{1,0:T(8,128)S(1)}, f32[24,256]{1,0:T(8,128)S(1)}, u32[]{:S(2)}, u32[]{:S(2)}) collective-permute-start(f32[24,256]{1,0:T(8,128)S(1)} %add.154), channel_id=1, source_target_pairs={{0,9},{1,8},{2,11},{3,10},{4,13},{5,12},{6,15},{7,14},{8,1},{9,0},... | collective-permute-start | bytes 73736 | tf_op jit(solution)/shard_map/ppermute | solution.py:30
  205.0 1.0 collective-permute-done.29
  206.4 1.6 convolution_select_fusion._
  208.2 1.1 collective-permute-start.31
  209.6 2.1 collective-permute-done.31
  213.1 1.1 score_late.1
  (91 shorter events, 11.5 us)
Async XLA Ops:
  1.0 19.2 %collective-permute-start.1 = (bf16[32,4096]{1,0:T(8,128)(2,1)S(1)}, bf16[32,4096]{1,0:T(8,128)(2,1)S(1)}, u32[]{:S(2)}, u32[]{:S(2)}) collective-permute-start(bf16[32,4096]{1,0:T(8,128)(2,1)S(1)} %head.1), channel_id=1, source_target_pairs={{0,16},{1,17},{2,18},{3,19},{4,20},{5,21},{6,22},{7,23},{8,24},{9,... | collective-permute-start | bytes 786440 | tf_op jit(solution)/shard_map/ppermute | solution.py:30
  20.1 16.7 %copy-start.6 = (bf16[32,4096]{1,0:T(8,128)(2,1)}, bf16[32,4096]{1,0:T(8,128)(2,1)S(1)}, u32[]{:S(2)}) copy-start(bf16[32,4096]{1,0:T(8,128)(2,1)S(1)} %collective-permute-done.1) | copy-start | bytes 786436
  38.4 1.7 collective-permute-start.2
  38.4 71.9 %collective-permute-start.7 = (bf16[64,16384]{1,0:T(8,128)(2,1)}, bf16[64,16384]{1,0:T(8,128)(2,1)S(1)}, u32[]{:S(2)}, u32[]{:S(2)}) collective-permute-start(bf16[64,16384]{1,0:T(8,128)(2,1)} %slice.71), channel_id=1, source_target_pairs={{0,16},{1,17},{2,18},{3,19},{4,20},{5,21},{6,22},{7,23},{8,24},{9,... | collective-permute-start | bytes 6291464 | tf_op jit(solution)/shard_map/ppermute | solution.py:30
  41.1 7.7 %collective-permute-start.3 = (f32[224,256]{1,0:T(8,128)S(1)}, f32[224,256]{1,0:T(8,128)S(1)}, u32[]{:S(2)}, u32[]{:S(2)}) collective-permute-start(f32[224,256]{1,0:T(8,128)S(1)} %dynamic-slice_add_fusion), channel_id=1, source_target_pairs={{0,3},{1,2},{2,1},{3,0},{4,7},{5,6},{6,5},{7,4},{8,11},{9,10},{10,... | collective-permute-start | bytes 688136 | tf_op jit(solution)/shard_map/ppermute | solution.py:30
  48.8 7.4 %collective-permute-start.4 = (f32[224,256]{1,0:T(8,128)S(1)}, f32[224,256]{1,0:T(8,128)S(1)}, u32[]{:S(2)}, u32[]{:S(2)}) collective-permute-start(f32[224,256]{1,0:T(8,128)S(1)} %add.129), channel_id=1, source_target_pairs={{0,5},{1,4},{2,7},{3,6},{4,1},{5,0},{6,3},{7,2},{8,13},{9,12},{10,... | collective-permute-start | bytes 688136 | tf_op jit(solution)/shard_map/ppermute | solution.py:30
  56.2 13.5 %collective-permute-start.5 = (f32[224,256]{1,0:T(8,128)S(1)}, f32[224,256]{1,0:T(8,128)}, u32[]{:S(2)}, u32[]{:S(2)}) collective-permute-start(f32[224,256]{1,0:T(8,128)S(1)} %add.130), channel_id=1, source_target_pairs={{0,9},{1,8},{2,11},{3,10},{4,13},{5,12},{6,15},{7,14},{8,1},{9,0},... | collective-permute-start | bytes 688136 | tf_op jit(solution)/shard_map/ppermute | solution.py:30
  59.2 44.9 %collective-permute-start.6 = (bf16[32,12288]{1,0:T(8,128)(2,1)}, bf16[32,12288]{1,0:T(8,128)(2,1)}, u32[]{:S(2)}, u32[]{:S(2)}) collective-permute-start(bf16[32,12288]{1,0:T(8,128)(2,1)} %slice.70), channel_id=1, source_target_pairs={{0,16},{1,17},{2,18},{3,19},{4,20},{5,21},{6,22},{7,23},{8,24},{9,... | collective-permute-start | bytes 2359304 | tf_op jit(solution)/shard_map/ppermute | solution.py:30
  59.7 83.7 %collective-permute-start.12 = (bf16[56,16384]{1,0:T(8,128)(2,1)}, bf16[56,16384]{1,0:T(8,128)(2,1)}, u32[]{:S(2)}, u32[]{:S(2)}) collective-permute-start(bf16[56,16384]{1,0:T(8,128)(2,1)} %slice.73), channel_id=1, source_target_pairs={{0,16},{1,17},{2,18},{3,19},{4,20},{5,21},{6,22},{7,23},{8,24},{9,... | collective-permute-start | bytes 5505032 | tf_op jit(solution)/shard_map/ppermute | solution.py:30
  104.1 39.3 %slice-start = ((s8[16777216]{0:T(1024)(128)(4,1)}), s8[4194304]{0:T(1024)(128)(4,1)S(1)}, s32[]{:S(2)}) async-start(s8[16777216]{0:T(1024)(128)(4,1)} %bitcast.12), calls=%async_computation | async-start | bytes 8388608
  104.1 39.3 %slice-start.1 = ((s8[16777216]{0:T(1024)(128)(4,1)}), s8[4194304]{0:T(1024)(128)(4,1)S(1)}, s32[]{:S(2)}) async-start(s8[16777216]{0:T(1024)(128)(4,1)} %bitcast.12), calls=%async_computation.1 | async-start | bytes 8388608
  110.3 33.1 %slice-start.2 = ((s8[16777216]{0:T(1024)(128)(4,1)}), s8[4194304]{0:T(1024)(128)(4,1)S(1)}, s32[]{:S(2)}) async-start(s8[16777216]{0:T(1024)(128)(4,1)} %bitcast.12), calls=%async_computation.2 | async-start | bytes 8388608
  110.3 33.1 %slice-start.3 = ((s8[16777216]{0:T(1024)(128)(4,1)}), s8[4194304]{0:T(1024)(128)(4,1)S(1)}, s32[]{:S(2)}) async-start(s8[16777216]{0:T(1024)(128)(4,1)} %bitcast.12), calls=%async_computation.3 | async-start | bytes 8388608
  119.3 1.4 collective-permute-start.8
  120.7 4.8 %collective-permute-start.9 = (f32[96,256]{1,0:T(8,128)S(1)}, f32[96,256]{1,0:T(8,128)S(1)}, u32[]{:S(2)}, u32[]{:S(2)}) collective-permute-start(f32[96,256]{1,0:T(8,128)S(1)} %fusion.43), channel_id=1, source_target_pairs={{0,3},{1,2},{2,1},{3,0},{4,7},{5,6},{6,5},{7,4},{8,11},{9,10},{10,... | collective-permute-start | bytes 294920 | tf_op jit(solution)/shard_map/ppermute | solution.py:30
  125.5 4.4 %collective-permute-start.10 = (f32[96,256]{1,0:T(8,128)S(1)}, f32[96,256]{1,0:T(8,128)S(1)}, u32[]{:S(2)}, u32[]{:S(2)}) collective-permute-start(f32[96,256]{1,0:T(8,128)S(1)} %add.138), channel_id=1, source_target_pairs={{0,5},{1,4},{2,7},{3,6},{4,1},{5,0},{6,3},{7,2},{8,13},{9,12},{10,... | collective-permute-start | bytes 294920 | tf_op jit(solution)/shard_map/ppermute | solution.py:30
  130.0 8.0 %collective-permute-start.11 = (f32[96,256]{1,0:T(8,128)S(1)}, f32[96,256]{1,0:T(8,128)S(1)}, u32[]{:S(2)}, u32[]{:S(2)}) collective-permute-start(f32[96,256]{1,0:T(8,128)S(1)} %add.139), channel_id=1, source_target_pairs={{0,9},{1,8},{2,11},{3,10},{4,13},{5,12},{6,15},{7,14},{8,1},{9,0},... | collective-permute-start | bytes 294920 | tf_op jit(solution)/shard_map/ppermute | solution.py:30
  133.2 35.4 %collective-permute-start = (bf16[48,12288]{1,0:T(8,128)(2,1)S(1)}, bf16[48,12288]{1,0:T(8,128)(2,1)S(1)}, u32[]{:S(2)}, u32[]{:S(2)}) collective-permute-start(bf16[48,12288]{1,0:T(8,128)(2,1)S(1)} %slice.72), channel_id=1, source_target_pairs={{0,16},{1,17},{2,18},{3,19},{4,20},{5,21},{6,22},{7,23},{8,24},{9,... | collective-permute-start | bytes 3538952 | tf_op jit(solution)/shard_map/ppermute | solution.py:30
  138.0 25.4 %copy-start.2 = (bf16[48,4096]{1,0:T(8,128)(2,1)S(1)}, bf16[48,4096]{1,0:T(8,128)(2,1)}, u32[]{:S(2)}) copy-start(bf16[48,4096]{1,0:T(8,128)(2,1)} %slice.74) | copy-start | bytes 1179652
  138.0 25.9 %copy-start.1 = (bf16[24,8192]{1,0:T(8,128)(2,1)S(1)}, bf16[24,8192]{1,0:T(8,128)(2,1)}, u32[]{:S(2)}) copy-start(bf16[24,8192]{1,0:T(8,128)(2,1)} %slice.75) | copy-start | bytes 1179652
  147.8 1.3 collective-permute-start.13
  149.1 3.9 %collective-permute-start.14 = (f32[56,256]{1,0:T(8,128)S(1)}, f32[56,256]{1,0:T(8,128)S(1)}, u32[]{:S(2)}, u32[]{:S(2)}) collective-permute-start(f32[56,256]{1,0:T(8,128)S(1)} %dynamic-slice_add_fusion.1), channel_id=1, source_target_pairs={{0,3},{1,2},{2,1},{3,0},{4,7},{5,6},{6,5},{7,4},{8,11},{9,10},{10,... | collective-permute-start | bytes 172040 | tf_op jit(solution)/shard_map/ppermute | solution.py:30
  153.1 3.7 %collective-permute-start.15 = (f32[56,256]{1,0:T(8,128)S(1)}, f32[56,256]{1,0:T(8,128)S(1)}, u32[]{:S(2)}, u32[]{:S(2)}) collective-permute-start(f32[56,256]{1,0:T(8,128)S(1)} %add.142), channel_id=1, source_target_pairs={{0,5},{1,4},{2,7},{3,6},{4,1},{5,0},{6,3},{7,2},{8,13},{9,12},{10,... | collective-permute-start | bytes 172040 | tf_op jit(solution)/shard_map/ppermute | solution.py:30
  156.8 4.9 %collective-permute-start.16 = (f32[56,256]{1,0:T(8,128)S(1)}, f32[56,256]{1,0:T(8,128)S(1)}, u32[]{:S(2)}, u32[]{:S(2)}) collective-permute-start(f32[56,256]{1,0:T(8,128)S(1)} %add.143), channel_id=1, source_target_pairs={{0,9},{1,8},{2,11},{3,10},{4,13},{5,12},{6,15},{7,14},{8,1},{9,0},... | collective-permute-start | bytes 172040 | tf_op jit(solution)/shard_map/ppermute | solution.py:30
  161.7 3.8 %collective-permute-start.17 = (bf16[376,256]{1,0:T(8,128)(2,1)S(1)}, bf16[376,256]{1,0:T(8,128)(2,1)S(1)}, u32[]{:S(2)}, u32[]{:S(2)}) collective-permute-start(bf16[376,256]{1,0:T(8,128)(2,1)S(1)} %pad_maximum_fusion.3), channel_id=1, source_target_pairs={{0,1},{1,0},{2,3},{3,2},{4,5},{5,4},{6,7},{7,6},{8,9},{9,8},{10,11... | collective-permute-start | bytes 577544 | tf_op jit(solution)/shard_map/ppermute | solution.py:30
  163.4 13.6 %collective-permute-start.18 = (bf16[48,4096]{1,0:T(8,128)(2,1)S(1)}, bf16[48,4096]{1,0:T(8,128)(2,1)S(1)}, u32[]{:S(2)}, u32[]{:S(2)}) collective-permute-start(bf16[48,4096]{1,0:T(8,128)(2,1)S(1)} %copy-done.2), channel_id=1, source_target_pairs={{0,16},{1,17},{2,18},{3,19},{4,20},{5,21},{6,22},{7,23},{8,24},{9,... | collective-permute-start | bytes 1179656 | tf_op jit(solution)/shard_map/ppermute | solution.py:30
  163.9 21.5 %collective-permute-start.23 = (bf16[24,8192]{1,0:T(8,128)(2,1)S(1)}, bf16[24,8192]{1,0:T(8,128)(2,1)S(1)}, u32[]{:S(2)}, u32[]{:S(2)}) collective-permute-start(bf16[24,8192]{1,0:T(8,128)(2,1)S(1)} %copy-done.1), channel_id=1, source_target_pairs={{0,16},{1,17},{2,18},{3,19},{4,20},{5,21},{6,22},{7,23},{8,24},{9,... | collective-permute-start | bytes 1179656 | tf_op jit(solution)/shard_map/ppermute | solution.py:30
  171.3 9.3 %copy-start.3 = (bf16[24,6144]{1,0:T(8,128)(2,1)S(1)}, bf16[24,6144]{1,0:T(8,128)(2,1)}, u32[]{:S(2)}) copy-start(bf16[24,6144]{1,0:T(8,128)(2,1)} %slice.76) | copy-start | bytes 884740
  171.3 9.8 %copy-start.4 = (bf16[24,2048]{1,0:T(8,128)(2,1)S(1)}, bf16[24,2048]{1,0:T(8,128)(2,1)}, u32[]{:S(2)}) copy-start(bf16[24,2048]{1,0:T(8,128)(2,1)} %slice.77) | copy-start | bytes 294916
  177.9 1.3 collective-permute-start.19
  179.2 3.8 %collective-permute-start.20 = (f32[48,256]{1,0:T(8,128)S(1)}, f32[48,256]{1,0:T(8,128)S(1)}, u32[]{:S(2)}, u32[]{:S(2)}) collective-permute-start(f32[48,256]{1,0:T(8,128)S(1)} %dynamic-slice_add_fusion.2), channel_id=1, source_target_pairs={{0,3},{1,2},{2,1},{3,0},{4,7},{5,6},{6,5},{7,4},{8,11},{9,10},{10,... | collective-permute-start | bytes 147464 | tf_op jit(solution)/shard_map/ppermute | solution.py:30
  180.5 11.2 %collective-permute-start.24 = (bf16[24,6144]{1,0:T(8,128)(2,1)S(1)}, bf16[24,6144]{1,0:T(8,128)(2,1)S(1)}, u32[]{:S(2)}, u32[]{:S(2)}) collective-permute-start(bf16[24,6144]{1,0:T(8,128)(2,1)S(1)} %copy-done.3), channel_id=1, source_target_pairs={{0,16},{1,17},{2,18},{3,19},{4,20},{5,21},{6,22},{7,23},{8,24},{9,... | collective-permute-start | bytes 884744 | tf_op jit(solution)/shard_map/ppermute | solution.py:30
  181.1 12.4 %collective-permute-start.25 = (bf16[24,2048]{1,0:T(8,128)(2,1)S(1)}, bf16[24,2048]{1,0:T(8,128)(2,1)S(1)}, u32[]{:S(2)}, u32[]{:S(2)}) collective-permute-start(bf16[24,2048]{1,0:T(8,128)(2,1)S(1)} %copy-done.4), channel_id=1, source_target_pairs={{0,16},{1,17},{2,18},{3,19},{4,20},{5,21},{6,22},{7,23},{8,24},{9,... | collective-permute-start | bytes 294920 | tf_op jit(solution)/shard_map/ppermute | solution.py:30
  183.0 3.7 %collective-permute-start.21 = (f32[48,256]{1,0:T(8,128)S(1)}, f32[48,256]{1,0:T(8,128)S(1)}, u32[]{:S(2)}, u32[]{:S(2)}) collective-permute-start(f32[48,256]{1,0:T(8,128)S(1)} %add.147), channel_id=1, source_target_pairs={{0,5},{1,4},{2,7},{3,6},{4,1},{5,0},{6,3},{7,2},{8,13},{9,12},{10,... | collective-permute-start | bytes 147464 | tf_op jit(solution)/shard_map/ppermute | solution.py:30
  186.7 9.7 %copy-start.5 = (s32[448]{0:T(512)S(1)}, s32[448]{0:T(512)}, u32[]{:S(2)}) copy-start(s32[448]{0:T(512)} %param.9) | copy-start | bytes 5380
  186.7 13.3 %copy-start = (bf16[512,1024]{1,0:T(8,128)(2,1)S(1)}, bf16[512,1024]{1,0:T(8,128)(2,1)}, u32[]{:S(2)}) copy-start(bf16[512,1024]{1,0:T(8,128)(2,1)} %param.8) | copy-start | bytes 3145732
  186.7 6.0 %collective-permute-start.22 = (f32[48,256]{1,0:T(8,128)S(1)}, f32[48,256]{1,0:T(8,128)S(1)}, u32[]{:S(2)}, u32[]{:S(2)}) collective-permute-start(f32[48,256]{1,0:T(8,128)S(1)} %add.148), channel_id=1, source_target_pairs={{0,9},{1,8},{2,11},{3,10},{4,13},{5,12},{6,15},{7,14},{8,1},{9,0},... | collective-permute-start | bytes 147464 | tf_op jit(solution)/shard_map/ppermute | solution.py:30
  193.8 1.3 collective-permute-start.26
  193.9 12.2 %collective-permute-start.30 = (bf16[376,512]{1,0:T(8,128)(2,1)S(1)}, bf16[376,512]{1,0:T(8,128)(2,1)S(1)}, u32[]{:S(2)}, u32[]{:S(2)}) collective-permute-start(bf16[376,512]{1,0:T(8,128)(2,1)S(1)} %pad_maximum_fusion.1), channel_id=1, source_target_pairs={{0,17},{1,16},{2,19},{3,18},{4,21},{5,20},{6,23},{7,22},{8,25},{9,... | collective-permute-start | bytes 1155080 | tf_op jit(solution)/shard_map/ppermute | solution.py:30
  195.1 3.3 %collective-permute-start.27 = (f32[24,256]{1,0:T(8,128)S(1)}, f32[24,256]{1,0:T(8,128)S(1)}, u32[]{:S(2)}, u32[]{:S(2)}) collective-permute-start(f32[24,256]{1,0:T(8,128)S(1)} %dynamic-slice_add_fusion.3), channel_id=1, source_target_pairs={{0,3},{1,2},{2,1},{3,0},{4,7},{5,6},{6,5},{7,4},{8,11},{9,10},{10,... | collective-permute-start | bytes 73736 | tf_op jit(solution)/shard_map/ppermute | solution.py:30
  198.3 3.3 %collective-permute-start.28 = (f32[24,256]{1,0:T(8,128)S(1)}, f32[24,256]{1,0:T(8,128)S(1)}, u32[]{:S(2)}, u32[]{:S(2)}) collective-permute-start(f32[24,256]{1,0:T(8,128)S(1)} %add.153), channel_id=1, source_target_pairs={{0,5},{1,4},{2,7},{3,6},{4,1},{5,0},{6,3},{7,2},{8,13},{9,12},{10,... | collective-permute-start | bytes 73736 | tf_op jit(solution)/shard_map/ppermute | solution.py:30
  201.6 4.5 %collective-permute-start.29 = (f32[24,256]{1,0:T(8,128)S(1)}, f32[24,256]{1,0:T(8,128)S(1)}, u32[]{:S(2)}, u32[]{:S(2)}) collective-permute-start(f32[24,256]{1,0:T(8,128)S(1)} %add.154), channel_id=1, source_target_pairs={{0,9},{1,8},{2,11},{3,10},{4,13},{5,12},{6,15},{7,14},{8,1},{9,0},... | collective-permute-start | bytes 73736 | tf_op jit(solution)/shard_map/ppermute | solution.py:30
  208.2 3.4 %collective-permute-start.31 = (bf16[72,256]{1,0:T(8,128)(2,1)S(1)}, bf16[72,256]{1,0:T(8,128)(2,1)S(1)}, u32[]{:S(2)}, u32[]{:S(2)}) collective-permute-start(bf16[72,256]{1,0:T(8,128)(2,1)S(1)} %pad_maximum_fusion.5), channel_id=1, source_target_pairs={{0,17},{1,16},{2,19},{3,18},{4,21},{5,20},{6,23},{7,22},{8,25},{9,... | collective-permute-start | bytes 110600 | tf_op jit(solution)/shard_map/ppermute | solution.py:30
  211.7 1.4 collective-permute-start.32

commit v7 on v6

--- a/solution.py
+++ b/solution.py
@@ -64,17 +64,21 @@
     return place(row, blocks)
 
 
-def partial_scores(early, store, rows, tail):
+def partial_scores(early, late, store, rows, tail):
     row_groups, width = len(early), early[0].shape[1]
+    half = width // 2
     values = []
     for a in range(row_groups):
-        total = 0.0
+        left, right = [], []
         for flip in range(row_groups):
             end = ((a ^ flip) + 1) * rows
             if a ^ flip != row_groups - 1:
-                total += product(
-                    early[flip][end - tail : end], store[:, flip * width : (flip + 1) * width]
-                )
+                left.append(early[flip][end - tail : end])
+                right.append(store[:, flip * width : (flip + 1) * width])
+            else:
+                left.append(late[flip * tail : (flip + 1) * tail])
+                right.append(store[:, flip * width : flip * width + half])
+        total = product(jnp.concatenate(left, 1), jnp.concatenate(right, 1))
         values.append(total)
     return jnp.concatenate(values, 0)
 
@@ -86,20 +90,16 @@
 
 
 def score_late_kernel(
-    row_groups, rows, row_ref, late_ref, pair_ref, store_ref, partial_ref, index_ref, _, out_ref,
-    held, sent
+    row_groups, rows, row_ref, pair_ref, store_ref, partial_ref, index_ref, _, out_ref, held, sent
 ):
-    tail, half = late_ref.shape[0] // row_groups, late_ref.shape[1]
+    tail, half = pair_ref.shape[0] // row_groups, pair_ref.shape[1]
     copies = []
     for a in range(row_groups):
         flip = (row_groups - 1) ^ a
-        spot, column = flip * tail, 2 * flip * half
+        spot = flip * tail
         value = partial_ref[a * tail : (a + 1) * tail, :]
         value += product(
-            late_ref[spot : spot + tail, :], store_ref[:, column : column + half]
-        )
-        value += product(
-            pair_ref[spot : spot + tail, :], store_ref[:, column + half : column + 2 * half]
+            pair_ref[spot : spot + tail, :], store_ref[:, flip * half : (flip + 1) * half]
         )
         block = row_ref[0] ^ a
         index = index_ref[pl.ds(pl.multiple_of(block * tail, 8), tail), :]
@@ -118,24 +118,24 @@
         copy.wait()
 
 
-def score_late(row, late, pair, store, partial_value, index, value, row_groups):
+def score_late(row, pair, store, partial_value, index, value, row_groups):
     rows = value.shape[0] // row_groups
     vmem = pl.BlockSpec(memory_space=pltpu.VMEM)
     return pl.pallas_call(
         functools.partial(score_late_kernel, row_groups, rows),
         out_shape=jax.ShapeDtypeStruct(value.shape, value.dtype),
         in_specs=[pl.BlockSpec(memory_space=pltpu.SMEM)]
-        + [vmem] * 5
+        + [vmem] * 4
         + [pl.BlockSpec(memory_space=pl.ANY)],
         out_specs=pl.BlockSpec(memory_space=pl.ANY),
         scratch_shapes=[
             pltpu.VMEM(partial_value.shape, jnp.float32),
             pltpu.SemaphoreType.DMA((row_groups,)),
         ],
-        input_output_aliases={6: 0},
+        input_output_aliases={5: 0},
         compiler_params=pltpu.CompilerParams(vmem_limit_bytes=16 << 20),
         name="score_late",
-    )(row.astype(jnp.int32).reshape(1), late, pair, store, partial_value, index, value)
+    )(row.astype(jnp.int32).reshape(1), pair, store, partial_value, index, value)
 
 
 def dot_kernel(left_ref, right_ref, out_ref):
@@ -212,8 +212,8 @@
         (0, lead, (0, 2 * unit, features)),
         (lead, ends[0], (0, features)),
         (ends[0], ends[1], (0, features)),
-        (ends[1], ends[2], (0, 6 * unit, features)),
-        (ends[2], ends[3], (0, 4 * unit, 7 * unit, features)),
+        (ends[1], ends[2], (0, 7 * unit, features)),
+        (ends[2], ends[3], (0, 4 * unit, 7 * unit + unit // 2, features)),
     ]
     cuts = [
         (r0, r1, f0, f1) for r0, r1, marks in plan for f0, f1 in zip(marks[:-1], marks[1:])
@@ -294,13 +294,14 @@
     others = [after(part, late) for part in early[1:]]
     whitened = arrange(row, [early[0]] + others, rows, tail)
     value = masked_product(whitened, store, shifted)
-    others = [after(part, value) for part in early]
-    partial_value = partial_scores(others, store, rows, tail)
     late = jnp.concatenate([middle, late], 0)
     others = [cross(late, flip) for flip in range(1, row_groups)]
     late = jnp.concatenate([late] + others, 0)
     pair = swap(after(late, value), row_flip=0, feat_flip=1)
-    return score_late(row, late, pair, store, partial_value, index, value, row_groups)
+    others = [after(part, value) for part in early]
+    partial_value = partial_scores(others, late, store, rows, tail)
+    rest = jnp.concatenate(order[1::2], 1)
+    return score_late(row, pair, rest, partial_value, index, value, row_groups)
 
 
 def plain(slab_grads, basis, eigenvalues, store_rows, slab_index, *, row_groups, feat_groups):

time: 215 us -> 213 us (level)
  transfers between devices with their start and end apart: 33 -> 33, of which waited for: 27 -> 26; matrix products, arithmetic and copies ran while one was open for 22% -> 24% of each run, Pallas kernels for 0% -> 0%
where the time goes in v7:
time: 213 us; the launch traced here: 212 us
  waiting for transfers between devices  96.9 us (45%)
  starting transfers between devices  43.1 us (20%)
  matrix products  30.8 us (14%)
  Pallas kernels  18.6 us (9%)
  local copies, waits for them, and re-layouts  17.6 us (8%)
  other arithmetic  4.19 us (2%)
    ppermute x33, waiting for transfers between devices, exchange(): return lax.ppermute(value, ('rows', 'feat'), pairs)  96.9 us
    ppermute x33, starting transfers between devices, exchange(): return lax.ppermute(value, ('rows', 'feat'), pairs)  43.1 us
    dot_general x9, matrix products, project(): jnp.dot(after(moved[i], *needed), basis[f0:f1], preferred_element_type=jn...  28.5 us
    pallas_call x1, Pallas kernels, dot(): pl.pallas_call(dot_kernel, out_shape=jax.ShapeDtypeStruct((rows, columns)...  16.7 us
    slice x8, local copies, waits for them, and re-layouts, shards(): pieces.append(head(ready, r1, f1) if i == 0 else ready[r0:r1, f0:f1])  15.3 us
  transfers between devices with their start and end apart: 33, of which 26 were waited for; matrix products, arithmetic and copies ran while one was open for 24% of the time, Pallas kernels for 0%

profile of v7, /device:TPU:0, one launch (start us, length us, event | category | flops | bytes accessed | tf_op | source)
XLA Modules:
  0.0 211.7 jit_solution(6321736349877444375)
XLA Ops:
  1.0 3.0 %collective-permute-start.1 = (bf16[32,4096]{1,0:T(8,128)(2,1)S(1)}, bf16[32,4096]{1,0:T(8,128)(2,1)S(1)}, u32[]{:S(2)}, u32[]{:S(2)}) collective-permute-start(bf16[32,4096]{1,0:T(8,128)(2,1)S(1)} %head.1), channel_id=1, source_target_pairs={{0,16},{1,17},{2,18},{3,19},{4,20},{5,21},{6,22},{7,23},{8,24},{9,... | collective-permute-start | bytes 786440 | tf_op jit(solution)/shard_map/ppermute | solution.py:30
  4.0 2.1 slice.70
  6.1 3.1 %slice.71 = bf16[64,16384]{1,0:T(8,128)(2,1)} slice(bf16[224,16384]{1,0:T(8,128)(2,1)} %left_ref), slice={[32:96], [0:16384]} | slice | bytes 4194304 | tf_op jit(solution)/shard_map/slice | solution.py:226
  9.1 2.9 %slice.73 = bf16[56,16384]{1,0:T(8,128)(2,1)} slice(bf16[224,16384]{1,0:T(8,128)(2,1)} %left_ref), slice={[96:152], [0:16384]} | slice | bytes 3670016 | tf_op jit(solution)/shard_map/slice | solution.py:226
  12.0 1.4 slice.72
  13.4 1.8 slice.75
  15.2 1.7 slice.76
  16.9 1.6 slice.74
  19.3 16.7 %dot.1 = f32[224,512]{1,0:T(8,128)} custom-call(bf16[224,16384]{1,0:T(8,128)(2,1)} %left_ref, bf16[16384,512]{1,0:T(8,128)(2,1)} %right_ref.1), custom_call_target="tpu_custom_call" | custom-call | flops 3758096384 | bytes 24576000 | tf_op jit(solution)/shard_map/dot/pallas_call | solution.py:176
  36.0 1.7 constant_dynamic-slice_fusion.7
  37.7 1.8 collective-permute-done.2
  39.5 1.1 dynamic-slice_add_fusion
  40.6 1.3 collective-permute-start.3
  41.9 6.3 %collective-permute-done.3 = f32[224,256]{1,0:T(8,128)S(1)} collective-permute-done((f32[224,256]{1,0:T(8,128)S(1)}, f32[224,256]{1,0:T(8,128)S(1)}, u32[]{:S(2)}, u32[]{:S(2)}) %collective-permute-start.3) | collective-permute-done | bytes 229408 | tf_op jit(solution)/shard_map/ppermute | solution.py:30
  48.3 1.7 collective-permute-start.4
  50.0 5.7 %collective-permute-done.4 = f32[224,256]{1,0:T(8,128)S(1)} collective-permute-done((f32[224,256]{1,0:T(8,128)S(1)}, f32[224,256]{1,0:T(8,128)S(1)}, u32[]{:S(2)}, u32[]{:S(2)}) %collective-permute-start.4) | collective-permute-done | bytes 229408 | tf_op jit(solution)/shard_map/ppermute | solution.py:30
  56.4 2.9 %collective-permute-start.5 = (f32[224,256]{1,0:T(8,128)}, f32[224,256]{1,0:T(8,128)}, u32[]{:S(2)}, u32[]{:S(2)}) collective-permute-start(f32[224,256]{1,0:T(8,128)} %add.130), channel_id=1, source_target_pairs={{0,9},{1,8},{2,11},{3,10},{4,13},{5,12},{6,15},{7,14},{8,1},{9,0},... | collective-permute-start | bytes 688136 | tf_op jit(solution)/shard_map/ppermute | solution.py:30
  59.8 1.5 collective-permute-start.12
  62.1 8.0 %collective-permute-done.5 = f32[224,256]{1,0:T(8,128)} collective-permute-done((f32[224,256]{1,0:T(8,128)}, f32[224,256]{1,0:T(8,128)}, u32[]{:S(2)}, u32[]{:S(2)}) %collective-permute-start.5) | collective-permute-done | bytes 229408 | tf_op jit(solution)/shard_map/ppermute | solution.py:30
  70.1 1.1 divide_convert_fusion
  71.1 3.1 %fusion.8 = f32[32,512]{1,0:T(8,128)S(1)} fusion(bf16[32,4096]{1,0:T(8,128)(2,1)} %copy-done.5, bf16[16384,512]{1,0:T(8,128)(2,1)} %right_ref.1), kind=kOutput, calls=%fused_computation.8 | convolution fusion | flops 134217728 | bytes 4521984 | tf_op jit(solution)/shard_map/dot_general | solution.py:249
  74.2 29.1 %collective-permute-done.6 = bf16[32,12288]{1,0:T(8,128)(2,1)} collective-permute-done((bf16[32,12288]{1,0:T(8,128)(2,1)}, bf16[32,12288]{1,0:T(8,128)(2,1)}, u32[]{:S(2)}, u32[]{:S(2)}) %collective-permute-start.6) | collective-permute-done | bytes 786464 | tf_op jit(solution)/shard_map/ppermute | solution.py:30
  103.4 6.2 %fusion.15 = f32[32,512]{1,0:T(8,128)S(1)} fusion(f32[32,512]{1,0:T(8,128)S(1)} %fusion.8, bf16[32,12288]{1,0:T(8,128)(2,1)} %collective-permute-done.6, bf16[16384,512]{1,0:T(8,128)(2,1)} %right_ref.1), kind=kOutput, calls=%fused_computation.14 | convolution fusion | flops 402669568 | bytes 13500416 | tf_op jit(solution)/shard_map/dot_general | solution.py:249
  109.6 8.9 %fusion.60 = f32[64,512]{1,0:T(8,128)S(1)} fusion(bf16[64,16384]{1,0:T(8,128)(2,1)S(1)} %collective-permute-done.7, bf16[16384,512]{1,0:T(8,128)(2,1)} %right_ref.1), kind=kOutput, calls=%fused_computation.90 | convolution fusion | flops 1073741824 | bytes 19005440 | tf_op jit(solution)/shard_map/dot_general | solution.py:249
  118.6 1.3 collective-permute-done.8
  119.9 1.3 collective-permute-start.9
  121.3 3.5 %collective-permute-done.9 = f32[96,256]{1,0:T(8,128)S(1)} collective-permute-done((f32[96,256]{1,0:T(8,128)S(1)}, f32[96,256]{1,0:T(8,128)S(1)}, u32[]{:S(2)}, u32[]{:S(2)}) %collective-permute-start.9) | collective-permute-done | bytes 98336 | tf_op jit(solution)/shard_map/ppermute | solution.py:30
  124.8 1.8 collective-permute-start.10
  126.6 2.6 %collective-permute-done.10 = f32[96,256]{1,0:T(8,128)S(1)} collective-permute-done((f32[96,256]{1,0:T(8,128)S(1)}, f32[96,256]{1,0:T(8,128)S(1)}, u32[]{:S(2)}, u32[]{:S(2)}) %collective-permute-start.10) | collective-permute-done | bytes 98336 | tf_op jit(solution)/shard_map/ppermute | solution.py:30
  129.2 3.2 %collective-permute-start.11 = (f32[96,256]{1,0:T(8,128)S(1)}, f32[96,256]{1,0:T(8,128)S(1)}, u32[]{:S(2)}, u32[]{:S(2)}) collective-permute-start(f32[96,256]{1,0:T(8,128)S(1)} %add.139), channel_id=1, source_target_pairs={{0,9},{1,8},{2,11},{3,10},{4,13},{5,12},{6,15},{7,14},{8,1},{9,0},... | collective-permute-start | bytes 294920 | tf_op jit(solution)/shard_map/ppermute | solution.py:30
  133.0 4.3 %collective-permute-done.11 = f32[96,256]{1,0:T(8,128)S(1)} collective-permute-done((f32[96,256]{1,0:T(8,128)S(1)}, f32[96,256]{1,0:T(8,128)S(1)}, u32[]{:S(2)}, u32[]{:S(2)}) %collective-permute-start.11) | collective-permute-done | bytes 98336 | tf_op jit(solution)/shard_map/ppermute | solution.py:30
  137.3 5.4 %collective-permute-done.12 = bf16[56,16384]{1,0:T(8,128)(2,1)} collective-permute-done((bf16[56,16384]{1,0:T(8,128)(2,1)}, bf16[56,16384]{1,0:T(8,128)(2,1)}, u32[]{:S(2)}, u32[]{:S(2)}) %collective-permute-start.12) | collective-permute-done | bytes 1835040 | tf_op jit(solution)/shard_map/ppermute | solution.py:30
  142.7 4.3 %fusion.61 = f32[56,512]{1,0:T(8,128)S(1)} fusion(bf16[56,16384]{1,0:T(8,128)(2,1)} %collective-permute-done.12, bf16[16384,512]{1,0:T(8,128)(2,1)S(1)} %bitcast.13), kind=kOutput, calls=%fused_computation.91 | convolution fusion | flops 939524096 | bytes 18726912 | tf_op jit(solution)/shard_map/dot_general | solution.py:249
  147.1 1.2 collective-permute-done.13
  148.4 1.4 collective-permute-start.14
  149.7 2.6 %collective-permute-done.14 = f32[56,256]{1,0:T(8,128)S(1)} collective-permute-done((f32[56,256]{1,0:T(8,128)S(1)}, f32[56,256]{1,0:T(8,128)S(1)}, u32[]{:S(2)}, u32[]{:S(2)}) %collective-permute-start.14) | collective-permute-done | bytes 57376 | tf_op jit(solution)/shard_map/ppermute | solution.py:30
  152.3 1.7 collective-permute-start.15
  154.0 2.0 collective-permute-done.15
  156.0 3.0 %collective-permute-start.16 = (f32[56,256]{1,0:T(8,128)S(1)}, f32[56,256]{1,0:T(8,128)S(1)}, u32[]{:S(2)}, u32[]{:S(2)}) collective-permute-start(f32[56,256]{1,0:T(8,128)S(1)} %add.143), channel_id=1, source_target_pairs={{0,9},{1,8},{2,11},{3,10},{4,13},{5,12},{6,15},{7,14},{8,1},{9,0},... | collective-permute-start | bytes 172040 | tf_op jit(solution)/shard_map/ppermute | solution.py:30
  159.0 1.9 collective-permute-done.16
  160.9 1.7 collective-permute-start.17
  163.2 1.5 collective-permute-start.23
  164.7 7.4 %collective-permute-done = bf16[48,14336]{1,0:T(8,128)(2,1)S(1)} collective-permute-done((bf16[48,14336]{1,0:T(8,128)(2,1)S(1)}, bf16[48,14336]{1,0:T(8,128)(2,1)S(1)}, u32[]{:S(2)}, u32[]{:S(2)}) %collective-permute-start) | collective-permute-done | bytes 1376288 | tf_op jit(solution)/shard_map/ppermute | solution.py:30
  172.1 3.0 %fusion = f32[48,512]{1,0:T(8,128)S(1)} fusion(bf16[48,14336]{1,0:T(8,128)(2,1)S(1)} %collective-permute-done, bf16[16384,512]{1,0:T(8,128)(2,1)S(1)} %bitcast.13), kind=kOutput, calls=%fused_computation | convolution fusion | flops 704643072 | bytes 16154624 | tf_op jit(solution)/shard_map/dot_general | solution.py:249
  175.1 1.2 collective-permute-done.18
  176.9 1.2 collective-permute-done.19
  178.1 1.3 collective-permute-start.20
  180.0 1.5 collective-permute-start.25
  181.9 1.7 collective-permute-start.21
  183.6 1.1 collective-permute-done.23
  184.7 1.2 fusion.4
  186.0 2.5 %collective-permute-start.22 = (f32[48,256]{1,0:T(8,128)S(1)}, f32[48,256]{1,0:T(8,128)S(1)}, u32[]{:S(2)}, u32[]{:S(2)}) collective-permute-start(f32[48,256]{1,0:T(8,128)S(1)} %add.148), channel_id=1, source_target_pairs={{0,9},{1,8},{2,11},{3,10},{4,13},{5,12},{6,15},{7,14},{8,1},{9,0},... | collective-permute-start | bytes 147464 | tf_op jit(solution)/shard_map/ppermute | solution.py:30
  188.5 3.6 %collective-permute-done.24 = bf16[24,7168]{1,0:T(8,128)(2,1)S(1)} collective-permute-done((bf16[24,7168]{1,0:T(8,128)(2,1)S(1)}, bf16[24,7168]{1,0:T(8,128)(2,1)S(1)}, u32[]{:S(2)}, u32[]{:S(2)}) %collective-permute-start.24) | collective-permute-done | bytes 344096 | tf_op jit(solution)/shard_map/ppermute | solution.py:30
  192.1 1.1 fusion.18
  193.7 1.1 collective-permute-done.26
  194.7 1.3 collective-permute-start.27
  196.0 2.0 collective-permute-done.27
  198.0 1.6 collective-permute-start.28
  199.8 1.5 collective-permute-done.28
  201.2 2.9 %collective-permute-start.29 = (f32[24,256]{1,0:T(8,128)S(1)}, f32[24,256]{1,0:T(8,128)S(1)}, u32[]{:S(2)}, u32[]{:S(2)}) collective-permute-start(f32[24,256]{1,0:T(8,128)S(1)} %add.154), channel_id=1, source_target_pairs={{0,9},{1,8},{2,11},{3,10},{4,13},{5,12},{6,15},{7,14},{8,1},{9,0},... | collective-permute-start | bytes 73736 | tf_op jit(solution)/shard_map/ppermute | solution.py:30
  204.6 1.1 collective-permute-done.29
  205.8 1.1 collective-permute-start.31
  207.1 1.6 convolution_select_fusion._
  210.6 1.0 score_late.1
  (91 shorter events, 9.9 us)
Async XLA Ops:
  1.0 18.4 %collective-permute-start.1 = (bf16[32,4096]{1,0:T(8,128)(2,1)S(1)}, bf16[32,4096]{1,0:T(8,128)(2,1)S(1)}, u32[]{:S(2)}, u32[]{:S(2)}) collective-permute-start(bf16[32,4096]{1,0:T(8,128)(2,1)S(1)} %head.1), channel_id=1, source_target_pairs={{0,16},{1,17},{2,18},{3,19},{4,20},{5,21},{6,22},{7,23},{8,24},{9,... | collective-permute-start | bytes 786440 | tf_op jit(solution)/shard_map/ppermute | solution.py:30
  19.3 16.7 %copy-start.5 = (bf16[32,4096]{1,0:T(8,128)(2,1)}, bf16[32,4096]{1,0:T(8,128)(2,1)S(1)}, u32[]{:S(2)}) copy-start(bf16[32,4096]{1,0:T(8,128)(2,1)S(1)} %collective-permute-done.1) | copy-start | bytes 786436
  37.7 1.8 collective-permute-start.2
  37.7 71.9 %collective-permute-start.7 = (bf16[64,16384]{1,0:T(8,128)(2,1)}, bf16[64,16384]{1,0:T(8,128)(2,1)S(1)}, u32[]{:S(2)}, u32[]{:S(2)}) collective-permute-start(bf16[64,16384]{1,0:T(8,128)(2,1)} %slice.71), channel_id=1, source_target_pairs={{0,16},{1,17},{2,18},{3,19},{4,20},{5,21},{6,22},{7,23},{8,24},{9,... | collective-permute-start | bytes 6291464 | tf_op jit(solution)/shard_map/ppermute | solution.py:30
  40.6 7.7 %collective-permute-start.3 = (f32[224,256]{1,0:T(8,128)S(1)}, f32[224,256]{1,0:T(8,128)S(1)}, u32[]{:S(2)}, u32[]{:S(2)}) collective-permute-start(f32[224,256]{1,0:T(8,128)S(1)} %dynamic-slice_add_fusion), channel_id=1, source_target_pairs={{0,3},{1,2},{2,1},{3,0},{4,7},{5,6},{6,5},{7,4},{8,11},{9,10},{10,... | collective-permute-start | bytes 688136 | tf_op jit(solution)/shard_map/ppermute | solution.py:30
  48.3 7.4 %collective-permute-start.4 = (f32[224,256]{1,0:T(8,128)S(1)}, f32[224,256]{1,0:T(8,128)S(1)}, u32[]{:S(2)}, u32[]{:S(2)}) collective-permute-start(f32[224,256]{1,0:T(8,128)S(1)} %add.129), channel_id=1, source_target_pairs={{0,5},{1,4},{2,7},{3,6},{4,1},{5,0},{6,3},{7,2},{8,13},{9,12},{10,... | collective-permute-start | bytes 688136 | tf_op jit(solution)/shard_map/ppermute | solution.py:30
  56.4 13.7 %collective-permute-start.5 = (f32[224,256]{1,0:T(8,128)}, f32[224,256]{1,0:T(8,128)}, u32[]{:S(2)}, u32[]{:S(2)}) collective-permute-start(f32[224,256]{1,0:T(8,128)} %add.130), channel_id=1, source_target_pairs={{0,9},{1,8},{2,11},{3,10},{4,13},{5,12},{6,15},{7,14},{8,1},{9,0},... | collective-permute-start | bytes 688136 | tf_op jit(solution)/shard_map/ppermute | solution.py:30
  59.3 44.1 %collective-permute-start.6 = (bf16[32,12288]{1,0:T(8,128)(2,1)}, bf16[32,12288]{1,0:T(8,128)(2,1)}, u32[]{:S(2)}, u32[]{:S(2)}) collective-permute-start(bf16[32,12288]{1,0:T(8,128)(2,1)} %slice.70), channel_id=1, source_target_pairs={{0,16},{1,17},{2,18},{3,19},{4,20},{5,21},{6,22},{7,23},{8,24},{9,... | collective-permute-start | bytes 2359304 | tf_op jit(solution)/shard_map/ppermute | solution.py:30
  59.8 82.8 %collective-permute-start.12 = (bf16[56,16384]{1,0:T(8,128)(2,1)}, bf16[56,16384]{1,0:T(8,128)(2,1)}, u32[]{:S(2)}, u32[]{:S(2)}) collective-permute-start(bf16[56,16384]{1,0:T(8,128)(2,1)} %slice.73), channel_id=1, source_target_pairs={{0,16},{1,17},{2,18},{3,19},{4,20},{5,21},{6,22},{7,23},{8,24},{9,... | collective-permute-start | bytes 5505032 | tf_op jit(solution)/shard_map/ppermute | solution.py:30
  103.4 39.3 %slice-start = ((s8[16777216]{0:T(1024)(128)(4,1)}), s8[4194304]{0:T(1024)(128)(4,1)S(1)}, s32[]{:S(2)}) async-start(s8[16777216]{0:T(1024)(128)(4,1)} %bitcast.12), calls=%async_computation | async-start | bytes 8388608
  103.4 39.3 %slice-start.1 = ((s8[16777216]{0:T(1024)(128)(4,1)}), s8[4194304]{0:T(1024)(128)(4,1)S(1)}, s32[]{:S(2)}) async-start(s8[16777216]{0:T(1024)(128)(4,1)} %bitcast.12), calls=%async_computation.1 | async-start | bytes 8388608
  109.6 33.1 %slice-start.2 = ((s8[16777216]{0:T(1024)(128)(4,1)}), s8[4194304]{0:T(1024)(128)(4,1)S(1)}, s32[]{:S(2)}) async-start(s8[16777216]{0:T(1024)(128)(4,1)} %bitcast.12), calls=%async_computation.2 | async-start | bytes 8388608
  109.6 33.1 %slice-start.3 = ((s8[16777216]{0:T(1024)(128)(4,1)}), s8[4194304]{0:T(1024)(128)(4,1)S(1)}, s32[]{:S(2)}) async-start(s8[16777216]{0:T(1024)(128)(4,1)} %bitcast.12), calls=%async_computation.3 | async-start | bytes 8388608
  118.5 1.4 collective-permute-start.8
  119.9 4.8 %collective-permute-start.9 = (f32[96,256]{1,0:T(8,128)S(1)}, f32[96,256]{1,0:T(8,128)S(1)}, u32[]{:S(2)}, u32[]{:S(2)}) collective-permute-start(f32[96,256]{1,0:T(8,128)S(1)} %fusion.56), channel_id=1, source_target_pairs={{0,3},{1,2},{2,1},{3,0},{4,7},{5,6},{6,5},{7,4},{8,11},{9,10},{10,... | collective-permute-start | bytes 294920 | tf_op jit(solution)/shard_map/ppermute | solution.py:30
  124.8 4.4 %collective-permute-start.10 = (f32[96,256]{1,0:T(8,128)S(1)}, f32[96,256]{1,0:T(8,128)S(1)}, u32[]{:S(2)}, u32[]{:S(2)}) collective-permute-start(f32[96,256]{1,0:T(8,128)S(1)} %add.138), channel_id=1, source_target_pairs={{0,5},{1,4},{2,7},{3,6},{4,1},{5,0},{6,3},{7,2},{8,13},{9,12},{10,... | collective-permute-start | bytes 294920 | tf_op jit(solution)/shard_map/ppermute | solution.py:30
  129.2 8.1 %collective-permute-start.11 = (f32[96,256]{1,0:T(8,128)S(1)}, f32[96,256]{1,0:T(8,128)S(1)}, u32[]{:S(2)}, u32[]{:S(2)}) collective-permute-start(f32[96,256]{1,0:T(8,128)S(1)} %add.139), channel_id=1, source_target_pairs={{0,9},{1,8},{2,11},{3,10},{4,13},{5,12},{6,15},{7,14},{8,1},{9,0},... | collective-permute-start | bytes 294920 | tf_op jit(solution)/shard_map/ppermute | solution.py:30
  132.4 39.7 %collective-permute-start = (bf16[48,14336]{1,0:T(8,128)(2,1)S(1)}, bf16[48,14336]{1,0:T(8,128)(2,1)S(1)}, u32[]{:S(2)}, u32[]{:S(2)}) collective-permute-start(bf16[48,14336]{1,0:T(8,128)(2,1)S(1)} %slice.72), channel_id=1, source_target_pairs={{0,16},{1,17},{2,18},{3,19},{4,20},{5,21},{6,22},{7,23},{8,24},{9,... | collective-permute-start | bytes 4128776 | tf_op jit(solution)/shard_map/ppermute | solution.py:30
  137.3 25.4 %copy-start.3 = (bf16[48,2048]{1,0:T(8,128)(2,1)S(1)}, bf16[48,2048]{1,0:T(8,128)(2,1)}, u32[]{:S(2)}) copy-start(bf16[48,2048]{1,0:T(8,128)(2,1)} %slice.74) | copy-start | bytes 589828
  137.3 25.9 %copy-start.1 = (bf16[24,8192]{1,0:T(8,128)(2,1)S(1)}, bf16[24,8192]{1,0:T(8,128)(2,1)}, u32[]{:S(2)}) copy-start(bf16[24,8192]{1,0:T(8,128)(2,1)} %slice.75) | copy-start | bytes 1179652
  147.0 1.3 collective-permute-start.13
  148.4 3.9 %collective-permute-start.14 = (f32[56,256]{1,0:T(8,128)S(1)}, f32[56,256]{1,0:T(8,128)S(1)}, u32[]{:S(2)}, u32[]{:S(2)}) collective-permute-start(f32[56,256]{1,0:T(8,128)S(1)} %dynamic-slice_add_fusion.1), channel_id=1, source_target_pairs={{0,3},{1,2},{2,1},{3,0},{4,7},{5,6},{6,5},{7,4},{8,11},{9,10},{10,... | collective-permute-start | bytes 172040 | tf_op jit(solution)/shard_map/ppermute | solution.py:30
  152.3 3.7 %collective-permute-start.15 = (f32[56,256]{1,0:T(8,128)S(1)}, f32[56,256]{1,0:T(8,128)S(1)}, u32[]{:S(2)}, u32[]{:S(2)}) collective-permute-start(f32[56,256]{1,0:T(8,128)S(1)} %add.142), channel_id=1, source_target_pairs={{0,5},{1,4},{2,7},{3,6},{4,1},{5,0},{6,3},{7,2},{8,13},{9,12},{10,... | collective-permute-start | bytes 172040 | tf_op jit(solution)/shard_map/ppermute | solution.py:30
  156.0 4.9 %collective-permute-start.16 = (f32[56,256]{1,0:T(8,128)S(1)}, f32[56,256]{1,0:T(8,128)S(1)}, u32[]{:S(2)}, u32[]{:S(2)}) collective-permute-start(f32[56,256]{1,0:T(8,128)S(1)} %add.143), channel_id=1, source_target_pairs={{0,9},{1,8},{2,11},{3,10},{4,13},{5,12},{6,15},{7,14},{8,1},{9,0},... | collective-permute-start | bytes 172040 | tf_op jit(solution)/shard_map/ppermute | solution.py:30
  160.9 3.8 %collective-permute-start.17 = (bf16[376,256]{1,0:T(8,128)(2,1)S(1)}, bf16[376,256]{1,0:T(8,128)(2,1)S(1)}, u32[]{:S(2)}, u32[]{:S(2)}) collective-permute-start(bf16[376,256]{1,0:T(8,128)(2,1)S(1)} %pad_maximum_fusion.5), channel_id=1, source_target_pairs={{0,1},{1,0},{2,3},{3,2},{4,5},{5,4},{6,7},{7,6},{8,9},{9,8},{10,11... | collective-permute-start | bytes 577544 | tf_op jit(solution)/shard_map/ppermute | solution.py:30
  162.7 13.6 %collective-permute-start.18 = (bf16[48,2048]{1,0:T(8,128)(2,1)S(1)}, bf16[48,2048]{1,0:T(8,128)(2,1)S(1)}, u32[]{:S(2)}, u32[]{:S(2)}) collective-permute-start(bf16[48,2048]{1,0:T(8,128)(2,1)S(1)} %copy-done.3), channel_id=1, source_target_pairs={{0,16},{1,17},{2,18},{3,19},{4,20},{5,21},{6,22},{7,23},{8,24},{9,... | collective-permute-start | bytes 589832 | tf_op jit(solution)/shard_map/ppermute | solution.py:30
  163.2 21.5 %collective-permute-start.23 = (bf16[24,8192]{1,0:T(8,128)(2,1)S(1)}, bf16[24,8192]{1,0:T(8,128)(2,1)S(1)}, u32[]{:S(2)}, u32[]{:S(2)}) collective-permute-start(bf16[24,8192]{1,0:T(8,128)(2,1)S(1)} %copy-done.1), channel_id=1, source_target_pairs={{0,16},{1,17},{2,18},{3,19},{4,20},{5,21},{6,22},{7,23},{8,24},{9,... | collective-permute-start | bytes 1179656 | tf_op jit(solution)/shard_map/ppermute | solution.py:30
  175.1 4.4 %copy-start.2 = (bf16[24,7168]{1,0:T(8,128)(2,1)S(1)}, bf16[24,7168]{1,0:T(8,128)(2,1)}, u32[]{:S(2)}) copy-start(bf16[24,7168]{1,0:T(8,128)(2,1)} %slice.76) | copy-start | bytes 1032196
  176.8 1.3 collective-permute-start.19
  178.1 3.8 %collective-permute-start.20 = (f32[48,256]{1,0:T(8,128)S(1)}, f32[48,256]{1,0:T(8,128)S(1)}, u32[]{:S(2)}, u32[]{:S(2)}) collective-permute-start(f32[48,256]{1,0:T(8,128)S(1)} %dynamic-slice_add_fusion.2), channel_id=1, source_target_pairs={{0,3},{1,2},{2,1},{3,0},{4,7},{5,6},{6,5},{7,4},{8,11},{9,10},{10,... | collective-permute-start | bytes 147464 | tf_op jit(solution)/shard_map/ppermute | solution.py:30
  179.4 12.7 %collective-permute-start.24 = (bf16[24,7168]{1,0:T(8,128)(2,1)S(1)}, bf16[24,7168]{1,0:T(8,128)(2,1)S(1)}, u32[]{:S(2)}, u32[]{:S(2)}) collective-permute-start(bf16[24,7168]{1,0:T(8,128)(2,1)S(1)} %copy-done.2), channel_id=1, source_target_pairs={{0,16},{1,17},{2,18},{3,19},{4,20},{5,21},{6,22},{7,23},{8,24},{9,... | collective-permute-start | bytes 1032200 | tf_op jit(solution)/shard_map/ppermute | solution.py:30
  180.0 13.2 %collective-permute-start.25 = (bf16[24,1024]{1,0:T(8,128)(2,1)S(1)}, bf16[24,1024]{1,0:T(8,128)(2,1)S(1)}, u32[]{:S(2)}, u32[]{:S(2)}) collective-permute-start(bf16[24,1024]{1,0:T(8,128)(2,1)S(1)} %slice.77), channel_id=1, source_target_pairs={{0,16},{1,17},{2,18},{3,19},{4,20},{5,21},{6,22},{7,23},{8,24},{9,... | collective-permute-start | bytes 147464 | tf_op jit(solution)/shard_map/ppermute | solution.py:30
  181.9 4.1 %collective-permute-start.21 = (f32[48,256]{1,0:T(8,128)S(1)}, f32[48,256]{1,0:T(8,128)S(1)}, u32[]{:S(2)}, u32[]{:S(2)}) collective-permute-start(f32[48,256]{1,0:T(8,128)S(1)} %add.147), channel_id=1, source_target_pairs={{0,5},{1,4},{2,7},{3,6},{4,1},{5,0},{6,3},{7,2},{8,13},{9,12},{10,... | collective-permute-start | bytes 147464 | tf_op jit(solution)/shard_map/ppermute | solution.py:30
  186.0 10.1 %copy-start.4 = (s32[448]{0:T(512)S(1)}, s32[448]{0:T(512)}, u32[]{:S(2)}) copy-start(s32[448]{0:T(512)} %param.9) | copy-start | bytes 5380
  186.0 7.2 %collective-permute-start.22 = (f32[48,256]{1,0:T(8,128)S(1)}, f32[48,256]{1,0:T(8,128)S(1)}, u32[]{:S(2)}, u32[]{:S(2)}) collective-permute-start(f32[48,256]{1,0:T(8,128)S(1)} %add.148), channel_id=1, source_target_pairs={{0,9},{1,8},{2,11},{3,10},{4,13},{5,12},{6,15},{7,14},{8,1},{9,0},... | collective-permute-start | bytes 147464 | tf_op jit(solution)/shard_map/ppermute | solution.py:30
  193.2 6.5 %copy-start = (bf16[512,1024]{1,0:T(8,128)(2,1)S(1)}, bf16[512,1024]{1,0:T(8,128)(2,1)}, u32[]{:S(2)}) copy-start(bf16[512,1024]{1,0:T(8,128)(2,1)} %param.8) | copy-start | bytes 3145732
  193.5 1.3 collective-permute-start.26
  193.6 12.2 %collective-permute-start.30 = (bf16[376,512]{1,0:T(8,128)(2,1)S(1)}, bf16[376,512]{1,0:T(8,128)(2,1)S(1)}, u32[]{:S(2)}, u32[]{:S(2)}) collective-permute-start(bf16[376,512]{1,0:T(8,128)(2,1)S(1)} %pad_maximum_fusion.3), channel_id=1, source_target_pairs={{0,17},{1,16},{2,19},{3,18},{4,21},{5,20},{6,23},{7,22},{8,25},{9,... | collective-permute-start | bytes 1155080 | tf_op jit(solution)/shard_map/ppermute | solution.py:30
  194.7 3.3 %collective-permute-start.27 = (f32[24,256]{1,0:T(8,128)S(1)}, f32[24,256]{1,0:T(8,128)S(1)}, u32[]{:S(2)}, u32[]{:S(2)}) collective-permute-start(f32[24,256]{1,0:T(8,128)S(1)} %dynamic-slice_add_fusion.3), channel_id=1, source_target_pairs={{0,3},{1,2},{2,1},{3,0},{4,7},{5,6},{6,5},{7,4},{8,11},{9,10},{10,... | collective-permute-start | bytes 73736 | tf_op jit(solution)/shard_map/ppermute | solution.py:30
  198.0 3.3 %collective-permute-start.28 = (f32[24,256]{1,0:T(8,128)S(1)}, f32[24,256]{1,0:T(8,128)S(1)}, u32[]{:S(2)}, u32[]{:S(2)}) collective-permute-start(f32[24,256]{1,0:T(8,128)S(1)} %add.153), channel_id=1, source_target_pairs={{0,5},{1,4},{2,7},{3,6},{4,1},{5,0},{6,3},{7,2},{8,13},{9,12},{10,... | collective-permute-start | bytes 73736 | tf_op jit(solution)/shard_map/ppermute | solution.py:30
  201.2 4.5 %collective-permute-start.29 = (f32[24,256]{1,0:T(8,128)S(1)}, f32[24,256]{1,0:T(8,128)S(1)}, u32[]{:S(2)}, u32[]{:S(2)}) collective-permute-start(f32[24,256]{1,0:T(8,128)S(1)} %add.154), channel_id=1, source_target_pairs={{0,9},{1,8},{2,11},{3,10},{4,13},{5,12},{6,15},{7,14},{8,1},{9,0},... | collective-permute-start | bytes 73736 | tf_op jit(solution)/shard_map/ppermute | solution.py:30
  205.8 3.4 %collective-permute-start.31 = (bf16[72,256]{1,0:T(8,128)(2,1)S(1)}, bf16[72,256]{1,0:T(8,128)(2,1)S(1)}, u32[]{:S(2)}, u32[]{:S(2)}) collective-permute-start(bf16[72,256]{1,0:T(8,128)(2,1)S(1)} %pad_maximum_fusion.7), channel_id=1, source_target_pairs={{0,17},{1,16},{2,19},{3,18},{4,21},{5,20},{6,23},{7,22},{8,25},{9,... | collective-permute-start | bytes 110600 | tf_op jit(solution)/shard_map/ppermute | solution.py:30
  209.2 1.4 collective-permute-start.32
